TPU v7x, 32 devices: a whole 2x2x4 slice. The times are simulated.
32 devices in a mesh: ctx: 8 (over z, x), chan: 2 (over core), dp: 2 (over y).
Axes of the slice: x: 2, y: 2, z: 4, core: 2. Of those that a mesh axis runs over, the one named last changes fastest.
Arguments:
- q_stream: bfloat16 [2, 2048, 4096], P('dp', 'ctx', 'chan'), may hold values from -6 to 6
- k_stream: bfloat16 [2, 2048, 4096], P('dp', 'ctx', 'chan'), may hold values from -6 to 6
- v_stream: bfloat16 [2, 2048, 4096], P('dp', 'ctx', 'chan'), may hold values from -6 to 6
- out_grad: bfloat16 [2, 2048, 4096], P('dp', 'ctx', 'chan'), may hold values from -6 to 6
- norm_gain: float32 [4096], P('chan'), may hold values from 0.1 to 1.9
- residue: float32 [4096, 16], P('chan'), may hold values from -6 to 6
- rate: float32 [4096, 16], P('chan'), may hold values from -1.5 to 6
Outputs:
- y_out: bfloat16 [2, 2048, 4096], P('dp', 'ctx', 'chan')
- grad_q: bfloat16 [2, 2048, 4096], P('dp', 'ctx', 'chan')
- grad_k: bfloat16 [2, 2048, 4096], P('dp', 'ctx', 'chan')
- grad_v: bfloat16 [2, 2048, 4096], P('dp', 'ctx', 'chan')
- grad_residue: float32 [4096, 16], P('chan')
- grad_rate: float32 [4096, 16], P('chan')
- grad_gain: float32 [4096], P('chan')
All inputs are finite; a program needn't handle non-finite values.
Results may differ from a plain program's by a relative error of at most 0.0051.
Values may be sent and summed in bfloat16 or wider, within the bound.
No kernel may reach another device: no remote copies, remote signals or barrier semaphores. Data moves between devices by JAX's collectives and lax.ppermute only.
A program may use at most 128 MiB of HBM per device.

v0:
```python
import math

import jax
import jax.numpy as jnp
from jax import lax
from jax.sharding import PartitionSpec as P

D = 4096


highest = lax.Precision.HIGHEST
epsilon = 1e-06


def modal(decays, angles, parity, seq_len, with_slope):
    shrink = jnp.exp(-decays)[None, :]
    gap_one = (-jnp.expm1(-decays))[None, :]
    tail_val = jnp.exp(-decays * seq_len)[None, :]
    gap_all = (-jnp.expm1(-decays * seq_len))[None, :]
    odd_rows = (parity > 0)[:, None]
    numer = jnp.where(odd_rows, 1.0 + tail_val, gap_all)
    half_sin = jnp.sin(angles * 0.5)[:, None]
    full_sin = jnp.sin(angles)[:, None]
    den_real = gap_one + 2.0 * shrink * half_sin * half_sin
    den_imag = shrink * full_sin
    magnitude = den_real * den_real + den_imag * den_imag
    value_real = numer * den_real / magnitude
    value_imag = -numer * den_imag / magnitude
    if not with_slope:
        return (value_real, value_imag)
    power = jnp.where(odd_rows, -tail_val, tail_val)
    z_real = shrink * jnp.cos(angles)[:, None]
    z_imag = -shrink * full_sin
    top_real = seq_len * power * den_real - numer * z_real
    top_imag = seq_len * power * den_imag - numer * z_imag
    square_real = den_real * den_real - den_imag * den_imag
    square_imag = 2.0 * den_real * den_imag
    quartic = magnitude * magnitude
    slope_real = (top_real * square_real + top_imag * square_imag) / quartic
    slope_imag = (top_imag * square_real - top_real * square_imag) / quartic
    return (value_real, value_imag, slope_real, slope_imag)


def gating(conv, q_part, grad_part, norm_gain):
    q_float = q_part.astype(jnp.float32)
    grad_float = grad_part.astype(jnp.float32)
    mixed = q_float * conv
    scaled = norm_gain * grad_float
    squares, inner_sum = lax.psum(
        (jnp.sum(mixed * mixed, axis=-1), jnp.sum(scaled * mixed, axis=-1)), "chan"
    )
    inv_rms = lax.rsqrt(squares / D + epsilon)[..., None]
    inner_sum = inner_sum[..., None]
    y_part = (norm_gain * mixed * inv_rms).astype(jnp.bfloat16)
    mixed_grad = inv_rms * scaled - mixed * (inv_rms * inv_rms * inv_rms * inner_sum / D)
    grad_q = (mixed_grad * conv).astype(jnp.bfloat16)
    gate_grad = mixed_grad * q_float
    gain_part = jnp.sum((grad_float * mixed * inv_rms).reshape(-1, conv.shape[-1]), axis=0)
    return (y_part, grad_q, gate_grad, gain_part)


def transform_plan(q_stream, k_stream, v_stream, out_grad, norm_gain, residue, rate):
    ctx_count = lax.axis_size("ctx")
    ctx_rank = lax.axis_index("ctx")
    batch_rows, length, channels = q_stream.shape
    slice_len = length // ctx_count
    seq_len = length * ctx_count
    period = 2 * seq_len
    is_first = ctx_rank == 0
    slots = jnp.arange(ctx_count, dtype=jnp.int32)
    slot_angle = (slots[:, None] * slots[None, :] % (2 * ctx_count)).astype(jnp.float32) * (
        math.pi / ctx_count
    )
    signs = (1 - 2 * (slots % 2)).astype(jnp.float32)
    lead_row = slots[:, None] == 0
    lead_col = slots[None, :] == 0
    forward_real = jnp.where(lead_row, 1.0, jnp.cos(slot_angle))
    forward_imag = jnp.where(lead_row, signs[None, :], -jnp.sin(slot_angle))
    inverse_real = jnp.where(lead_col, 1.0, 2.0 * jnp.cos(slot_angle)) / period
    inverse_imag = jnp.where(lead_col, signs[:, None], -2.0 * jnp.sin(slot_angle)) / period
    columns = jnp.arange(length, dtype=jnp.int32)
    freq_a = jnp.where(is_first, 0, ctx_rank) + 2 * ctx_count * columns
    freq_b = jnp.where(is_first, ctx_count, ctx_rank) + 2 * ctx_count * columns

    def twiddle(freq):
        phase = (freq[:, None] * columns[None, :] % period).astype(jnp.float32) * (
            2.0 * math.pi / period
        )
        return (jnp.cos(phase), jnp.sin(phase))

    cosine_a, sine_a = twiddle(freq_a)
    cosine_b, sine_b = twiddle(freq_b)
    angles_a = freq_a.astype(jnp.float32) * (2.0 * math.pi / period)
    angles_b = freq_b.astype(jnp.float32) * (2.0 * math.pi / period)
    parity_a = freq_a % 2
    parity_b = freq_b % 2

    def spectrum(slices):
        slot_real = jnp.einsum("kb,xbjc->xkjc", forward_real, slices, precision=highest)
        slot_imag = jnp.einsum("kb,xbjc->xkjc", forward_imag, slices, precision=highest)
        rows_real, rows_imag = (
            lax.all_to_all(slot_real, "ctx", split_axis=1, concat_axis=1, tiled=True),
            lax.all_to_all(slot_imag, "ctx", split_axis=1, concat_axis=1, tiled=True),
        )
        rows_real = rows_real.reshape(batch_rows, length, channels)
        rows_imag = rows_imag.reshape(batch_rows, length, channels)
        a_real = jnp.einsum("kj,xjc->xkc", cosine_a, rows_real, precision=highest)
        a_imag = -jnp.einsum("kj,xjc->xkc", sine_a, rows_real, precision=highest)
        b_real = jnp.einsum("kj,xjc->xkc", cosine_b, rows_imag, precision=highest)
        b_imag = -jnp.einsum("kj,xjc->xkc", sine_b, rows_imag, precision=highest)
        return (a_real, a_imag, b_real, b_imag)

    def positions(spec):
        g_ar, g_ai, g_br, g_bi = spec
        u_first = g_ar - g_bi
        u_second = g_ai + g_br
        x_first = jnp.where(is_first, g_ar, u_first)
        x_second = jnp.where(is_first, g_ai, u_second)
        y_first = jnp.where(is_first, g_br, u_second)
        y_second = jnp.where(is_first, -g_bi, u_first)
        out_real = jnp.einsum("kj,xkc->xjc", cosine_a, x_first, precision=highest) - jnp.einsum(
            "kj,xkc->xjc", sine_a, x_second, precision=highest
        )
        out_imag = jnp.einsum("kj,xkc->xjc", cosine_b, y_first, precision=highest) + jnp.einsum(
            "kj,xkc->xjc", sine_b, y_second, precision=highest
        )
        out_real = out_real.reshape(batch_rows, ctx_count, slice_len, channels)
        out_imag = out_imag.reshape(batch_rows, ctx_count, slice_len, channels)
        recv_real, recv_imag = (
            lax.all_to_all(out_real, "ctx", split_axis=1, concat_axis=1, tiled=True),
            lax.all_to_all(out_imag, "ctx", split_axis=1, concat_axis=1, tiled=True),
        )
        return jnp.einsum("bk,xkjc->xbjc", inverse_real, recv_real, precision=highest) + jnp.einsum(
            "bk,xkjc->xbjc", inverse_imag, recv_imag, precision=highest
        )

    def multiply(spec, kernel_rows, flip):
        s_ar, s_ai, s_br, s_bi = spec
        h_ar, h_ai, h_br, h_bi = kernel_rows
        if flip:
            h_ai = -h_ai
            h_bi = -h_bi
        return (
            s_ar * h_ar - s_ai * h_ai,
            s_ai * h_ar + s_ar * h_ai,
            s_br * h_br - s_bi * h_bi,
            s_bi * h_br + s_br * h_bi,
        )

    decays = jnp.exp(rate) / seq_len
    flat_decays = decays.reshape(-1)
    mode_count = residue.shape[1]
    block = math.gcd(length, 64)
    block_count = length // block
    block_ids = jnp.arange(block_count, dtype=jnp.int32)

    def kernel_block(carry, block_index):
        row_start = block_index * block
        pieces_now = []
        for angles, parity in ((angles_a, parity_a), (angles_b, parity_b)):
            angle_rows = lax.dynamic_slice_in_dim(angles, row_start, block)
            parity_rows = lax.dynamic_slice_in_dim(parity, row_start, block)
            f_real, f_imag = modal(flat_decays, angle_rows, parity_rows, seq_len, False)
            pieces_now.append(
                jnp.sum(f_real.reshape(block, channels, mode_count) * residue, axis=-1)
            )
            pieces_now.append(
                jnp.sum(f_imag.reshape(block, channels, mode_count) * residue, axis=-1)
            )
        return (carry, tuple(pieces_now))

    _, kernel_pieces = lax.scan(kernel_block, 0.0, block_ids)
    kernel_rows = tuple((piece.reshape(length, channels) for piece in kernel_pieces))
    value_blocks = (k_stream.astype(jnp.float32) * v_stream.astype(jnp.float32)).astype(
        jnp.bfloat16
    )
    value_sl = lax.all_to_all(
        value_blocks.reshape(batch_rows, ctx_count, slice_len, channels),
        "ctx",
        split_axis=1,
        concat_axis=1,
        tiled=True,
    ).astype(jnp.float32)
    value_spec = spectrum(value_sl)
    conv_sl = positions(multiply(value_spec, kernel_rows, False))
    conv_blk = lax.all_to_all(conv_sl, "ctx", split_axis=1, concat_axis=1, tiled=True).reshape(
        batch_rows, length, channels
    )
    y_out, grad_q, gate_blk, gain_part = gating(conv_blk, q_stream, out_grad, norm_gain)
    gate_sl = lax.all_to_all(
        gate_blk.reshape(batch_rows, ctx_count, slice_len, channels),
        "ctx",
        split_axis=1,
        concat_axis=1,
        tiled=True,
    )
    gate_spec = spectrum(gate_sl)
    grad_sl = positions(multiply(gate_spec, kernel_rows, True))
    value_grad = lax.all_to_all(grad_sl, "ctx", split_axis=1, concat_axis=1, tiled=True).reshape(
        batch_rows, length, channels
    )
    grad_k = (value_grad * v_stream.astype(jnp.float32)).astype(jnp.bfloat16)
    grad_v = (value_grad * k_stream.astype(jnp.float32)).astype(jnp.bfloat16)

    def true_rows(spec):
        s_ar, s_ai, s_br, s_bi = spec
        return (
            jnp.where(is_first, s_ar, s_ar - s_bi),
            jnp.where(is_first, s_ai, s_ai + s_br),
            s_br,
            s_bi,
        )

    z_ar, z_ai, z_br, z_bi = true_rows(value_spec)
    g_ar, g_ai, g_br, g_bi = true_rows(gate_spec)
    cross_ar = jnp.sum(g_ar * z_ar + g_ai * z_ai, axis=0)
    cross_ai = jnp.sum(g_ai * z_ar - g_ar * z_ai, axis=0)
    cross_br = jnp.sum(g_br * z_br + g_bi * z_bi, axis=0)
    cross_bi = jnp.sum(g_bi * z_br - g_br * z_bi, axis=0)
    weight_a = jnp.where(is_first, 1.0, 2.0) / period
    weight_b = jnp.where(is_first, 1.0, 0.0) / period

    def grad_block(totals, block_index):
        row_start = block_index * block
        sums_now = []
        for angles, parity, cross_real, cross_imag in (
            (angles_a, parity_a, cross_ar, cross_ai),
            (angles_b, parity_b, cross_br, cross_bi),
        ):
            angle_rows = lax.dynamic_slice_in_dim(angles, row_start, block)
            parity_rows = lax.dynamic_slice_in_dim(parity, row_start, block)
            real_rows = lax.dynamic_slice_in_dim(cross_real, row_start, block)[:, :, None]
            imag_rows = lax.dynamic_slice_in_dim(cross_imag, row_start, block)[:, :, None]
            f_real, f_imag, d_real, d_imag = modal(
                flat_decays, angle_rows, parity_rows, seq_len, True
            )
            shape_three = (block, channels, mode_count)
            sums_now.append(
                jnp.sum(
                    real_rows * f_real.reshape(shape_three)
                    + imag_rows * f_imag.reshape(shape_three),
                    axis=0,
                )
            )
            sums_now.append(
                jnp.sum(
                    real_rows * d_real.reshape(shape_three)
                    + imag_rows * d_imag.reshape(shape_three),
                    axis=0,
                )
            )
        return (tuple((total + part for total, part in zip(totals, sums_now))), None)

    zero_modes = jnp.zeros((channels, mode_count), jnp.float32)
    (res_a, slope_a, res_b, slope_b), _ = lax.scan(
        grad_block, (zero_modes, zero_modes, zero_modes, zero_modes), block_ids
    )
    res_part = weight_a * res_a + weight_b * res_b
    rate_part = decays * residue * (weight_a * slope_a + weight_b * slope_b)
    return (y_out, grad_q, grad_k, grad_v, res_part, rate_part, gain_part)


def shards(q_stream, k_stream, v_stream, out_grad, norm_gain, residue, rate):
    results = transform_plan(q_stream, k_stream, v_stream, out_grad, norm_gain, residue, rate)
    y_out, grad_q, grad_k, grad_v, res_part, rate_part, gain_part = results
    grad_residue, grad_rate, grad_gain = lax.psum((res_part, rate_part, gain_part), ("ctx", "dp"))
    return (y_out, grad_q, grad_k, grad_v, grad_residue, grad_rate, grad_gain)


def solution(mesh):
    in_specs = (
        P("dp", "ctx", "chan"),
        P("dp", "ctx", "chan"),
        P("dp", "ctx", "chan"),
        P("dp", "ctx", "chan"),
        P("chan"),
        P("chan", None),
        P("chan", None),
    )
    out_specs = (
        P("dp", "ctx", "chan"),
        P("dp", "ctx", "chan"),
        P("dp", "ctx", "chan"),
        P("dp", "ctx", "chan"),
        P("chan", None),
        P("chan", None),
        P("chan"),
    )
    return jax.shard_map(shards, mesh=mesh, in_specs=in_specs, out_specs=out_specs, check_vma=False)
```

profile of v0, /device:TPU:0, one launch (start us, length us, event | category | flops | bytes accessed | tf_op | source)
XLA Modules:
  0.0 1118.8 jit_solution(14108941958894904162)
XLA Ops:
  10.1 7.3 all-to-all-start
  18.8 24.3 %all-to-all-done = bf16[1,8,32,2048]{3,2,0,1:T(8,128)(2,1)S(1)} async-done(((bf16[1,8,32,2048]{3,2,0,1:T(8,128)(2,1)}), bf16[1,8,32,2048]{3,2,0,1:T(8,128)(2,1)S(1)}, u32[]{:S(2)}, u32[]{:S(2)}) %all-to-all-start) | async-done | bytes 1048608 | tf_op jit(solution)/shard_map/all_to_all | solution.py:177
  57.4 41.7 %all-to-all-done.2 = f32[1,8,32,2048]{3,2,0,1:T(8,128)S(1)} async-done(((f32[1,8,32,2048]{3,2,0,1:T(8,128)}), f32[1,8,32,2048]{3,2,0,1:T(8,128)S(1)}, u32[]{:S(2)}, u32[]{:S(2)}) %all-to-all-start.2) | async-done | bytes 2097184 | tf_op jit(solution)/shard_map/all_to_all | solution.py:103
  99.1 4.6 all-to-all-start.1
  103.7 114.4 %while.39 = (s32[]{:T(128)}, f32[4,64,2048]{2,1,0:T(8,128)}, f32[4,64,2048]{2,1,0:T(8,128)}, f32[4,64,2048]{2,1,0:T(8,128)}, f32[4,64,2048]{2,1,0:T(8,128)}, /*i...) while((s32[]{:T(128)}, f32[4,64,2048]{2,1,0:T(8,128)}, ...), condition=%wide.region_5.6_spmd, body=%wide.region_0.5_spmd.sunk | while | flops 70910216 | bytes 10621447 | solution.py:172
  115.0 15.1 %fusion.311 = (f32[64,2048]{1,0:T(8,128)S(1)}, f32[64,2048]{1,0:T(8,128)S(1)}, f32[64,2048]{1,0:T(8,128)S(1)}, f32[64,2048]{1,0:T(8,128)S(1)}) fusion(f32[64]{0:T(128)S(1)} %get-tuple-element.922, f32[64]{0:T(128)S(1)} %get-tuple-element.923, f32[2048,16]{0,1:T(8,128)S(1)} %get-tuple-element.1021, f32[2048,16]{0,1:T(8,128)S(1)} %copy.198, ...), kind=kLoop, calls=%fused_computation.19.clone.1 | loop fusion | flops 70778880 | bytes 2884736 | tf_op jit(solution)/shard_map/while/body/eval_jaxpr/reduce_sum | solution.py:168
  143.7 15.1 %fusion.311 = (f32[64,2048]{1,0:T(8,128)S(1)}, f32[64,2048]{1,0:T(8,128)S(1)}, f32[64,2048]{1,0:T(8,128)S(1)}, f32[64,2048]{1,0:T(8,128)S(1)}) fusion(f32[64]{0:T(128)S(1)} %get-tuple-element.922, f32[64]{0:T(128)S(1)} %get-tuple-element.923, f32[2048,16]{0,1:T(8,128)S(1)} %get-tuple-element.1021, f32[2048,16]{0,1:T(8,128)S(1)} %copy.198, ...), kind=kLoop, calls=%fused_computation.19.clone.1 | loop fusion | flops 70778880 | bytes 2884736 | tf_op jit(solution)/shard_map/while/body/eval_jaxpr/reduce_sum | solution.py:168
  172.2 15.1 %fusion.311 = (f32[64,2048]{1,0:T(8,128)S(1)}, f32[64,2048]{1,0:T(8,128)S(1)}, f32[64,2048]{1,0:T(8,128)S(1)}, f32[64,2048]{1,0:T(8,128)S(1)}) fusion(f32[64]{0:T(128)S(1)} %get-tuple-element.922, f32[64]{0:T(128)S(1)} %get-tuple-element.923, f32[2048,16]{0,1:T(8,128)S(1)} %get-tuple-element.1021, f32[2048,16]{0,1:T(8,128)S(1)} %copy.198, ...), kind=kLoop, calls=%fused_computation.19.clone.1 | loop fusion | flops 70778880 | bytes 2884736 | tf_op jit(solution)/shard_map/while/body/eval_jaxpr/reduce_sum | solution.py:168
  200.8 15.1 %fusion.311 = (f32[64,2048]{1,0:T(8,128)S(1)}, f32[64,2048]{1,0:T(8,128)S(1)}, f32[64,2048]{1,0:T(8,128)S(1)}, f32[64,2048]{1,0:T(8,128)S(1)}) fusion(f32[64]{0:T(128)S(1)} %get-tuple-element.922, f32[64]{0:T(128)S(1)} %get-tuple-element.923, f32[2048,16]{0,1:T(8,128)S(1)} %get-tuple-element.1021, f32[2048,16]{0,1:T(8,128)S(1)} %copy.198, ...), kind=kLoop, calls=%fused_computation.19.clone.1 | loop fusion | flops 70778880 | bytes 2884736 | tf_op jit(solution)/shard_map/while/body/eval_jaxpr/reduce_sum | solution.py:168
  229.2 5.9 convolution_bitcast_fusion.7
  235.2 6.7 fusion.38
  241.9 8.5 multiply_subtract_fusion.2
  250.4 9.0 multiply_add_fusion.6
  262.7 4.8 convolution_subtract_fusion.1
  267.5 6.1 all-to-all-start.3
  273.6 4.9 fusion.51
  278.6 4.7 convolution_add_fusion.3
  283.2 37.7 %all-to-all-done.3 = f32[1,8,32,2048]{3,2,0,1:T(8,128)} async-done(((f32[1,8,32,2048]{3,2,0,1:T(8,128)}), f32[1,8,32,2048]{3,2,0,1:T(8,128)}, u32[]{:S(2)}, u32[]{:S(2)}) %all-to-all-start.3) | async-done | bytes 2097184 | tf_op jit(solution)/shard_map/all_to_all | solution.py:130
  325.0 6.2 fusion.68
  331.2 42.2 %all-to-all-done.4 = f32[1,8,32,2048]{3,2,0,1:T(8,128)S(1)} async-done(((f32[1,8,32,2048]{3,2,0,1:T(8,128)}), f32[1,8,32,2048]{3,2,0,1:T(8,128)S(1)}, u32[]{:S(2)}, u32[]{:S(2)}) %all-to-all-start.4) | async-done | bytes 2097184 | tf_op jit(solution)/shard_map/all_to_all | solution.py:131
  373.3 4.9 fusion.37
  379.5 51.9 %all_to_all.60 = f32[1,8,32,2048]{3,2,0,1:T(8,128)S(1)} all-to-all(f32[1,8,32,2048]{3,2,0,1:T(8,128)S(1)} %copy.131), channel_id=1, replica_groups=mesh['ctx'=8,'chan'=2,'dp'=2] {'ctx'}, dimensions={1} | all-to-all | bytes 4194304 | tf_op jit(solution)/shard_map/all_to_all | solution.py:186
  442.2 52.1 %all_to_all.61 = f32[1,8,32,2048]{3,2,0,1:T(8,128)S(1)} all-to-all(f32[1,8,32,2048]{3,2,0,1:T(8,128)S(1)} %bitcast.214), channel_id=1, replica_groups=mesh['ctx'=8,'chan'=2,'dp'=2] {'ctx'}, dimensions={1} | all-to-all | bytes 4194304 | tf_op jit(solution)/shard_map/all_to_all | solution.py:190
  510.3 41.6 %all-to-all-done.8 = f32[1,8,32,2048]{3,2,0,1:T(8,128)} async-done(((f32[1,8,32,2048]{3,2,0,1:T(8,128)}), f32[1,8,32,2048]{3,2,0,1:T(8,128)}, u32[]{:S(2)}, u32[]{:S(2)}) %all-to-all-start.8) | async-done | bytes 2097184 | tf_op jit(solution)/shard_map/all_to_all | solution.py:103
  555.7 7.2 convolution_bitcast_fusion
  562.9 7.3 convolution_bitcast_fusion.1
  570.2 33.8 %all-to-all-done.7 = f32[1,8,32,2048]{3,2,0,1:T(8,128)S(1)} async-done(((f32[1,8,32,2048]{3,2,0,1:T(8,128)}), f32[1,8,32,2048]{3,2,0,1:T(8,128)S(1)}, u32[]{:S(2)}, u32[]{:S(2)}) %all-to-all-start.7) | async-done | bytes 2097184 | tf_op jit(solution)/shard_map/all_to_all | solution.py:102
  603.9 5.9 convolution_bitcast_fusion.3
  609.8 18.4 %subtract_bitcast_fusion.1 = (f32[256,2048]{0,1:T(8,128)}, f32[256,2048]{0,1:T(8,128)}, f32[256,2048]{0,1:T(8,128)}, f32[256,2048]{0,1:T(8,128)}, f32[1,256,2048...) fusion(f32[1,256,2048]{1,2,0:T(8,128)} %copy-done.9, ...), kind=kOutput, calls=%fused_computation.170 | convolution fusion | flops 1630928896 | bytes 41944064 | tf_op jit(solution)/shard_map/kj,xjc->xkc/dot_general | solution.py:107
  631.5 4.6 convolution_subtract_fusion
  636.0 4.5 all-to-all-start.9
  640.6 5.6 fusion.56
  646.1 4.7 convolution_add_fusion.1
  650.8 37.5 %all-to-all-done.9 = f32[1,8,32,2048]{3,2,0,1:T(8,128)} async-done(((f32[1,8,32,2048]{3,2,0,1:T(8,128)}), f32[1,8,32,2048]{3,2,0,1:T(8,128)}, u32[]{:S(2)}, u32[]{:S(2)}) %all-to-all-start.9) | async-done | bytes 2097184 | tf_op jit(solution)/shard_map/all_to_all | solution.py:130
  692.8 69.5 %psum.39 = f32[2048]{0:T(1024)} all-reduce(f32[2048]{0:T(1024)S(1)} %get-tuple-element.596), channel_id=1, replica_groups=mesh['ctx'=8,'chan'=2,'dp'=2] {'ctx','dp'}, use_global_device_ids=true, to_apply=%region_19.20 | all-reduce | flops 2048 | bytes 16384 | tf_op jit(solution)/shard_map/psum | solution.py:266
  772.1 6.2 fusion.60
  778.3 5.5 fusion.36
  786.3 7.2 all-to-all-start.11
  794.2 203.1 %while.40 = (s32[]{:T(128)}, f32[2048,16]{0,1:T(8,128)}, f32[2048,16]{0,1:T(8,128)}, f32[2048,16]{0,1:T(8,128)}, f32[2048,16]{0,1:T(8,128)}, /*index=5*/s32[4]{0...) while((s32[]{:T(128)}, f32[2048,16]{0,1:T(8,128)}, ...), condition=%wide.region_15.16_spmd.clone, body=%wide.region_10.15_spmd.clone.sunk | while | flops 180650240 | bytes 40907724 | solution.py:255
  812.7 13.5 %add_reduce_fusion.8 = (f32[2048,16]{0,1:T(8,128)S(1)}, f32[2048,16]{0,1:T(8,128)S(1)}) fusion(f32[64]{0:T(128)S(1)} %get-tuple-element.965, f32[64,2048]{1,0:T(8,128)S(1)} %copy-done, f32[64]{0:T(128)S(1)} %get-tuple-element.966, f32[64]{0:T(128)S(1)} %get-tuple-element.967, f32[64,2048]{1,0:T(8,128)S(1)} %copy-done.1, f32[2048,16]{0,1:T(8,128)S(1)} %copy.203, ...), kind=kLoop, calls=%fused_computation.71.clone.1 | loop fusion | flops 90112000 | bytes 2360128 | tf_op jit(solution)/shard_map/while/body/eval_jaxpr/reduce_sum | solution.py:246
  830.1 12.9 %add_reduce_fusion.7 = (f32[2048,16]{0,1:T(8,128)S(1)}, f32[2048,16]{0,1:T(8,128)S(1)}) fusion(f32[2048,16]{0,1:T(8,128)S(1)} %copy.203, f32[64]{0:T(128)S(1)} %get-tuple-element.954, f32[2048,16]{0,1:T(8,128)S(1)} %copy.204, f32[2048,16]{0,1:T(8,128)S(1)} %copy.205, f32[64,2048]{1,0:T(8,128)S(1)} %constant_dynamic-slice_fusion.8, ...), kind=kLoop, calls=%fused_computation.75.clone.1 | loop fusion | flops 90112000 | bytes 2360128 | tf_op jit(solution)/shard_map/while/body/eval_jaxpr/reduce_sum | solution.py:246
  862.8 13.5 %add_reduce_fusion.8 = (f32[2048,16]{0,1:T(8,128)S(1)}, f32[2048,16]{0,1:T(8,128)S(1)}) fusion(f32[64]{0:T(128)S(1)} %get-tuple-element.965, f32[64,2048]{1,0:T(8,128)S(1)} %copy-done, f32[64]{0:T(128)S(1)} %get-tuple-element.966, f32[64]{0:T(128)S(1)} %get-tuple-element.967, f32[64,2048]{1,0:T(8,128)S(1)} %copy-done.1, f32[2048,16]{0,1:T(8,128)S(1)} %copy.203, ...), kind=kLoop, calls=%fused_computation.71.clone.1 | loop fusion | flops 90112000 | bytes 2360128 | tf_op jit(solution)/shard_map/while/body/eval_jaxpr/reduce_sum | solution.py:246
  881.1 12.9 %add_reduce_fusion.7 = (f32[2048,16]{0,1:T(8,128)S(1)}, f32[2048,16]{0,1:T(8,128)S(1)}) fusion(f32[2048,16]{0,1:T(8,128)S(1)} %copy.203, f32[64]{0:T(128)S(1)} %get-tuple-element.954, f32[2048,16]{0,1:T(8,128)S(1)} %copy.204, f32[2048,16]{0,1:T(8,128)S(1)} %copy.205, f32[64,2048]{1,0:T(8,128)S(1)} %constant_dynamic-slice_fusion.8, ...), kind=kLoop, calls=%fused_computation.75.clone.1 | loop fusion | flops 90112000 | bytes 2360128 | tf_op jit(solution)/shard_map/while/body/eval_jaxpr/reduce_sum | solution.py:246
  913.7 13.5 %add_reduce_fusion.8 = (f32[2048,16]{0,1:T(8,128)S(1)}, f32[2048,16]{0,1:T(8,128)S(1)}) fusion(f32[64]{0:T(128)S(1)} %get-tuple-element.965, f32[64,2048]{1,0:T(8,128)S(1)} %copy-done, f32[64]{0:T(128)S(1)} %get-tuple-element.966, f32[64]{0:T(128)S(1)} %get-tuple-element.967, f32[64,2048]{1,0:T(8,128)S(1)} %copy-done.1, f32[2048,16]{0,1:T(8,128)S(1)} %copy.203, ...), kind=kLoop, calls=%fused_computation.71.clone.1 | loop fusion | flops 90112000 | bytes 2360128 | tf_op jit(solution)/shard_map/while/body/eval_jaxpr/reduce_sum | solution.py:246
  932.0 12.9 %add_reduce_fusion.7 = (f32[2048,16]{0,1:T(8,128)S(1)}, f32[2048,16]{0,1:T(8,128)S(1)}) fusion(f32[2048,16]{0,1:T(8,128)S(1)} %copy.203, f32[64]{0:T(128)S(1)} %get-tuple-element.954, f32[2048,16]{0,1:T(8,128)S(1)} %copy.204, f32[2048,16]{0,1:T(8,128)S(1)} %copy.205, f32[64,2048]{1,0:T(8,128)S(1)} %constant_dynamic-slice_fusion.8, ...), kind=kLoop, calls=%fused_computation.75.clone.1 | loop fusion | flops 90112000 | bytes 2360128 | tf_op jit(solution)/shard_map/while/body/eval_jaxpr/reduce_sum | solution.py:246
  964.6 13.5 %add_reduce_fusion.8 = (f32[2048,16]{0,1:T(8,128)S(1)}, f32[2048,16]{0,1:T(8,128)S(1)}) fusion(f32[64]{0:T(128)S(1)} %get-tuple-element.965, f32[64,2048]{1,0:T(8,128)S(1)} %copy-done, f32[64]{0:T(128)S(1)} %get-tuple-element.966, f32[64]{0:T(128)S(1)} %get-tuple-element.967, f32[64,2048]{1,0:T(8,128)S(1)} %copy-done.1, f32[2048,16]{0,1:T(8,128)S(1)} %copy.203, ...), kind=kLoop, calls=%fused_computation.71.clone.1 | loop fusion | flops 90112000 | bytes 2360128 | tf_op jit(solution)/shard_map/while/body/eval_jaxpr/reduce_sum | solution.py:246
  982.9 12.9 %add_reduce_fusion.7 = (f32[2048,16]{0,1:T(8,128)S(1)}, f32[2048,16]{0,1:T(8,128)S(1)}) fusion(f32[2048,16]{0,1:T(8,128)S(1)} %copy.203, f32[64]{0:T(128)S(1)} %get-tuple-element.954, f32[2048,16]{0,1:T(8,128)S(1)} %copy.204, f32[2048,16]{0,1:T(8,128)S(1)} %copy.205, f32[64,2048]{1,0:T(8,128)S(1)} %constant_dynamic-slice_fusion.8, ...), kind=kLoop, calls=%fused_computation.75.clone.1 | loop fusion | flops 90112000 | bytes 2360128 | tf_op jit(solution)/shard_map/while/body/eval_jaxpr/reduce_sum | solution.py:246
  1004.8 103.6 %all-reduce.3.cloned.1.call-done = (f32[2048,16]{0,1:T(8,128)}, f32[2048,16]{0,1:T(8,128)}) async-done(((f32[2048,16]{0,1:T(8,128)}, f32[2048,16]{0,1:T(8,128)}), (f32[2048,16]{0,1:T(8,128)}, f32[2048,16]{0,1:T(8,128)})) %all-reduce.3.cloned.1.call-update) | async-done | bytes 262160 | tf_op jit(solution)/shard_map/psum | solution.py:266
  (439 shorter events, 244.7 us)
Async XLA Ops:
  7.2 10.2 copy-start.36
  10.1 33.0 %all-to-all-start = ((bf16[1,8,32,2048]{3,2,0,1:T(8,128)(2,1)}), bf16[1,8,32,2048]{3,2,0,1:T(8,128)(2,1)S(1)}, u32[]{:S(2)}, u32[]{:S(2)}) async-start(bf16[1,8,32,2048]{3,2,0,1:T(8,128)(2,1)} %bitcast.6), calls=%async_computation | async-start | bytes 2097152 | tf_op jit(solution)/shard_map/all_to_all | solution.py:177
  47.1 52.0 %all-to-all-start.2 = ((f32[1,8,32,2048]{3,2,0,1:T(8,128)}), f32[1,8,32,2048]{3,2,0,1:T(8,128)S(1)}, u32[]{:S(2)}, u32[]{:S(2)}) async-start(f32[1,8,32,2048]{3,2,0,1:T(8,128)} %copy.120), calls=%async_computation.2 | async-start | bytes 4194304 | tf_op jit(solution)/shard_map/all_to_all | solution.py:103
  57.4 46.3 %copy-start.27 = (f32[2048,16]{0,1:T(8,128)S(1)}, f32[2048,16]{0,1:T(8,128)}, u32[]{:S(2)}) copy-start(f32[2048,16]{0,1:T(8,128)} %param.16) | copy-start | bytes 393220
  99.1 136.0 %all-to-all-start.1 = ((f32[1,8,32,2048]{3,2,0,1:T(8,128)}), f32[1,8,32,2048]{3,2,0,1:T(8,128)}, u32[]{:S(2)}, u32[]{:S(2)}) async-start(f32[1,8,32,2048]{3,2,0,1:T(8,128)} %copy.116), calls=%async_computation.1 | async-start | bytes 4194304 | tf_op jit(solution)/shard_map/all_to_all | solution.py:102
  235.1 6.7 copy-start.7
  235.1 6.7 copy-start.10
  235.2 6.7 copy-start.11
  241.9 8.5 copy-start.9
  241.9 8.5 copy-start.12
  241.9 8.5 copy-start.13
  250.4 9.0 copy-start.14
  250.4 12.2 %copy-start.16 = (f32[1,256,2048]{1,2,0:T(8,128)}, f32[1,256,2048]{1,2,0:T(8,128)S(1)}, u32[]{:S(2)}) copy-start(f32[1,256,2048]{1,2,0:T(8,128)S(1)} %get-tuple-element.692) | copy-start | bytes 6291460
  267.5 6.1 copy-start.17
  267.5 53.4 %all-to-all-start.3 = ((f32[1,8,32,2048]{3,2,0,1:T(8,128)}), f32[1,8,32,2048]{3,2,0,1:T(8,128)}, u32[]{:S(2)}, u32[]{:S(2)}) async-start(f32[1,8,32,2048]{3,2,0,1:T(8,128)} %bitcast.213), calls=%async_computation.3 | async-start | bytes 4194304 | tf_op jit(solution)/shard_map/all_to_all | solution.py:130
  320.9 52.4 %all-to-all-start.4 = ((f32[1,8,32,2048]{3,2,0,1:T(8,128)}), f32[1,8,32,2048]{3,2,0,1:T(8,128)S(1)}, u32[]{:S(2)}, u32[]{:S(2)}) async-start(f32[1,8,32,2048]{3,2,0,1:T(8,128)} %bitcast.44), calls=%async_computation.4 | async-start | bytes 4194304 | tf_op jit(solution)/shard_map/all_to_all | solution.py:131
  379.4 52.0 %copy-start.25 = (bf16[1,256,2048]{2,1,0:T(8,128)(2,1)S(1)}, bf16[1,256,2048]{2,1,0:T(8,128)(2,1)}, u32[]{:S(2)}) copy-start(bf16[1,256,2048]{2,1,0:T(8,128)(2,1)} %param.11) | copy-start | bytes 3145732
  500.1 51.8 %all-to-all-start.8 = ((f32[1,8,32,2048]{3,2,0,1:T(8,128)}), f32[1,8,32,2048]{3,2,0,1:T(8,128)}, u32[]{:S(2)}, u32[]{:S(2)}) async-start(f32[1,8,32,2048]{3,2,0,1:T(8,128)} %copy.137), calls=%async_computation.8 | async-start | bytes 4194304 | tf_op jit(solution)/shard_map/all_to_all | solution.py:103
  551.9 52.0 %all-to-all-start.7 = ((f32[1,8,32,2048]{3,2,0,1:T(8,128)}), f32[1,8,32,2048]{3,2,0,1:T(8,128)S(1)}, u32[]{:S(2)}, u32[]{:S(2)}) async-start(f32[1,8,32,2048]{3,2,0,1:T(8,128)} %copy.134), calls=%async_computation.7 | async-start | bytes 4194304 | tf_op jit(solution)/shard_map/all_to_all | solution.py:102
  628.2 7.8 copy-start.4
  628.2 7.8 copy-start.5
  636.0 52.3 %all-to-all-start.9 = ((f32[1,8,32,2048]{3,2,0,1:T(8,128)}), f32[1,8,32,2048]{3,2,0,1:T(8,128)}, u32[]{:S(2)}, u32[]{:S(2)}) async-start(f32[1,8,32,2048]{3,2,0,1:T(8,128)} %bitcast.212), calls=%async_computation.9 | async-start | bytes 4194304 | tf_op jit(solution)/shard_map/all_to_all | solution.py:130
  688.4 89.9 %all-to-all-start.10 = ((f32[1,8,32,2048]{3,2,0,1:T(8,128)}), f32[1,8,32,2048]{3,2,0,1:T(8,128)}, u32[]{:S(2)}, u32[]{:S(2)}) async-start(f32[1,8,32,2048]{3,2,0,1:T(8,128)} %bitcast.211), calls=%async_computation.10 | async-start | bytes 4194304 | tf_op jit(solution)/shard_map/all_to_all | solution.py:131
  786.3 214.4 %all-to-all-start.11 = ((f32[1,8,32,2048]{3,2,0,1:T(8,128)}), f32[1,8,32,2048]{3,2,0,1:T(8,128)}, u32[]{:S(2)}, u32[]{:S(2)}) async-start(f32[1,8,32,2048]{3,2,0,1:T(8,128)} %copy.148), calls=%async_computation.11 | async-start | bytes 4194304 | tf_op jit(solution)/shard_map/all_to_all | solution.py:199
  793.5 314.8 %all-reduce.3.cloned.1.call-start = ((), (), s32[]{:S(2)}) async-start(), calls=%async_computation.12 | async-start | bytes 524288 | tf_op jit(solution)/shard_map/psum | solution.py:266
  794.4 6.0 copy-start.23
  812.1 14.2 %copy-start.33 = (f32[2048,16]{0,1:T(8,128)S(1)}, f32[2048,16]{0,1:T(8,128)}, u32[]{:S(2)}) copy-start(f32[2048,16]{0,1:T(8,128)} %get-tuple-element.1055) | copy-start | bytes 393220 | tf_op jit(solution)/shard_map/while
  812.7 14.3 %copy-start.38 = (f32[256]{0:T(256)S(1)}, f32[256]{0:T(256)}, u32[]{:S(2)}) copy-start(f32[256]{0:T(256)} %get-tuple-element.1086) | copy-start | bytes 3076 | tf_op jit(solution)/shard_map/while
  827.7 15.4 %copy-start.29 = (f32[2048,16]{0,1:T(8,128)S(1)}, f32[2048,16]{0,1:T(8,128)}, u32[]{:S(2)}) copy-start(f32[2048,16]{0,1:T(8,128)} %get-tuple-element.1053) | copy-start | bytes 393220 | tf_op jit(solution)/shard_map/while
  827.7 15.4 %copy-start.31 = (f32[2048,16]{0,1:T(8,128)S(1)}, f32[2048,16]{0,1:T(8,128)}, u32[]{:S(2)}) copy-start(f32[2048,16]{0,1:T(8,128)} %get-tuple-element.1054) | copy-start | bytes 393220 | tf_op jit(solution)/shard_map/while
  828.8 15.7 %copy-start.24 = (f32[256,2048]{1,0:T(8,128)S(1)}, f32[256,2048]{1,0:T(8,128)}, u32[]{:S(2)}) copy-start(f32[256,2048]{1,0:T(8,128)} %copy-done.23) | copy-start | bytes 6291460 | tf_op jit(solution)/shard_map/while
  844.4 6.0 copy-start.23
  862.1 14.2 %copy-start.33 = (f32[2048,16]{0,1:T(8,128)S(1)}, f32[2048,16]{0,1:T(8,128)}, u32[]{:S(2)}) copy-start(f32[2048,16]{0,1:T(8,128)} %get-tuple-element.1055) | copy-start | bytes 393220 | tf_op jit(solution)/shard_map/while
  862.7 15.2 %copy-start.38 = (f32[256]{0:T(256)S(1)}, f32[256]{0:T(256)}, u32[]{:S(2)}) copy-start(f32[256]{0:T(256)} %get-tuple-element.1086) | copy-start | bytes 3076 | tf_op jit(solution)/shard_map/while
  878.6 15.4 %copy-start.29 = (f32[2048,16]{0,1:T(8,128)S(1)}, f32[2048,16]{0,1:T(8,128)}, u32[]{:S(2)}) copy-start(f32[2048,16]{0,1:T(8,128)} %get-tuple-element.1053) | copy-start | bytes 393220 | tf_op jit(solution)/shard_map/while
  878.6 15.4 %copy-start.31 = (f32[2048,16]{0,1:T(8,128)S(1)}, f32[2048,16]{0,1:T(8,128)}, u32[]{:S(2)}) copy-start(f32[2048,16]{0,1:T(8,128)} %get-tuple-element.1054) | copy-start | bytes 393220 | tf_op jit(solution)/shard_map/while
  879.7 15.7 %copy-start.24 = (f32[256,2048]{1,0:T(8,128)S(1)}, f32[256,2048]{1,0:T(8,128)}, u32[]{:S(2)}) copy-start(f32[256,2048]{1,0:T(8,128)} %copy-done.23) | copy-start | bytes 6291460 | tf_op jit(solution)/shard_map/while
  895.4 6.0 copy-start.23
  913.0 14.2 %copy-start.33 = (f32[2048,16]{0,1:T(8,128)S(1)}, f32[2048,16]{0,1:T(8,128)}, u32[]{:S(2)}) copy-start(f32[2048,16]{0,1:T(8,128)} %get-tuple-element.1055) | copy-start | bytes 393220 | tf_op jit(solution)/shard_map/while
  913.7 15.2 %copy-start.38 = (f32[256]{0:T(256)S(1)}, f32[256]{0:T(256)}, u32[]{:S(2)}) copy-start(f32[256]{0:T(256)} %get-tuple-element.1086) | copy-start | bytes 3076 | tf_op jit(solution)/shard_map/while
  929.5 15.4 %copy-start.29 = (f32[2048,16]{0,1:T(8,128)S(1)}, f32[2048,16]{0,1:T(8,128)}, u32[]{:S(2)}) copy-start(f32[2048,16]{0,1:T(8,128)} %get-tuple-element.1053) | copy-start | bytes 393220 | tf_op jit(solution)/shard_map/while
  929.5 15.4 %copy-start.31 = (f32[2048,16]{0,1:T(8,128)S(1)}, f32[2048,16]{0,1:T(8,128)}, u32[]{:S(2)}) copy-start(f32[2048,16]{0,1:T(8,128)} %get-tuple-element.1054) | copy-start | bytes 393220 | tf_op jit(solution)/shard_map/while
  930.6 15.7 %copy-start.24 = (f32[256,2048]{1,0:T(8,128)S(1)}, f32[256,2048]{1,0:T(8,128)}, u32[]{:S(2)}) copy-start(f32[256,2048]{1,0:T(8,128)} %copy-done.23) | copy-start | bytes 6291460 | tf_op jit(solution)/shard_map/while
  964.0 14.2 %copy-start.33 = (f32[2048,16]{0,1:T(8,128)S(1)}, f32[2048,16]{0,1:T(8,128)}, u32[]{:S(2)}) copy-start(f32[2048,16]{0,1:T(8,128)} %get-tuple-element.1055) | copy-start | bytes 393220 | tf_op jit(solution)/shard_map/while
  964.6 15.2 %copy-start.38 = (f32[256]{0:T(256)S(1)}, f32[256]{0:T(256)}, u32[]{:S(2)}) copy-start(f32[256]{0:T(256)} %get-tuple-element.1086) | copy-start | bytes 3076 | tf_op jit(solution)/shard_map/while
  980.4 15.4 %copy-start.29 = (f32[2048,16]{0,1:T(8,128)S(1)}, f32[2048,16]{0,1:T(8,128)}, u32[]{:S(2)}) copy-start(f32[2048,16]{0,1:T(8,128)} %get-tuple-element.1053) | copy-start | bytes 393220 | tf_op jit(solution)/shard_map/while
  980.4 15.4 %copy-start.31 = (f32[2048,16]{0,1:T(8,128)S(1)}, f32[2048,16]{0,1:T(8,128)}, u32[]{:S(2)}) copy-start(f32[2048,16]{0,1:T(8,128)} %get-tuple-element.1054) | copy-start | bytes 393220 | tf_op jit(solution)/shard_map/while
  981.6 15.7 %copy-start.24 = (f32[256,2048]{1,0:T(8,128)S(1)}, f32[256,2048]{1,0:T(8,128)}, u32[]{:S(2)}) copy-start(f32[256,2048]{1,0:T(8,128)} %copy-done.23) | copy-start | bytes 6291460 | tf_op jit(solution)/shard_map/while
  (47 other events, 113.2 us)
Sparse Core Ops, SparseCore 0:
  1000.8 107.5 all-reduce.2
where the time goes:
time: 1130 us; the launch traced here: 1120 us
  waiting for transfers between devices  362 us (32%)
  other arithmetic  254 us (22%)
  blocking collectives  178 us (16%)
  matrix products  136 us (12%)
  local copies, waits for them, and re-layouts  116 us (10%)
  starting transfers between devices  49.9 us (4%)
  between operations  15 us (1%)
    reduce_sum x8, other arithmetic, grad_block(): jnp.sum(real_rows * d_real.reshape(shape_three) + imag_rows * d_imag.resh...  106 us
    psum x1, waiting for transfers between devices, shards(): lax.psum((res_part, rate_part, gain_part), ('ctx', 'dp'))  104 us
    all_to_all x2, waiting for transfers between devices, spectrum(): lax.all_to_all(slot_imag, 'ctx', split_axis=1, concat_axis=1, tiled=True)  83.3 us
    all_to_all x2, waiting for transfers between devices, positions(): lax.all_to_all(out_real, 'ctx', split_axis=1, concat_axis=1, tiled=True)  75.2 us
    psum x1, blocking collectives, shards(): lax.psum((res_part, rate_part, gain_part), ('ctx', 'dp'))  69.5 us
    reduce_sum x4, other arithmetic, kernel_block(): jnp.sum(f_imag.reshape(block, channels, mode_count) * residue, axis=-1)  60.5 us
    all_to_all x1, blocking collectives, transform_plan(): lax.all_to_all(gate_blk.reshape(batch_rows, ctx_count, slice_len, channel...  52.1 us
    all_to_all x1, blocking collectives, transform_plan(): lax.all_to_all(conv_sl, 'ctx', split_axis=1, concat_axis=1, tiled=True)  51.9 us
  transfers between devices with their start and end apart: 11, of which 8 were waited for; matrix products, arithmetic and copies ran while one was open for 36% of the time, Pallas kernels for 0%

commit v1 on v0

v1 whole, which is shorter than its diff:
```python
import functools

import jax
import jax.numpy as jnp
import numpy as np
from jax import lax
from jax.experimental import pallas as pl
from jax.experimental.pallas import tpu as pltpu
from jax.sharding import PartitionSpec as P

EPSILON = 1e-06
LANES = 128
ROWS = 8
F32 = jnp.float32
BF16 = jnp.bfloat16
VMEM_LIMIT = 40 * 1024 * 1024


def fourier(length):
    freq = 2 * np.arange(length)[:, None] + 1
    phase = (freq * np.arange(length)[None, :]) % (4 * length) * (2.0 * np.pi / (4 * length))
    full = np.concatenate([np.cos(phase), -np.sin(phase)], axis=0).astype(np.float32)
    return full


def halves(full):
    high = full.astype(jnp.bfloat16)
    low = (full - high.astype(np.float32)).astype(jnp.bfloat16)
    return jnp.asarray(high), jnp.asarray(low)


def split(x):
    high = x.astype(BF16)
    return high, (x - high.astype(F32)).astype(BF16)


def dot(a, b):
    return jnp.dot(a, b, preferred_element_type=F32)


def dot3(a_high, a_low, x):
    high, low = split(x)
    return dot(a_high, high) + (dot(a_high, low) + dot(a_low, high))


def spread(ref, cols):
    return jnp.stack(
        [jnp.broadcast_to(ref[m : m + 1, cols], (ROWS, LANES)) for m in range(ref.shape[0])]
    )


def sublane():
    return lax.broadcasted_iota(jnp.int32, (1, ROWS, LANES), 1).astype(F32)


def group(i):
    return pl.ds(pl.multiple_of(i * LANES, LANES), LANES)


def evaluate(start, step, tiles):
    term = start
    for i in range(tiles):
        yield jnp.sum(term, axis=0)
        if i + 1 < tiles:
            term = term * step


def combine(pieces, decay_block, gap):
    total = pieces[-1]
    slope = jnp.zeros_like(total)
    for piece in pieces[-2::-1]:
        slope = decay_block * (slope + total)
        total = piece + decay_block * total
    return total, slope * gap


def state_kernel(k_ref, v_ref, lam_ref, val_ref, s_ref):
    length, width = k_ref.shape

    def body(i, _):
        cols = group(i)
        lam = spread(lam_ref, cols)
        step = jnp.exp(-ROWS * lam)
        acc = jnp.zeros_like(lam)
        for a in range(0, length, 16):
            vals = (k_ref[a : a + 16, cols].astype(F32) * v_ref[a : a + 16, cols].astype(F32)).astype(BF16)
            val_ref[a : a + 16, cols] = vals
            vals = vals.astype(F32)
            acc = acc * step + vals[None, :ROWS]
            acc = acc * step + vals[None, ROWS:]
        weight = jnp.exp(-lam * (ROWS - 1 - sublane()))
        s_ref[:, cols] = jnp.sum(acc * weight, axis=1).astype(s_ref.dtype)
        return 0

    lax.fori_loop(0, width // LANES, body, 0)


def local_kernel(val_ref, lam_ref, res_ref, fh_ref, fl_ref, th_ref, tl_ref,
                 conv_ref, vs_ref, ks_ref, slope_ref, ker):
    length, width = val_ref.shape
    tiles = length // ROWS

    def body(i, _):
        cols = group(i)
        lam = spread(lam_ref, cols)
        step = jnp.exp(-ROWS * lam)
        start = spread(res_ref, cols) * jnp.exp(-lam * sublane())
        for a, tile in enumerate(evaluate(start, step, tiles)):
            ker[a * ROWS : (a + 1) * ROWS, cols] = tile
        acc = jnp.zeros_like(lam)
        for a in range(0, length, 16):
            vals = val_ref[a : a + 16, cols].astype(F32)
            for h in (0, ROWS):
                away = (length - 1 - a - h) - sublane()[0]
                acc = acc * step + (vals[h : h + ROWS] * away)[None]
        weight = jnp.exp(-lam * (ROWS - 1 - sublane()))
        slope_ref[:, cols] = jnp.sum(acc * weight, axis=1).astype(slope_ref.dtype)
        return 0

    lax.fori_loop(0, width // LANES, body, 0)
    vals = val_ref[...]
    vs = dot(fh_ref[...], vals) + dot(fl_ref[...], vals)
    vs_ref[...] = vs
    ks = dot3(fh_ref[...], fl_ref[...], ker[...])
    ks_ref[...] = ks
    vr, vi = vs[:length], vs[length:]
    kr, ki = ks[:length], ks[length:]
    prod = jnp.concatenate([vr * kr - vi * ki, vr * ki + vi * kr], axis=0) * (1.0 / length)
    conv_ref[...] = dot3(th_ref[...], tl_ref[...], prod)


def forward_kernel(n_in, length_gap, *refs):
    pieces, (lam_ref, res_ref, conv_in_ref, q_ref, og_ref, gain_ref,
             conv_ref, sums_ref, state_ref, held) = refs[:n_in], refs[n_in:]
    length, width = q_ref.shape

    @pl.when(pl.program_id(0) == 0)
    def _():
        sums_ref[...] = jnp.zeros_like(sums_ref)

    def body(i, _):
        cols = group(i)
        decay_block = jnp.exp(-length_gap * lam_ref[:, cols])
        total, _ = combine([p[:, cols].astype(F32) for p in pieces], decay_block, length_gap)
        state_ref[:, cols] = total
        held[...] = total * res_ref[:, cols]
        lam = spread(lam_ref, cols)
        step = jnp.exp(-ROWS * lam)
        start = spread(held, slice(None)) * jnp.exp(-lam * (sublane() + 1.0))
        gain = gain_ref[:, cols]
        tiles = evaluate(start, step, length // ROWS)
        for a in range(0, length, 16):
            rows = slice(a, a + 16)
            conv = conv_in_ref[rows, cols] + jnp.concatenate([next(tiles), next(tiles)], axis=0)
            conv_ref[rows, cols] = conv
            mixed = q_ref[rows, cols].astype(F32) * conv
            scaled = gain * og_ref[rows, cols].astype(F32)
            sums_ref[0, rows] += mixed * mixed
            sums_ref[1, rows] += scaled * mixed
        return 0

    lax.fori_loop(0, width // LANES, body, 0)


def gate_kernel(model_width, sums_ref, peer_ref, lam_ref, conv_ref, q_ref, og_ref, gain_ref,
                y_ref, gq_ref, gate_ref, gain_part_ref, gw_ref, inv_ref, coef_ref):
    length, width = q_ref.shape

    @pl.when(pl.program_id(0) == 0)
    def _():
        squares = jnp.sum(sums_ref[0] + peer_ref[0], axis=1, keepdims=True)
        inner = jnp.sum(sums_ref[1] + peer_ref[1], axis=1, keepdims=True)
        inv = lax.rsqrt(squares / model_width + EPSILON)
        coef = inv * inv * inv * inner / model_width
        inv_ref[...] = jnp.broadcast_to(inv, inv_ref.shape)
        coef_ref[...] = jnp.broadcast_to(coef, coef_ref.shape)

    def body(i, _):
        cols = group(i)
        lam = spread(lam_ref, cols)
        step = jnp.exp(-ROWS * lam)
        acc = jnp.zeros_like(lam)
        gain = gain_ref[:, cols]
        gain_acc = jnp.zeros((16, LANES), F32)
        for a in range(length - 16, -1, -16):
            rows = slice(a, a + 16)
            inv = inv_ref[rows]
            q = q_ref[rows, cols].astype(F32)
            og = og_ref[rows, cols].astype(F32)
            conv = conv_ref[rows, cols]
            mixed = q * conv
            normed = mixed * inv
            y_ref[rows, cols] = (gain * normed).astype(BF16)
            gain_acc = gain_acc + og * normed
            mixed_grad = inv * (gain * og) - mixed * coef_ref[rows]
            gq_ref[rows, cols] = (mixed_grad * conv).astype(BF16)
            gate = mixed_grad * q
            gate_ref[rows, cols] = gate
            acc = acc * step + gate[None, ROWS:]
            acc = acc * step + gate[None, :ROWS]
        gain_part_ref[:, cols] = jnp.sum(gain_acc, axis=0, keepdims=True)
        weight = jnp.exp(-lam * (sublane() + 1.0))
        gw_ref[:, cols] = jnp.sum(acc * weight, axis=1)
        return 0

    lax.fori_loop(0, width // LANES, body, 0)


def backward_kernel(n_in, length_gap, *refs):
    pieces, slopes = refs[:n_in], refs[n_in : 2 * n_in]
    (lam_ref, res_ref, gate_ref, vs_ref, ks_ref, state_ref, gw_ref, gain_part_ref,
     fh_ref, fl_ref, th_ref, tl_ref, vg_ref, grads_ref, kg) = refs[2 * n_in :]
    length, width = gate_ref.shape
    gs = dot3(fh_ref[...], fl_ref[...], gate_ref[...])
    gr, gi = gs[:length], gs[length:]
    vr, vi = vs_ref[:length], vs_ref[length:]
    prod = jnp.concatenate([gr * vr + gi * vi, gi * vr - gr * vi], axis=0) * (1.0 / length)
    kg[...] = dot3(th_ref[...], tl_ref[...], prod)
    kr, ki = ks_ref[:length], ks_ref[length:]
    prod = jnp.concatenate([gr * kr + gi * ki, gi * kr - gr * ki], axis=0) * (1.0 / length)
    vg_ref[...] = dot3(th_ref[...], tl_ref[...], prod)

    def body(i, _):
        cols = group(i)
        lam = spread(lam_ref, cols)
        step = jnp.exp(-ROWS * lam)
        acc_r = jnp.zeros_like(lam)
        acc_s = jnp.zeros_like(lam)
        for a in range(length - ROWS, -1, -ROWS):
            tile = kg[a : a + ROWS, cols]
            acc_r = acc_r * step + tile[None]
            acc_s = acc_s * step + (tile * (sublane()[0] + float(a)))[None]
        weight = jnp.exp(-lam * sublane())
        part_r = jnp.sum(acc_r * weight, axis=1)
        part_s = jnp.sum(acc_s * weight, axis=1)
        acc_g = jnp.zeros_like(lam)
        for a in range(length - ROWS, -1, -ROWS):
            tile = gate_ref[a : a + ROWS, cols]
            acc_g = acc_g * step + (tile * (sublane()[0] + float(a + 1)))[None]
        g_one = jnp.sum(acc_g * jnp.exp(-lam * (sublane() + 1.0)), axis=1)
        lam_rows = lam_ref[:, cols]
        decay_block = jnp.exp(-length_gap * lam_rows)
        _, moved = combine([p[:, cols].astype(F32) for p in pieces], decay_block, length_gap)
        slope, _ = combine([p[:, cols].astype(F32) for p in slopes], decay_block, length_gap)
        state = state_ref[:, cols]
        gw = gw_ref[:, cols]
        total_r = part_r + gw * state
        total_s = part_s + g_one * state + gw * (slope + moved)
        modes = lam_rows.shape[0]
        grads_ref[i, :modes] = total_r.astype(grads_ref.dtype)
        grads_ref[i, modes : 2 * modes] = (-lam_rows * res_ref[:, cols] * total_s).astype(grads_ref.dtype)
        grads_ref[i, 2 * modes :] = jnp.broadcast_to(gain_part_ref[:, cols], (16, LANES)).astype(grads_ref.dtype)
        return 0

    lax.fori_loop(0, width // LANES, body, 0)


def finish_kernel(n_in, length_gap, *refs):
    pieces, (lam_ref, res_ref, vg_ref, k_ref, v_ref, gk_ref, gv_ref, held) = refs[:n_in], refs[n_in:]
    length, width = k_ref.shape

    def body(i, _):
        cols = group(i)
        decay_block = jnp.exp(-length_gap * lam_ref[:, cols])
        total, _ = combine([p[:, cols].astype(F32) for p in pieces], decay_block, length_gap)
        held[...] = total * res_ref[:, cols]
        lam = spread(lam_ref, cols)
        step = jnp.exp(-ROWS * lam)
        start = spread(held, slice(None)) * jnp.exp(-lam * (ROWS - 1 - sublane()))
        tiles = evaluate(start, step, length // ROWS)
        for a in range(length - 16, -1, -16):
            rows = slice(a, a + 16)
            upper = next(tiles)
            grad = vg_ref[rows, cols] + jnp.concatenate([next(tiles), upper], axis=0)
            gk_ref[rows, cols] = (grad * v_ref[rows, cols].astype(F32)).astype(BF16)
            gv_ref[rows, cols] = (grad * k_ref[rows, cols].astype(F32)).astype(BF16)
        return 0

    lax.fori_loop(0, width // LANES, body, 0)


def call(kernel, grid, ins, outs, scratch, flops):
    moved = sum(a.size * a.dtype.itemsize for a, _, _ in ins)
    moved += sum(int(np.prod(s)) * jnp.dtype(d).itemsize for s, d, _, _ in outs)
    return pl.pallas_call(
        kernel,
        grid=(grid,),
        in_specs=[pl.BlockSpec(b, m) for _, b, m in ins],
        out_specs=[pl.BlockSpec(b, m) for _, _, b, m in outs],
        out_shape=[jax.ShapeDtypeStruct(s, d) for s, d, _, _ in outs],
        scratch_shapes=scratch,
        compiler_params=pltpu.CompilerParams(
            dimension_semantics=("arbitrary",), vmem_limit_bytes=VMEM_LIMIT
        ),
        cost_estimate=pl.CostEstimate(flops=flops, bytes_accessed=moved, transcendentals=0),
    )(*[a for a, _, _ in ins])


def exchange(x, count, forward):
    if count <= 16:
        pieces = []
        for j in range(1, count):
            pairs = [(i, i + j) if forward else (i + j, i) for i in range(count - j)]
            pieces.append(lax.ppermute(x, "ctx", pairs))
        return pieces
    rank = lax.axis_index("ctx")
    every = lax.all_gather(x, "ctx")
    pieces = []
    for j in range(1, count):
        source = rank - j if forward else rank + j
        inside = (source >= 0) & (source < count)
        piece = lax.dynamic_index_in_dim(every, jnp.clip(source, 0, count - 1), 0, keepdims=False)
        pieces.append(jnp.where(inside, piece, jnp.zeros_like(piece)))
    return pieces


def shards(q_stream, k_stream, v_stream, out_grad, norm_gain, residue, rate):
    count = lax.axis_size("ctx")
    _, length, channels = q_stream.shape
    seq_len = length * count
    modes = residue.shape[1]
    model_width = float(channels * lax.axis_size("chan"))
    groups = channels // LANES
    width = min(channels, 512)
    grid = channels // width
    q, k, v, og = (x[0] for x in (q_stream, k_stream, v_stream, out_grad))
    lam = (jnp.exp(rate) / seq_len).T
    res = residue.T
    gain = norm_gain[None]
    full = fourier(length)
    fh, fl = halves(full)
    th, tl = halves(full.T)

    def wide(rows):
        return ((rows, width), lambda i: (0, i))

    def fixed(shape):
        return (shape, lambda i: (0,) * len(shape))

    def inputs(*arrays):
        return [(a, *wide(a.shape[0])) for a in arrays]

    def outputs(*rows_types):
        return [((r, channels), d, *wide(r)) for r, d in rows_types]

    basis = [(x, *fixed(x.shape)) for x in (fh, fl, th, tl)]
    unit = 2 * length * channels * modes

    vals, state = call(
        state_kernel, grid, inputs(k, v, lam), outputs((length, BF16), (modes, BF16)), [], unit
    )
    pieces = exchange(state, count, True)
    conv_local, vs, ks, slope = call(
        local_kernel, grid, inputs(vals, lam, res) + basis,
        outputs((length, F32), (2 * length, F32), (2 * length, F32), (modes, BF16)),
        [pltpu.VMEM((length, width), F32)], 16 * length * length * channels,
    )
    slopes = exchange(slope, count, True)
    sums_shape = (2, length, LANES)
    conv, sums, carried = call(
        functools.partial(forward_kernel, count - 1, float(length)), grid,
        inputs(*pieces, lam, res, conv_local, q, og, gain),
        outputs((length, F32)) + [(sums_shape, F32, *fixed(sums_shape))] + outputs((modes, F32)),
        [pltpu.VMEM((modes, LANES), F32)], unit,
    )
    peers = lax.ppermute(sums, "chan", [(0, 1), (1, 0)])
    y_out, grad_q, gate, gain_part, gw = call(
        functools.partial(gate_kernel, model_width), grid,
        [(sums, *fixed(sums_shape)), (peers, *fixed(sums_shape))] + inputs(lam, conv, q, og, gain),
        outputs((length, BF16), (length, BF16), (length, F32), (1, F32), (modes, F32)),
        [pltpu.VMEM((length, LANES), F32)] * 2, unit,
    )
    later = exchange(gw.astype(BF16), count, False)
    rows = 2 * modes + 16
    vg_local, grads = call(
        functools.partial(backward_kernel, count - 1, float(length)), grid,
        inputs(*pieces, *slopes, lam, res, gate, vs, ks, carried, gw, gain_part) + basis,
        outputs((length, F32))
        + [((groups, rows, LANES), BF16, (width // LANES, rows, LANES), lambda i: (i, 0, 0))],
        [pltpu.VMEM((length, width), F32)], 16 * length * length * channels,
    )
    grad_k, grad_v = call(
        functools.partial(finish_kernel, count - 1, float(length)), grid,
        inputs(*later, lam, res, vg_local, k, v),
        outputs((length, BF16), (length, BF16)),
        [pltpu.VMEM((modes, LANES), F32)], unit,
    )
    both = ("ctx", "dp")
    if count * lax.axis_size("dp") == groups:
        parts = lax.all_to_all(grads, both, 0, 0)
        mine = jnp.sum(parts.astype(F32), axis=0).astype(BF16)
        total = lax.all_to_all(jnp.broadcast_to(mine[None], grads.shape), both, 0, 0).astype(F32)
    else:
        total = lax.psum(grads.astype(F32), both)
    total = total.transpose(0, 2, 1).reshape(channels, rows)
    return (
        y_out[None],
        grad_q[None],
        grad_k[None],
        grad_v[None],
        total[:, :modes],
        total[:, modes : 2 * modes],
        total[:, 2 * modes],
    )


def solution(mesh):
    streams = P("dp", "ctx", "chan")
    in_specs = (streams,) * 4 + (P("chan"), P("chan", None), P("chan", None))
    out_specs = (streams,) * 4 + (P("chan", None), P("chan", None), P("chan"))
    return jax.shard_map(shards, mesh=mesh, in_specs=in_specs, out_specs=out_specs, check_vma=False)
```

time: 1130 us -> 130 us (0.12)
  waiting for transfers between devices: 362 us -> 14 us
  other arithmetic: 254 us -> 1.04 us
  blocking collectives: 178 us -> 14 us
  matrix products: 136 us -> 0 us
  local copies, waits for them, and re-layouts: 116 us -> 9.43 us
  Pallas kernels: 0 us -> 48.5 us
  between operations: 15 us -> 1.08 us
    all_to_all x10 -> x1, waiting for transfers between devices: 259 us -> 0.01 us  [shards(): lax.all_to_all(jnp.broadcast_to(mine[None], grads.shape), both, 0, 0)]
    reduce_sum x14 -> x1, other arithmetic: 168 us -> 0.04 us  [shards(): mine = jnp.sum(parts.astype(F32), axis=0).astype(BF16)]
    dot_general x24 -> x0, matrix products: 136 us -> none  [the longest x2 27.4 us: spectrum(): a_real = jnp.einsum('kj,xjc->xkc', cosine_a, rows_real, precision=highest)]
    psum x1 -> x0, waiting for transfers between devices: 104 us -> none  [shards(): lax.psum((res_part, rate_part, gain_part), ('ctx', 'dp'))]
    all_to_all x2 -> x1, blocking collectives: 104 us -> 14 us  [shards(): parts = lax.all_to_all(grads, both, 0, 0)]
    psum x3 -> x0, blocking collectives: 74.4 us -> none  [the longest x1 69.5 us: shards(): lax.psum((res_part, rate_part, gain_part), ('ctx', 'dp'))]
    pallas_call x0 -> x6, Pallas kernels: none -> 48.5 us  [call(): pl.pallas_call(kernel, grid=(grid,), in_specs=[pl.BlockSpec(b, m) for _,...]
    all_to_all x10 -> x1, starting transfers between devices: 49.9 us -> 3.52 us  [shards(): lax.all_to_all(jnp.broadcast_to(mine[None], grads.shape), both, 0, 0)]
  transfers between devices with their start and end apart: 11 -> 23, of which waited for: 8 -> 5; matrix products, arithmetic and copies ran while one was open for 36% -> 0% of each run, Pallas kernels for 0% -> 17%
where the time goes in v1:
time: 130 us; the launch traced here: 129 us
  Pallas kernels  48.5 us (37%)
  starting transfers between devices  41.2 us (32%)
  waiting for transfers between devices  14 us (11%)
  blocking collectives  14 us (11%)
  local copies, waits for them, and re-layouts  9.43 us (7%)
    pallas_call x6, Pallas kernels, call(): pl.pallas_call(kernel, grid=(grid,), in_specs=[pl.BlockSpec(b, m) for _,...  48.5 us
    ppermute x21, starting transfers between devices, exchange(): pieces.append(lax.ppermute(x, 'ctx', pairs))  37.6 us
    all_to_all x1, blocking collectives, shards(): parts = lax.all_to_all(grads, both, 0, 0)  14 us
    ppermute x21, waiting for transfers between devices, exchange(): pieces.append(lax.ppermute(x, 'ctx', pairs))  14 us
    unnamed x30, local copies, waits for them, and re-layouts  7.41 us
    all_to_all x1, starting transfers between devices, shards(): lax.all_to_all(jnp.broadcast_to(mine[None], grads.shape), both, 0, 0)  3.52 us
  transfers between devices with their start and end apart: 23, of which 5 were waited for; matrix products, arithmetic and copies ran while one was open for 0% of the time, Pallas kernels for 17%

profile of v1, /device:TPU:0, one launch (start us, length us, event | category | flops | bytes accessed | tf_op | source)
XLA Modules:
  0.0 129.3 jit_solution(18155322088831547625)
XLA Ops:
  0.6 1.0 multiply_bitcast_fusion.lam_ref.refs_7_.refs_14_
  1.6 0.0 copy-start.2
  1.6 1.2 copy-done.2
  2.8 1.2 copy-done.4
  4.1 3.6 %shard_map.162 = (bf16[256,2048]{1,0:T(8,128)(2,1)S(1)}, bf16[16,2048]{1,0:T(8,128)(2,1)S(1)}) custom-call(bf16[256,2048]{1,0:T(8,128)(2,1)S(1)} %bitcast.23, bf16[256,2048]{1,0:T(8,128)(2,1)S(1)} %bitcast.25, f32[16,2048]{1,0:T(8,128)S(1)} %multiply_bitcast_fusion.lam_ref.refs_7_.refs_14_), custom_call_target="tpu_custom_call" | custom-call | flops 16777216 | bytes 3342336 | tf_op jit(solution)/shard_map/pallas_call | solution.py:285
  7.7 4.8 %collective-permute-start = (bf16[16,2048]{1,0:T(8,128)(2,1)S(1)}, bf16[16,2048]{1,0:T(8,128)(2,1)S(1)}, u32[]{:S(2)}, u32[]{:S(2)}) collective-permute-start(bf16[16,2048]{1,0:T(8,128)(2,1)S(1)} %get-tuple-element.25), channel_id=1, source_target_pairs={{0,4},{4,8},{8,12},{12,16},{16,20},{20,24},{24,28},{1,5},{5,9},{9,... | collective-permute-start | bytes 196616 | tf_op jit(solution)/shard_map/ppermute | solution.py:304
  12.6 3.5 %collective-permute-start.1 = (bf16[16,2048]{1,0:T(8,128)(2,1)S(1)}, bf16[16,2048]{1,0:T(8,128)(2,1)S(1)}, u32[]{:S(2)}, u32[]{:S(2)}) collective-permute-start(bf16[16,2048]{1,0:T(8,128)(2,1)S(1)} %get-tuple-element.25), channel_id=1, source_target_pairs={{0,8},{4,12},{8,16},{12,20},{16,24},{20,28},{1,9},{5,13},{9,17},{1... | collective-permute-start | bytes 196616 | tf_op jit(solution)/shard_map/ppermute | solution.py:304
  16.1 4.5 %collective-permute-start.2 = (bf16[16,2048]{1,0:T(8,128)(2,1)S(1)}, bf16[16,2048]{1,0:T(8,128)(2,1)S(1)}, u32[]{:S(2)}, u32[]{:S(2)}) collective-permute-start(bf16[16,2048]{1,0:T(8,128)(2,1)S(1)} %get-tuple-element.25), channel_id=1, source_target_pairs={{0,12},{4,16},{8,20},{12,24},{16,28},{1,13},{5,17},{9,21},{13,25},... | collective-permute-start | bytes 196616 | tf_op jit(solution)/shard_map/ppermute | solution.py:304
  20.5 1.9 %collective-permute-start.3 = (bf16[16,2048]{1,0:T(8,128)(2,1)S(1)}, bf16[16,2048]{1,0:T(8,128)(2,1)S(1)}, u32[]{:S(2)}, u32[]{:S(2)}) collective-permute-start(bf16[16,2048]{1,0:T(8,128)(2,1)S(1)} %get-tuple-element.25), channel_id=1, source_target_pairs={{0,16},{4,20},{8,24},{12,28},{1,17},{5,21},{9,25},{13,29},{2,18},{... | collective-permute-start | bytes 196616 | tf_op jit(solution)/shard_map/ppermute | solution.py:304
  22.5 1.3 %collective-permute-start.4 = (bf16[16,2048]{1,0:T(8,128)(2,1)S(1)}, bf16[16,2048]{1,0:T(8,128)(2,1)S(1)}, u32[]{:S(2)}, u32[]{:S(2)}) collective-permute-start(bf16[16,2048]{1,0:T(8,128)(2,1)S(1)} %get-tuple-element.25), channel_id=1, source_target_pairs={{0,20},{4,24},{8,28},{1,21},{5,25},{9,29},{2,22},{6,26},{10,30},{3... | collective-permute-start | bytes 196616 | tf_op jit(solution)/shard_map/ppermute | solution.py:304
  23.8 1.3 %collective-permute-start.5 = (bf16[16,2048]{1,0:T(8,128)(2,1)S(1)}, bf16[16,2048]{1,0:T(8,128)(2,1)S(1)}, u32[]{:S(2)}, u32[]{:S(2)}) collective-permute-start(bf16[16,2048]{1,0:T(8,128)(2,1)S(1)} %get-tuple-element.25), channel_id=1, source_target_pairs={{0,24},{4,28},{1,25},{5,29},{2,26},{6,30},{3,27},{7,31}} | collective-permute-start | bytes 196616 | tf_op jit(solution)/shard_map/ppermute | solution.py:304
  25.1 1.3 %collective-permute-start.6 = (bf16[16,2048]{1,0:T(8,128)(2,1)S(1)}, bf16[16,2048]{1,0:T(8,128)(2,1)S(1)}, u32[]{:S(2)}, u32[]{:S(2)}) collective-permute-start(bf16[16,2048]{1,0:T(8,128)(2,1)S(1)} %get-tuple-element.25), channel_id=1, source_target_pairs={{0,28},{1,29},{2,30},{3,31}} | collective-permute-start | bytes 196616 | tf_op jit(solution)/shard_map/ppermute | solution.py:304
  26.5 0.0 copy-start
  26.5 0.0 copy-start.14
  26.5 12.3 %shard_map.163 = (f32[256,2048]{1,0:T(8,128)S(1)}, f32[512,2048]{1,0:T(8,128)S(1)}, f32[512,2048]{1,0:T(8,128)S(1)}, bf16[16,2048]{1,0:T(8,128)(2,1)S(1)}) custom-call(bf16[256,2048]{1,0:T(8,128)(2,1)S(1)} %get-tuple-element.26.val_ref, f32[16,2048]{1,0:T(8,128)S(1)} %multiply_bitcast_fusion.lam_ref.refs_7_.refs_14_, f32[16,2048]{1,0:T(8,128)S(1)} %bitcast.27, ...), custom_call_target="tpu_custom_call" | custom-call | flops 2147483648 | bytes 12910592 | tf_op jit(solution)/shard_map/pallas_call | solution.py:285
  38.8 2.0 %copy-done.6 = f32[512,2048]{1,0:T(8,128)} copy-done((f32[512,2048]{1,0:T(8,128)}, f32[512,2048]{1,0:T(8,128)S(1)}, u32[]{:S(2)}) %copy-start.6) | copy-done | bytes 4194328
  40.8 4.3 %shard_map.164 = (f32[256,2048]{1,0:T(8,128)S(1)}, f32[2,256,128]{2,1,0:T(8,128)S(1)}, f32[16,2048]{1,0:T(8,128)S(1)}) custom-call(bf16[16,2048]{1,0:T(8,128)(2,1)S(1)} %collective-permute-done.refs_0_, bf16[16,2048]{1,0:T(8,128)(2,1)S(1)} %collective-permute-done.1.refs_1_, bf16[16,2048]{1,0:T(8,128)(2,1)S(1)} %collective-permute-done.2.refs_2_, ...), custom_call_target="tpu_custom_call" | custom-call | flops 16777216 | bytes 7413760 | tf_op jit(solution)/shard_map/pallas_call | solution.py:285
  45.1 0.1 collective-permute-start.7
  45.2 2.2 %collective-permute-start.15 = (bf16[16,2048]{1,0:T(8,128)(2,1)S(1)}, bf16[16,2048]{1,0:T(8,128)(2,1)S(1)}, u32[]{:S(2)}, u32[]{:S(2)}) collective-permute-start(bf16[16,2048]{1,0:T(8,128)(2,1)S(1)} %get-tuple-element.33), channel_id=1, source_target_pairs={{0,4},{4,8},{8,12},{12,16},{16,20},{20,24},{24,28},{1,5},{5,9},{9,... | collective-permute-start | bytes 196616 | tf_op jit(solution)/shard_map/ppermute | solution.py:304
  47.3 1.3 %collective-permute-start.16 = (bf16[16,2048]{1,0:T(8,128)(2,1)S(1)}, bf16[16,2048]{1,0:T(8,128)(2,1)S(1)}, u32[]{:S(2)}, u32[]{:S(2)}) collective-permute-start(bf16[16,2048]{1,0:T(8,128)(2,1)S(1)} %get-tuple-element.33), channel_id=1, source_target_pairs={{0,8},{4,12},{8,16},{12,20},{16,24},{20,28},{1,9},{5,13},{9,17},{1... | collective-permute-start | bytes 196616 | tf_op jit(solution)/shard_map/ppermute | solution.py:304
  48.6 1.3 %collective-permute-start.17 = (bf16[16,2048]{1,0:T(8,128)(2,1)S(1)}, bf16[16,2048]{1,0:T(8,128)(2,1)S(1)}, u32[]{:S(2)}, u32[]{:S(2)}) collective-permute-start(bf16[16,2048]{1,0:T(8,128)(2,1)S(1)} %get-tuple-element.33), channel_id=1, source_target_pairs={{0,12},{4,16},{8,20},{12,24},{16,28},{1,13},{5,17},{9,21},{13,25},... | collective-permute-start | bytes 196616 | tf_op jit(solution)/shard_map/ppermute | solution.py:304
  49.9 1.3 %collective-permute-start.18 = (bf16[16,2048]{1,0:T(8,128)(2,1)S(1)}, bf16[16,2048]{1,0:T(8,128)(2,1)S(1)}, u32[]{:S(2)}, u32[]{:S(2)}) collective-permute-start(bf16[16,2048]{1,0:T(8,128)(2,1)S(1)} %get-tuple-element.33), channel_id=1, source_target_pairs={{0,16},{4,20},{8,24},{12,28},{1,17},{5,21},{9,25},{13,29},{2,18},{... | collective-permute-start | bytes 196616 | tf_op jit(solution)/shard_map/ppermute | solution.py:304
  51.2 1.3 %collective-permute-start.19 = (bf16[16,2048]{1,0:T(8,128)(2,1)S(1)}, bf16[16,2048]{1,0:T(8,128)(2,1)S(1)}, u32[]{:S(2)}, u32[]{:S(2)}) collective-permute-start(bf16[16,2048]{1,0:T(8,128)(2,1)S(1)} %get-tuple-element.33), channel_id=1, source_target_pairs={{0,20},{4,24},{8,28},{1,21},{5,25},{9,29},{2,22},{6,26},{10,30},{3... | collective-permute-start | bytes 196616 | tf_op jit(solution)/shard_map/ppermute | solution.py:304
  52.6 1.3 %collective-permute-start.20 = (bf16[16,2048]{1,0:T(8,128)(2,1)S(1)}, bf16[16,2048]{1,0:T(8,128)(2,1)S(1)}, u32[]{:S(2)}, u32[]{:S(2)}) collective-permute-start(bf16[16,2048]{1,0:T(8,128)(2,1)S(1)} %get-tuple-element.33), channel_id=1, source_target_pairs={{0,24},{4,28},{1,25},{5,29},{2,26},{6,30},{3,27},{7,31}} | collective-permute-start | bytes 196616 | tf_op jit(solution)/shard_map/ppermute | solution.py:304
  53.9 1.3 %collective-permute-start.21 = (bf16[16,2048]{1,0:T(8,128)(2,1)S(1)}, bf16[16,2048]{1,0:T(8,128)(2,1)S(1)}, u32[]{:S(2)}, u32[]{:S(2)}) collective-permute-start(bf16[16,2048]{1,0:T(8,128)(2,1)S(1)} %get-tuple-element.33), channel_id=1, source_target_pairs={{0,28},{1,29},{2,30},{3,31}} | collective-permute-start | bytes 196616 | tf_op jit(solution)/shard_map/ppermute | solution.py:304
  55.2 5.4 %shard_map.165 = (bf16[256,2048]{1,0:T(8,128)(2,1)}, bf16[256,2048]{1,0:T(8,128)(2,1)}, f32[256,2048]{1,0:T(8,128)S(1)}, f32[1,2048]{1,0:T(1,128)S(1)}, f32[16,2048]{1,0:T(8,128)S(1)}) custom-call(f32[2,256,128]{2,1,0:T(8,128)S(1)} %get-tuple-element.28.sums_ref, f32[2,256,128]{2,1,0:T(8,128)S(1)} %collective-permute-done.7.peer_ref, ...), custom_call_target="tpu_custom_call" | custom-call | flops 16777216 | bytes 9191424 | tf_op jit(solution)/shard_map/pallas_call | solution.py:285
  60.6 0.0 copy-start.5
  60.6 18.2 %shard_map.166 = (f32[256,2048]{1,0:T(8,128)S(1)}, bf16[16,48,128]{2,1,0:T(8,128)(2,1)S(1)}) custom-call(bf16[16,2048]{1,0:T(8,128)(2,1)S(1)} %collective-permute-done.refs_0_, bf16[16,2048]{1,0:T(8,128)(2,1)S(1)} %collective-permute-done.1.refs_1_, bf16[16,2048]{1,0:T(8,128)(2,1)S(1)} %collective-permute-done.2.refs_2_, ...), custom_call_target="tpu_custom_call" | custom-call | flops 2147483648 | bytes 15278080 | tf_op jit(solution)/shard_map/pallas_call | solution.py:285
  78.9 1.4 %copy-done.7 = f32[256,2048]{1,0:T(8,128)} copy-done((f32[256,2048]{1,0:T(8,128)}, f32[256,2048]{1,0:T(8,128)S(1)}, u32[]{:S(2)}) %copy-start.7) | copy-done | bytes 2097176
  80.2 14.0 %all_to_all.10 = bf16[16,48,128]{2,1,0:T(8,128)(2,1)S(1)} all-to-all(bf16[16,48,128]{2,1,0:T(8,128)(2,1)S(1)} %get-tuple-element.42), channel_id=1, replica_groups=mesh['ctx'=8,'chan'=2,'dp'=2] {'ctx','dp'}, dimensions={0} | all-to-all | bytes 393216 | tf_op jit(solution)/shard_map/all_to_all | solution.py:390
  94.3 0.7 broadcast_in_dim.26
  95.0 3.5 %all-to-all-start.1 = ((bf16[16,48,128]{2,1,0:T(8,128)(2,1)}), bf16[16,48,128]{2,1,0:T(8,128)(2,1)S(1)}, u32[]{:S(2)}, u32[]{:S(2)}) async-start(bf16[16,48,128]{2,1,0:T(8,128)(2,1)} %broadcast_in_dim.26), calls=%async_computation.1 | async-start | bytes 393216 | tf_op jit(solution)/shard_map/all_to_all | solution.py:392
  98.5 1.3 collective-permute-start.10
  99.8 1.3 collective-permute-start.11
  101.1 1.3 collective-permute-start.12
  102.4 1.3 collective-permute-start.13
  103.7 1.3 collective-permute-start.14
  105.0 1.4 %collective-permute-done.10.refs_2_ = bf16[16,2048]{1,0:T(8,128)(2,1)S(1)} collective-permute-done((bf16[16,2048]{1,0:T(8,128)(2,1)S(1)}, bf16[16,2048]{1,0:T(8,128)(2,1)S(1)}, u32[]{:S(2)}, u32[]{:S(2)}) %collective-permute-start.10) | collective-permute-done | bytes 65568 | tf_op jit(solution)/shard_map/ppermute | solution.py:304
  106.4 1.3 collective-permute-start.8
  107.7 6.1 %collective-permute-done.11.refs_3_ = bf16[16,2048]{1,0:T(8,128)(2,1)S(1)} collective-permute-done((bf16[16,2048]{1,0:T(8,128)(2,1)S(1)}, bf16[16,2048]{1,0:T(8,128)(2,1)S(1)}, u32[]{:S(2)}, u32[]{:S(2)}) %collective-permute-start.11) | collective-permute-done | bytes 65568 | tf_op jit(solution)/shard_map/ppermute | solution.py:304
  113.8 1.3 collective-permute-start.9
  115.1 0.8 collective-permute-done.12.refs_4_
  116.0 2.3 %collective-permute-done.8.refs_0_ = bf16[16,2048]{1,0:T(8,128)(2,1)S(1)} collective-permute-done((bf16[16,2048]{1,0:T(8,128)(2,1)S(1)}, bf16[16,2048]{1,0:T(8,128)(2,1)S(1)}, u32[]{:S(2)}, u32[]{:S(2)}) %collective-permute-start.8) | collective-permute-done | bytes 65568 | tf_op jit(solution)/shard_map/ppermute | solution.py:304
  118.2 3.4 %collective-permute-done.9.refs_1_ = bf16[16,2048]{1,0:T(8,128)(2,1)S(1)} collective-permute-done((bf16[16,2048]{1,0:T(8,128)(2,1)S(1)}, bf16[16,2048]{1,0:T(8,128)(2,1)S(1)}, u32[]{:S(2)}, u32[]{:S(2)}) %collective-permute-start.9) | collective-permute-done | bytes 65568 | tf_op jit(solution)/shard_map/ppermute | solution.py:304
  121.6 1.6 %copy-done.8 = f32[256,2048]{1,0:T(8,128)S(1)} copy-done((f32[256,2048]{1,0:T(8,128)S(1)}, f32[256,2048]{1,0:T(8,128)}, u32[]{:S(2)}) %copy-start.8) | copy-done | bytes 2097176
  123.2 4.7 %shard_map.167 = (bf16[256,2048]{1,0:T(8,128)(2,1)}, bf16[256,2048]{1,0:T(8,128)(2,1)}) custom-call(bf16[16,2048]{1,0:T(8,128)(2,1)S(1)} %collective-permute-done.8.refs_0_, bf16[16,2048]{1,0:T(8,128)(2,1)S(1)} %collective-permute-done.9.refs_1_, bf16[16,2048]{1,0:T(8,128)(2,1)S(1)} %collective-permute-done.10.refs_2_, ...), custom_call_target="tpu_custom_call" | custom-call | flops 16777216 | bytes 7012352 | tf_op jit(solution)/shard_map/pallas_call | solution.py:285
  127.9 0.7 fusion
  128.7 0.6 slice.14
  (42 shorter events, 0.2 us)
Async XLA Ops:
  0.6 25.8 %copy-start.9 = (f32[2048,16]{0,1:T(8,128)S(1)}, f32[2048,16]{0,1:T(8,128)}, u32[]{:S(2)}) copy-start(f32[2048,16]{0,1:T(8,128)} %param.16) | copy-start | bytes 393220
  1.6 1.2 copy-start.2
  2.8 1.2 copy-start.4
  4.1 22.4 %copy-start.10 = (bf16[512,256]{1,0:T(8,128)(2,1)S(1)}, bf16[512,256]{1,0:T(8,128)(2,1)}, u32[]{:S(2)}) copy-start(bf16[512,256]{1,0:T(8,128)(2,1)} %constant.14.clone.fh_ref.refs_22_) | copy-start | bytes 786436
  4.1 22.4 %copy-start.11 = (bf16[512,256]{1,0:T(8,128)(2,1)S(1)}, bf16[512,256]{1,0:T(8,128)(2,1)}, u32[]{:S(2)}) copy-start(bf16[512,256]{1,0:T(8,128)(2,1)} %constant.15.clone.fl_ref.refs_23_) | copy-start | bytes 786436
  4.1 22.4 %copy-start.12 = (bf16[256,512]{1,0:T(8,128)(2,1)S(1)}, bf16[256,512]{1,0:T(8,128)(2,1)}, u32[]{:S(2)}) copy-start(bf16[256,512]{1,0:T(8,128)(2,1)} %constant.16.clone.th_ref.refs_24_) | copy-start | bytes 786436
  4.1 22.4 %copy-start.13 = (bf16[256,512]{1,0:T(8,128)(2,1)S(1)}, bf16[256,512]{1,0:T(8,128)(2,1)}, u32[]{:S(2)}) copy-start(bf16[256,512]{1,0:T(8,128)(2,1)} %constant.17.clone.tl_ref.refs_25_) | copy-start | bytes 786436
  7.7 16.1 %collective-permute-start = (bf16[16,2048]{1,0:T(8,128)(2,1)S(1)}, bf16[16,2048]{1,0:T(8,128)(2,1)S(1)}, u32[]{:S(2)}, u32[]{:S(2)}) collective-permute-start(bf16[16,2048]{1,0:T(8,128)(2,1)S(1)} %get-tuple-element.25), channel_id=1, source_target_pairs={{0,4},{4,8},{8,12},{12,16},{16,20},{20,24},{24,28},{1,5},{5,9},{9,... | collective-permute-start | bytes 196616 | tf_op jit(solution)/shard_map/ppermute | solution.py:304
  12.6 12.5 %collective-permute-start.1 = (bf16[16,2048]{1,0:T(8,128)(2,1)S(1)}, bf16[16,2048]{1,0:T(8,128)(2,1)S(1)}, u32[]{:S(2)}, u32[]{:S(2)}) collective-permute-start(bf16[16,2048]{1,0:T(8,128)(2,1)S(1)} %get-tuple-element.25), channel_id=1, source_target_pairs={{0,8},{4,12},{8,16},{12,20},{16,24},{20,28},{1,9},{5,13},{9,17},{1... | collective-permute-start | bytes 196616 | tf_op jit(solution)/shard_map/ppermute | solution.py:304
  16.1 24.7 %collective-permute-start.2 = (bf16[16,2048]{1,0:T(8,128)(2,1)S(1)}, bf16[16,2048]{1,0:T(8,128)(2,1)S(1)}, u32[]{:S(2)}, u32[]{:S(2)}) collective-permute-start(bf16[16,2048]{1,0:T(8,128)(2,1)S(1)} %get-tuple-element.25), channel_id=1, source_target_pairs={{0,12},{4,16},{8,20},{12,24},{16,28},{1,13},{5,17},{9,21},{13,25},... | collective-permute-start | bytes 196616 | tf_op jit(solution)/shard_map/ppermute | solution.py:304
  20.5 20.2 %collective-permute-start.3 = (bf16[16,2048]{1,0:T(8,128)(2,1)S(1)}, bf16[16,2048]{1,0:T(8,128)(2,1)S(1)}, u32[]{:S(2)}, u32[]{:S(2)}) collective-permute-start(bf16[16,2048]{1,0:T(8,128)(2,1)S(1)} %get-tuple-element.25), channel_id=1, source_target_pairs={{0,16},{4,20},{8,24},{12,28},{1,17},{5,21},{9,25},{13,29},{2,18},{... | collective-permute-start | bytes 196616 | tf_op jit(solution)/shard_map/ppermute | solution.py:304
  22.5 18.3 %collective-permute-start.4 = (bf16[16,2048]{1,0:T(8,128)(2,1)S(1)}, bf16[16,2048]{1,0:T(8,128)(2,1)S(1)}, u32[]{:S(2)}, u32[]{:S(2)}) collective-permute-start(bf16[16,2048]{1,0:T(8,128)(2,1)S(1)} %get-tuple-element.25), channel_id=1, source_target_pairs={{0,20},{4,24},{8,28},{1,21},{5,25},{9,29},{2,22},{6,26},{10,30},{3... | collective-permute-start | bytes 196616 | tf_op jit(solution)/shard_map/ppermute | solution.py:304
  23.8 17.0 %collective-permute-start.5 = (bf16[16,2048]{1,0:T(8,128)(2,1)S(1)}, bf16[16,2048]{1,0:T(8,128)(2,1)S(1)}, u32[]{:S(2)}, u32[]{:S(2)}) collective-permute-start(bf16[16,2048]{1,0:T(8,128)(2,1)S(1)} %get-tuple-element.25), channel_id=1, source_target_pairs={{0,24},{4,28},{1,25},{5,29},{2,26},{6,30},{3,27},{7,31}} | collective-permute-start | bytes 196616 | tf_op jit(solution)/shard_map/ppermute | solution.py:304
  25.1 15.7 %collective-permute-start.6 = (bf16[16,2048]{1,0:T(8,128)(2,1)S(1)}, bf16[16,2048]{1,0:T(8,128)(2,1)S(1)}, u32[]{:S(2)}, u32[]{:S(2)}) collective-permute-start(bf16[16,2048]{1,0:T(8,128)(2,1)S(1)} %get-tuple-element.25), channel_id=1, source_target_pairs={{0,28},{1,29},{2,30},{3,31}} | collective-permute-start | bytes 196616 | tf_op jit(solution)/shard_map/ppermute | solution.py:304
  26.5 14.3 %copy-start = (bf16[1,256,2048]{2,1,0:T(8,128)(2,1)S(1)}, bf16[1,256,2048]{2,1,0:T(8,128)(2,1)}, u32[]{:S(2)}) copy-start(bf16[1,256,2048]{2,1,0:T(8,128)(2,1)} %param.11) | copy-start | bytes 3145732
  26.5 14.3 %copy-start.1 = (bf16[1,256,2048]{2,1,0:T(8,128)(2,1)S(1)}, bf16[1,256,2048]{2,1,0:T(8,128)(2,1)}, u32[]{:S(2)}) copy-start(bf16[1,256,2048]{2,1,0:T(8,128)(2,1)} %param.14) | copy-start | bytes 3145732
  26.5 14.3 %copy-start.14 = (f32[2048]{0:T(1024)S(1)}, f32[2048]{0:T(1024)}, u32[]{:S(2)}) copy-start(f32[2048]{0:T(1024)} %param.15) | copy-start | bytes 24580
  38.8 2.0 %copy-start.6 = (f32[512,2048]{1,0:T(8,128)}, f32[512,2048]{1,0:T(8,128)S(1)}, u32[]{:S(2)}) copy-start(f32[512,2048]{1,0:T(8,128)S(1)} %get-tuple-element.36.refs_18_) | copy-start | bytes 12582916
  45.1 8.8 %collective-permute-start.7 = (f32[2,256,128]{2,1,0:T(8,128)S(1)}, f32[2,256,128]{2,1,0:T(8,128)S(1)}, u32[]{:S(2)}, u32[]{:S(2)}) collective-permute-start(f32[2,256,128]{2,1,0:T(8,128)S(1)} %get-tuple-element.28.sums_ref), channel_id=1, source_target_pairs={{0,2},{2,0},{1,3},{3,1},{4,6},{6,4},{5,7},{7,5},{8,10},{10,8},{9,1... | collective-permute-start | bytes 786440 | tf_op jit(solution)/shard_map/ppermute | solution.py:366
  45.2 6.1 %collective-permute-start.15 = (bf16[16,2048]{1,0:T(8,128)(2,1)S(1)}, bf16[16,2048]{1,0:T(8,128)(2,1)S(1)}, u32[]{:S(2)}, u32[]{:S(2)}) collective-permute-start(bf16[16,2048]{1,0:T(8,128)(2,1)S(1)} %get-tuple-element.33), channel_id=1, source_target_pairs={{0,4},{4,8},{8,12},{12,16},{16,20},{20,24},{24,28},{1,5},{5,9},{9,... | collective-permute-start | bytes 196616 | tf_op jit(solution)/shard_map/ppermute | solution.py:304
  47.3 5.2 %collective-permute-start.16 = (bf16[16,2048]{1,0:T(8,128)(2,1)S(1)}, bf16[16,2048]{1,0:T(8,128)(2,1)S(1)}, u32[]{:S(2)}, u32[]{:S(2)}) collective-permute-start(bf16[16,2048]{1,0:T(8,128)(2,1)S(1)} %get-tuple-element.33), channel_id=1, source_target_pairs={{0,8},{4,12},{8,16},{12,20},{16,24},{20,28},{1,9},{5,13},{9,17},{1... | collective-permute-start | bytes 196616 | tf_op jit(solution)/shard_map/ppermute | solution.py:304
  48.6 12.0 %collective-permute-start.17 = (bf16[16,2048]{1,0:T(8,128)(2,1)S(1)}, bf16[16,2048]{1,0:T(8,128)(2,1)S(1)}, u32[]{:S(2)}, u32[]{:S(2)}) collective-permute-start(bf16[16,2048]{1,0:T(8,128)(2,1)S(1)} %get-tuple-element.33), channel_id=1, source_target_pairs={{0,12},{4,16},{8,20},{12,24},{16,28},{1,13},{5,17},{9,21},{13,25},... | collective-permute-start | bytes 196616 | tf_op jit(solution)/shard_map/ppermute | solution.py:304
  49.9 10.7 %collective-permute-start.18 = (bf16[16,2048]{1,0:T(8,128)(2,1)S(1)}, bf16[16,2048]{1,0:T(8,128)(2,1)S(1)}, u32[]{:S(2)}, u32[]{:S(2)}) collective-permute-start(bf16[16,2048]{1,0:T(8,128)(2,1)S(1)} %get-tuple-element.33), channel_id=1, source_target_pairs={{0,16},{4,20},{8,24},{12,28},{1,17},{5,21},{9,25},{13,29},{2,18},{... | collective-permute-start | bytes 196616 | tf_op jit(solution)/shard_map/ppermute | solution.py:304
  51.2 9.4 %collective-permute-start.19 = (bf16[16,2048]{1,0:T(8,128)(2,1)S(1)}, bf16[16,2048]{1,0:T(8,128)(2,1)S(1)}, u32[]{:S(2)}, u32[]{:S(2)}) collective-permute-start(bf16[16,2048]{1,0:T(8,128)(2,1)S(1)} %get-tuple-element.33), channel_id=1, source_target_pairs={{0,20},{4,24},{8,28},{1,21},{5,25},{9,29},{2,22},{6,26},{10,30},{3... | collective-permute-start | bytes 196616 | tf_op jit(solution)/shard_map/ppermute | solution.py:304
  52.6 8.0 %collective-permute-start.20 = (bf16[16,2048]{1,0:T(8,128)(2,1)S(1)}, bf16[16,2048]{1,0:T(8,128)(2,1)S(1)}, u32[]{:S(2)}, u32[]{:S(2)}) collective-permute-start(bf16[16,2048]{1,0:T(8,128)(2,1)S(1)} %get-tuple-element.33), channel_id=1, source_target_pairs={{0,24},{4,28},{1,25},{5,29},{2,26},{6,30},{3,27},{7,31}} | collective-permute-start | bytes 196616 | tf_op jit(solution)/shard_map/ppermute | solution.py:304
  53.9 6.7 %collective-permute-start.21 = (bf16[16,2048]{1,0:T(8,128)(2,1)S(1)}, bf16[16,2048]{1,0:T(8,128)(2,1)S(1)}, u32[]{:S(2)}, u32[]{:S(2)}) collective-permute-start(bf16[16,2048]{1,0:T(8,128)(2,1)S(1)} %get-tuple-element.33), channel_id=1, source_target_pairs={{0,28},{1,29},{2,30},{3,31}} | collective-permute-start | bytes 196616 | tf_op jit(solution)/shard_map/ppermute | solution.py:304
  60.6 61.0 %copy-start.5 = (bf16[1,256,2048]{2,1,0:T(8,128)(2,1)S(1)}, bf16[1,256,2048]{2,1,0:T(8,128)(2,1)}, u32[]{:S(2)}) copy-start(bf16[1,256,2048]{2,1,0:T(8,128)(2,1)} %param.13) | copy-start | bytes 3145732
  78.9 1.4 %copy-start.7 = (f32[256,2048]{1,0:T(8,128)}, f32[256,2048]{1,0:T(8,128)S(1)}, u32[]{:S(2)}) copy-start(f32[256,2048]{1,0:T(8,128)S(1)} %get-tuple-element.39.refs_9_) | copy-start | bytes 6291460
  80.2 41.4 %copy-start.3 = (bf16[1,256,2048]{2,1,0:T(8,128)(2,1)S(1)}, bf16[1,256,2048]{2,1,0:T(8,128)(2,1)}, u32[]{:S(2)}) copy-start(bf16[1,256,2048]{2,1,0:T(8,128)(2,1)} %param.12) | copy-start | bytes 3145732
  95.0 32.9 %all-to-all-start.1 = ((bf16[16,48,128]{2,1,0:T(8,128)(2,1)}), bf16[16,48,128]{2,1,0:T(8,128)(2,1)S(1)}, u32[]{:S(2)}, u32[]{:S(2)}) async-start(bf16[16,48,128]{2,1,0:T(8,128)(2,1)} %broadcast_in_dim.26), calls=%async_computation.1 | async-start | bytes 393216 | tf_op jit(solution)/shard_map/all_to_all | solution.py:392
  98.5 7.9 %collective-permute-start.10 = (bf16[16,2048]{1,0:T(8,128)(2,1)S(1)}, bf16[16,2048]{1,0:T(8,128)(2,1)S(1)}, u32[]{:S(2)}, u32[]{:S(2)}) collective-permute-start(bf16[16,2048]{1,0:T(8,128)(2,1)S(1)} %convert_element_type.2), channel_id=1, source_target_pairs={{12,0},{16,4},{20,8},{24,12},{28,16},{13,1},{17,5},{21,9},{25,13},... | collective-permute-start | bytes 196616 | tf_op jit(solution)/shard_map/ppermute | solution.py:304
  99.8 14.0 %collective-permute-start.11 = (bf16[16,2048]{1,0:T(8,128)(2,1)S(1)}, bf16[16,2048]{1,0:T(8,128)(2,1)S(1)}, u32[]{:S(2)}, u32[]{:S(2)}) collective-permute-start(bf16[16,2048]{1,0:T(8,128)(2,1)S(1)} %convert_element_type.2), channel_id=1, source_target_pairs={{16,0},{20,4},{24,8},{28,12},{17,1},{21,5},{25,9},{29,13},{18,2},{... | collective-permute-start | bytes 196616 | tf_op jit(solution)/shard_map/ppermute | solution.py:304
  101.1 14.8 %collective-permute-start.12 = (bf16[16,2048]{1,0:T(8,128)(2,1)S(1)}, bf16[16,2048]{1,0:T(8,128)(2,1)S(1)}, u32[]{:S(2)}, u32[]{:S(2)}) collective-permute-start(bf16[16,2048]{1,0:T(8,128)(2,1)S(1)} %convert_element_type.2), channel_id=1, source_target_pairs={{20,0},{24,4},{28,8},{21,1},{25,5},{29,9},{22,2},{26,6},{30,10},{2... | collective-permute-start | bytes 196616 | tf_op jit(solution)/shard_map/ppermute | solution.py:304
  102.4 13.5 %collective-permute-start.13 = (bf16[16,2048]{1,0:T(8,128)(2,1)S(1)}, bf16[16,2048]{1,0:T(8,128)(2,1)S(1)}, u32[]{:S(2)}, u32[]{:S(2)}) collective-permute-start(bf16[16,2048]{1,0:T(8,128)(2,1)S(1)} %convert_element_type.2), channel_id=1, source_target_pairs={{24,0},{28,4},{25,1},{29,5},{26,2},{30,6},{27,3},{31,7}} | collective-permute-start | bytes 196616 | tf_op jit(solution)/shard_map/ppermute | solution.py:304
  103.7 12.2 %collective-permute-start.14 = (bf16[16,2048]{1,0:T(8,128)(2,1)S(1)}, bf16[16,2048]{1,0:T(8,128)(2,1)S(1)}, u32[]{:S(2)}, u32[]{:S(2)}) collective-permute-start(bf16[16,2048]{1,0:T(8,128)(2,1)S(1)} %convert_element_type.2), channel_id=1, source_target_pairs={{28,0},{29,1},{30,2},{31,3}} | collective-permute-start | bytes 196616 | tf_op jit(solution)/shard_map/ppermute | solution.py:304
  106.4 11.8 %collective-permute-start.8 = (bf16[16,2048]{1,0:T(8,128)(2,1)S(1)}, bf16[16,2048]{1,0:T(8,128)(2,1)S(1)}, u32[]{:S(2)}, u32[]{:S(2)}) collective-permute-start(bf16[16,2048]{1,0:T(8,128)(2,1)S(1)} %convert_element_type.2), channel_id=1, source_target_pairs={{4,0},{8,4},{12,8},{16,12},{20,16},{24,20},{28,24},{5,1},{9,5},{13... | collective-permute-start | bytes 196616 | tf_op jit(solution)/shard_map/ppermute | solution.py:304
  113.8 7.8 %collective-permute-start.9 = (bf16[16,2048]{1,0:T(8,128)(2,1)S(1)}, bf16[16,2048]{1,0:T(8,128)(2,1)S(1)}, u32[]{:S(2)}, u32[]{:S(2)}) collective-permute-start(bf16[16,2048]{1,0:T(8,128)(2,1)S(1)} %convert_element_type.2), channel_id=1, source_target_pairs={{8,0},{12,4},{16,8},{20,12},{24,16},{28,20},{9,1},{13,5},{17,9},{2... | collective-permute-start | bytes 196616 | tf_op jit(solution)/shard_map/ppermute | solution.py:304
  121.6 1.6 %copy-start.8 = (f32[256,2048]{1,0:T(8,128)S(1)}, f32[256,2048]{1,0:T(8,128)}, u32[]{:S(2)}) copy-start(f32[256,2048]{1,0:T(8,128)} %copy-done.7) | copy-start | bytes 6291460

commit v2 on v1

--- a/solution.py
+++ b/solution.py
@@ -13,7 +13,7 @@
 ROWS = 8
 F32 = jnp.float32
 BF16 = jnp.bfloat16
-VMEM_LIMIT = 40 * 1024 * 1024
+VMEM_LIMIT = 20 * 1024 * 1024
 
 
 def fourier(length):
@@ -65,13 +65,17 @@
             term = term * step
 
 
-def combine(pieces, decay_block, gap):
-    total = pieces[-1]
-    slope = jnp.zeros_like(total)
-    for piece in pieces[-2::-1]:
-        slope = decay_block * (slope + total)
-        total = piece + decay_block * total
-    return total, slope * gap
+def gather_states(pieces_ref, cols, decay_block, forward):
+    rank = lax.axis_index("ctx")
+    count = pieces_ref.shape[0]
+    total = jnp.zeros_like(decay_block)
+    slope = jnp.zeros_like(decay_block)
+    for s in range(count) if forward else range(count - 1, -1, -1):
+        inside = (s < rank) if forward else (s > rank)
+        piece = pieces_ref[s, :, cols].astype(F32)
+        slope = jnp.where(inside, decay_block * (slope + total), slope)
+        total = jnp.where(inside, decay_block * total + piece, total)
+    return total, slope
 
 
 def state_kernel(k_ref, v_ref, lam_ref, val_ref, s_ref):
@@ -114,7 +118,7 @@
                 away = (length - 1 - a - h) - sublane()[0]
                 acc = acc * step + (vals[h : h + ROWS] * away)[None]
         weight = jnp.exp(-lam * (ROWS - 1 - sublane()))
-        slope_ref[:, cols] = jnp.sum(acc * weight, axis=1).astype(slope_ref.dtype)
+        slope_ref[:, cols] = jnp.sum(acc * weight, axis=1)
         return 0
 
     lax.fori_loop(0, width // LANES, body, 0)
@@ -129,9 +133,8 @@
     conv_ref[...] = dot3(th_ref[...], tl_ref[...], prod)
 
 
-def forward_kernel(n_in, length_gap, *refs):
-    pieces, (lam_ref, res_ref, conv_in_ref, q_ref, og_ref, gain_ref,
-             conv_ref, sums_ref, state_ref, held) = refs[:n_in], refs[n_in:]
+def forward_kernel(pieces_ref, lam_ref, res_ref, conv_in_ref, q_ref, og_ref, gain_ref,
+                   conv_ref, sums_ref, state_ref, moved_ref, held):
     length, width = q_ref.shape
 
     @pl.when(pl.program_id(0) == 0)
@@ -140,9 +143,10 @@
 
     def body(i, _):
         cols = group(i)
-        decay_block = jnp.exp(-length_gap * lam_ref[:, cols])
-        total, _ = combine([p[:, cols].astype(F32) for p in pieces], decay_block, length_gap)
+        decay_block = jnp.exp(-float(length) * lam_ref[:, cols])
+        total, moved = gather_states(pieces_ref, cols, decay_block, True)
         state_ref[:, cols] = total
+        moved_ref[:, cols] = moved * float(length)
         held[...] = total * res_ref[:, cols]
         lam = spread(lam_ref, cols)
         step = jnp.exp(-ROWS * lam)
@@ -206,10 +210,8 @@
     lax.fori_loop(0, width // LANES, body, 0)
 
 
-def backward_kernel(n_in, length_gap, *refs):
-    pieces, slopes = refs[:n_in], refs[n_in : 2 * n_in]
-    (lam_ref, res_ref, gate_ref, vs_ref, ks_ref, state_ref, gw_ref, gain_part_ref,
-     fh_ref, fl_ref, th_ref, tl_ref, vg_ref, grads_ref, kg) = refs[2 * n_in :]
+def backward_kernel(lam_ref, res_ref, gate_ref, vs_ref, ks_ref, state_ref, moved_ref, gw_ref, gain_part_ref,
+                    fh_ref, fl_ref, th_ref, tl_ref, vg_ref, grads_ref, kg):
     length, width = gate_ref.shape
     gs = dot3(fh_ref[...], fl_ref[...], gate_ref[...])
     gr, gi = gs[:length], gs[length:]
@@ -238,35 +240,43 @@
             tile = gate_ref[a : a + ROWS, cols]
             acc_g = acc_g * step + (tile * (sublane()[0] + float(a + 1)))[None]
         g_one = jnp.sum(acc_g * jnp.exp(-lam * (sublane() + 1.0)), axis=1)
-        lam_rows = lam_ref[:, cols]
-        decay_block = jnp.exp(-length_gap * lam_rows)
-        _, moved = combine([p[:, cols].astype(F32) for p in pieces], decay_block, length_gap)
-        slope, _ = combine([p[:, cols].astype(F32) for p in slopes], decay_block, length_gap)
         state = state_ref[:, cols]
         gw = gw_ref[:, cols]
-        total_r = part_r + gw * state
-        total_s = part_s + g_one * state + gw * (slope + moved)
-        modes = lam_rows.shape[0]
-        grads_ref[i, :modes] = total_r.astype(grads_ref.dtype)
-        grads_ref[i, modes : 2 * modes] = (-lam_rows * res_ref[:, cols] * total_s).astype(grads_ref.dtype)
-        grads_ref[i, 2 * modes :] = jnp.broadcast_to(gain_part_ref[:, cols], (16, LANES)).astype(grads_ref.dtype)
-        return 0
-
-    lax.fori_loop(0, width // LANES, body, 0)
-
-
-def finish_kernel(n_in, length_gap, *refs):
-    pieces, (lam_ref, res_ref, vg_ref, k_ref, v_ref, gk_ref, gv_ref, held) = refs[:n_in], refs[n_in:]
+        modes = gw.shape[0]
+        grads_ref[i, :modes] = part_r + gw * state
+        grads_ref[i, modes : 2 * modes] = part_s + g_one * state + gw * moved_ref[:, cols]
+        grads_ref[i, 2 * modes :] = jnp.broadcast_to(gain_part_ref[:, cols], (16, LANES))
+        return 0
+
+    lax.fori_loop(0, width // LANES, body, 0)
+
+
+def adjoint_kernel(length, pieces_ref, lam_ref, res_ref, slope_ref, grads_ref, adj_ref, out_ref):
+    modes, width = lam_ref.shape
+
+    def body(i, _):
+        cols = group(i)
+        lam = lam_ref[:, cols]
+        total, _ = gather_states(pieces_ref, cols, jnp.exp(-length * lam), False)
+        res = res_ref[:, cols]
+        adj_ref[:, cols] = total * res
+        out_ref[i, :modes] = grads_ref[i, :modes].astype(BF16)
+        total_s = grads_ref[i, modes : 2 * modes] + slope_ref[:, cols] * total
+        out_ref[i, modes : 2 * modes] = (-lam * res * total_s).astype(BF16)
+        out_ref[i, 2 * modes :] = grads_ref[i, 2 * modes :].astype(BF16)
+        return 0
+
+    lax.fori_loop(0, width // LANES, body, 0)
+
+
+def finish_kernel(adj_ref, lam_ref, vg_ref, k_ref, v_ref, gk_ref, gv_ref):
     length, width = k_ref.shape
 
     def body(i, _):
         cols = group(i)
-        decay_block = jnp.exp(-length_gap * lam_ref[:, cols])
-        total, _ = combine([p[:, cols].astype(F32) for p in pieces], decay_block, length_gap)
-        held[...] = total * res_ref[:, cols]
-        lam = spread(lam_ref, cols)
-        step = jnp.exp(-ROWS * lam)
-        start = spread(held, slice(None)) * jnp.exp(-lam * (ROWS - 1 - sublane()))
+        lam = spread(lam_ref, cols)
+        step = jnp.exp(-ROWS * lam)
+        start = spread(adj_ref, cols) * jnp.exp(-lam * (ROWS - 1 - sublane()))
         tiles = evaluate(start, step, length // ROWS)
         for a in range(length - 16, -1, -16):
             rows = slice(a, a + 16)
@@ -296,22 +306,8 @@
     )(*[a for a, _, _ in ins])
 
 
-def exchange(x, count, forward):
-    if count <= 16:
-        pieces = []
-        for j in range(1, count):
-            pairs = [(i, i + j) if forward else (i + j, i) for i in range(count - j)]
-            pieces.append(lax.ppermute(x, "ctx", pairs))
-        return pieces
-    rank = lax.axis_index("ctx")
-    every = lax.all_gather(x, "ctx")
-    pieces = []
-    for j in range(1, count):
-        source = rank - j if forward else rank + j
-        inside = (source >= 0) & (source < count)
-        piece = lax.dynamic_index_in_dim(every, jnp.clip(source, 0, count - 1), 0, keepdims=False)
-        pieces.append(jnp.where(inside, piece, jnp.zeros_like(piece)))
-    return pieces
+def exchange(x, count):
+    return lax.all_to_all(jnp.broadcast_to(x[None], (count,) + x.shape), "ctx", 0, 0)
 
 
 def shards(q_stream, k_stream, v_stream, out_grad, norm_gain, residue, rate):
@@ -346,21 +342,24 @@
     basis = [(x, *fixed(x.shape)) for x in (fh, fl, th, tl)]
     unit = 2 * length * channels * modes
 
+    def stacked(array):
+        return [(array, (array.shape[0], array.shape[1], width), lambda i: (0, 0, i))]
+
+    k_far, v_far = (pltpu.with_memory_space_constraint(x, pltpu.HBM) for x in (k, v))
     vals, state = call(
-        state_kernel, grid, inputs(k, v, lam), outputs((length, BF16), (modes, BF16)), [], unit
-    )
-    pieces = exchange(state, count, True)
+        state_kernel, grid, inputs(k_far, v_far, lam), outputs((length, BF16), (modes, BF16)), [], unit
+    )
+    pieces = exchange(state, count)
     conv_local, vs, ks, slope = call(
         local_kernel, grid, inputs(vals, lam, res) + basis,
-        outputs((length, F32), (2 * length, F32), (2 * length, F32), (modes, BF16)),
+        outputs((length, F32), (2 * length, F32), (2 * length, F32), (modes, F32)),
         [pltpu.VMEM((length, width), F32)], 16 * length * length * channels,
     )
-    slopes = exchange(slope, count, True)
     sums_shape = (2, length, LANES)
-    conv, sums, carried = call(
-        functools.partial(forward_kernel, count - 1, float(length)), grid,
-        inputs(*pieces, lam, res, conv_local, q, og, gain),
-        outputs((length, F32)) + [(sums_shape, F32, *fixed(sums_shape))] + outputs((modes, F32)),
+    conv, sums, carried, moved = call(
+        forward_kernel, grid,
+        stacked(pieces) + inputs(lam, res, conv_local, q, og, gain),
+        outputs((length, F32)) + [(sums_shape, F32, *fixed(sums_shape))] + outputs((modes, F32), (modes, F32)),
         [pltpu.VMEM((modes, LANES), F32)], unit,
     )
     peers = lax.ppermute(sums, "chan", [(0, 1), (1, 0)])
@@ -370,20 +369,24 @@
         outputs((length, BF16), (length, BF16), (length, F32), (1, F32), (modes, F32)),
         [pltpu.VMEM((length, LANES), F32)] * 2, unit,
     )
-    later = exchange(gw.astype(BF16), count, False)
+    later = exchange(gw.astype(BF16), count)
     rows = 2 * modes + 16
+    grads_shape = (groups, rows, LANES)
+    grads_spec = ((width // LANES, rows, LANES), lambda i: (i, 0, 0))
     vg_local, grads = call(
-        functools.partial(backward_kernel, count - 1, float(length)), grid,
-        inputs(*pieces, *slopes, lam, res, gate, vs, ks, carried, gw, gain_part) + basis,
-        outputs((length, F32))
-        + [((groups, rows, LANES), BF16, (width // LANES, rows, LANES), lambda i: (i, 0, 0))],
+        backward_kernel, grid,
+        inputs(lam, res, gate, vs, ks, carried, moved, gw, gain_part) + basis,
+        outputs((length, F32)) + [(grads_shape, F32, *grads_spec)],
         [pltpu.VMEM((length, width), F32)], 16 * length * length * channels,
     )
+    adj, grads = call(
+        functools.partial(adjoint_kernel, float(length)), grid,
+        stacked(later) + inputs(lam, res, slope) + [(grads, *grads_spec)],
+        outputs((modes, F32)) + [(grads_shape, BF16, *grads_spec)], [], channels * modes * 40,
+    )
     grad_k, grad_v = call(
-        functools.partial(finish_kernel, count - 1, float(length)), grid,
-        inputs(*later, lam, res, vg_local, k, v),
-        outputs((length, BF16), (length, BF16)),
-        [pltpu.VMEM((modes, LANES), F32)], unit,
+        finish_kernel, grid, inputs(adj, lam, vg_local, k, v),
+        outputs((length, BF16), (length, BF16)), [], unit,
     )
     both = ("ctx", "dp")
     if count * lax.axis_size("dp") == groups:

time: 130 us -> 117 us (0.900)
  starting transfers between devices: 41.2 us -> 16.8 us
  local copies, waits for them, and re-layouts: 9.43 us -> 30.4 us
  waiting for transfers between devices: 14 us -> 3.71 us
  blocking collectives: 14 us -> 15.3 us
    ppermute x21 -> x0, starting transfers between devices: 37.6 us -> none  [exchange(): pieces.append(lax.ppermute(x, 'ctx', pairs))]
    unnamed x30 -> x60, local copies, waits for them, and re-layouts: 7.41 us -> 26.6 us
    ppermute x21 -> x0, waiting for transfers between devices: 14 us -> none  [exchange(): pieces.append(lax.ppermute(x, 'ctx', pairs))]
    all_to_all x0 -> x2, starting transfers between devices: none -> 13.3 us  [exchange(): lax.all_to_all(jnp.broadcast_to(x[None], (count,) + x.shape), 'ctx', 0, 0)]
    all_to_all x1, waiting for transfers between devices: 0.01 us -> 2.17 us  [shards(): lax.all_to_all(jnp.broadcast_to(mine[None], grads.shape), both, 0, 0)]
    broadcast_in_dim x0 -> x2, local copies, waits for them, and re-layouts: none -> 1.75 us  [exchange(): jnp.broadcast_to(x[None], (count,) + x.shape)]
    ppermute x1, waiting for transfers between devices: 0.01 us -> 1.53 us  [shards(): peers = lax.ppermute(sums, 'chan', [(0, 1), (1, 0)])]
    pallas_call x6 -> x7, Pallas kernels: 48.5 us -> 48.4 us  [call(): pl.pallas_call(kernel, grid=(grid,), in_specs=[pl.BlockSpec(b, m) for _,...]
  transfers between devices with their start and end apart: 23 -> 4, of which waited for: 5 -> 2; matrix products, arithmetic and copies ran while one was open for 0% -> 0% of each run, Pallas kernels for 17% -> 29%
where the time goes in v2:
time: 117 us
  Pallas kernels  48.4 us (41%)
  local copies, waits for them, and re-layouts  30.4 us (26%)
  starting transfers between devices  16.8 us (14%)
  blocking collectives  15.3 us (13%)
  waiting for transfers between devices  3.71 us (3%)
    pallas_call x7, Pallas kernels, call(): pl.pallas_call(kernel, grid=(grid,), in_specs=[pl.BlockSpec(b, m) for _,...  48.4 us
    unnamed x60, local copies, waits for them, and re-layouts  26.6 us
    all_to_all x1, blocking collectives, shards(): parts = lax.all_to_all(grads, both, 0, 0)  15.3 us
    all_to_all x2, starting transfers between devices, exchange(): lax.all_to_all(jnp.broadcast_to(x[None], (count,) + x.shape), 'ctx', 0, 0)  13.3 us
    all_to_all x1, starting transfers between devices, shards(): lax.all_to_all(jnp.broadcast_to(mine[None], grads.shape), both, 0, 0)  3.52 us
  transfers between devices with their start and end apart: 4, of which 2 were waited for; matrix products, arithmetic and copies ran while one was open for 0% of the time, Pallas kernels for 29%

profile of v2, /device:TPU:0, one launch (start us, length us, event | category | flops | bytes accessed | tf_op | source)
XLA Modules:
  0.0 116.5 jit_solution(9594546082468627358)
XLA Ops:
  0.6 0.0 copy-start.15
  0.6 0.0 copy-start.17
  0.7 1.0 multiply_bitcast_fusion.lam_ref
  1.7 4.7 %shard_map.162 = (bf16[256,2048]{1,0:T(8,128)(2,1)S(1)}, bf16[16,2048]{1,0:T(8,128)(2,1)S(1)}) custom-call(bf16[256,2048]{1,0:T(8,128)(2,1)} %bitcast.23, bf16[256,2048]{1,0:T(8,128)(2,1)} %bitcast.25, f32[16,2048]{1,0:T(8,128)S(1)} %multiply_bitcast_fusion.lam_ref), custom_call_target="tpu_custom_call" | custom-call | flops 16777216 | bytes 3342336 | tf_op jit(solution)/shard_map/pallas_call | solution.py:295
  6.4 0.0 copy-start.28
  6.4 0.9 broadcast_in_dim.16
  7.3 7.3 %all-to-all-start = ((bf16[8,16,2048]{2,1,0:T(8,128)(2,1)}), bf16[8,16,2048]{2,1,0:T(8,128)(2,1)S(1)}, u32[]{:S(2)}, u32[]{:S(2)}) async-start(bf16[8,16,2048]{2,1,0:T(8,128)(2,1)} %broadcast_in_dim.16), calls=%async_computation | async-start | bytes 1048576 | tf_op jit(solution)/shard_map/all_to_all | solution.py:310
  14.6 0.0 copy-start.19
  14.6 0.9 copy-done.19
  15.5 0.9 copy-done.21
  16.5 1.2 %copy-done.29 = bf16[256,2048]{1,0:T(8,128)(2,1)S(1)} copy-done((bf16[256,2048]{1,0:T(8,128)(2,1)S(1)}, bf16[256,2048]{1,0:T(8,128)(2,1)}, u32[]{:S(2)}) %copy-start.29) | copy-done | bytes 1048600
  17.7 12.2 %shard_map.163 = (f32[256,2048]{1,0:T(8,128)S(1)}, f32[512,2048]{1,0:T(8,128)S(1)}, f32[512,2048]{1,0:T(8,128)S(1)}, f32[16,2048]{1,0:T(8,128)S(1)}) custom-call(bf16[256,2048]{1,0:T(8,128)(2,1)S(1)} %copy-done.29, f32[16,2048]{1,0:T(8,128)S(1)} %multiply_bitcast_fusion.lam_ref, f32[16,2048]{1,0:T(8,128)S(1)} %bitcast.27, bf16[512,256]{1,0:T(8,128)(2,1)S(1)} %copy-done.21, ...), custom_call_target="tpu_custom_call" | custom-call | flops 2147483648 | bytes 12976128 | tf_op jit(solution)/shard_map/pallas_call | solution.py:295
  29.9 2.0 %copy-done.4 = f32[512,2048]{1,0:T(8,128)} copy-done((f32[512,2048]{1,0:T(8,128)}, f32[512,2048]{1,0:T(8,128)S(1)}, u32[]{:S(2)}) %copy-start.4) | copy-done | bytes 4194328
  31.9 2.0 %copy-done.6 = f32[512,2048]{1,0:T(8,128)} copy-done((f32[512,2048]{1,0:T(8,128)}, f32[512,2048]{1,0:T(8,128)S(1)}, u32[]{:S(2)}) %copy-start.6) | copy-done | bytes 4194328
  33.9 1.4 %copy-done.8 = f32[256,2048]{1,0:T(8,128)} copy-done((f32[256,2048]{1,0:T(8,128)}, f32[256,2048]{1,0:T(8,128)S(1)}, u32[]{:S(2)}) %copy-start.8) | copy-done | bytes 2097176
  35.3 0.0 all-to-all-done.pieces_ref
  35.3 0.0 copy-done
  35.3 1.6 %copy-done.9 = f32[256,2048]{1,0:T(8,128)S(1)} copy-done((f32[256,2048]{1,0:T(8,128)S(1)}, f32[256,2048]{1,0:T(8,128)}, u32[]{:S(2)}) %copy-start.9) | copy-done | bytes 2097176
  36.9 4.3 %shard_map.164 = (f32[256,2048]{1,0:T(8,128)S(1)}, f32[2,256,128]{2,1,0:T(8,128)S(1)}, f32[16,2048]{1,0:T(8,128)S(1)}, f32[16,2048]{1,0:T(8,128)S(1)}) custom-call(bf16[8,16,2048]{2,1,0:T(8,128)(2,1)S(1)} %all-to-all-done.pieces_ref, f32[16,2048]{1,0:T(8,128)S(1)} %multiply_bitcast_fusion.lam_ref, f32[16,2048]{1,0:T(8,128)S(1)} %bitcast.28, ...), custom_call_target="tpu_custom_call" | custom-call | flops 16777216 | bytes 7610368 | tf_op jit(solution)/shard_map/pallas_call | solution.py:295
  41.2 0.0 copy-start.23
  41.2 0.6 copy-done.23
  41.8 0.0 collective-permute-start
  41.9 1.5 %collective-permute-done.peer_ref = f32[2,256,128]{2,1,0:T(8,128)S(1)} collective-permute-done((f32[2,256,128]{2,1,0:T(8,128)S(1)}, f32[2,256,128]{2,1,0:T(8,128)S(1)}, u32[]{:S(2)}, u32[]{:S(2)}) %collective-permute-start) | collective-permute-done | bytes 262176 | tf_op jit(solution)/shard_map/ppermute | solution.py:365
  43.4 5.4 %shard_map.165 = (bf16[256,2048]{1,0:T(8,128)(2,1)}, bf16[256,2048]{1,0:T(8,128)(2,1)}, f32[256,2048]{1,0:T(8,128)S(1)}, f32[1,2048]{1,0:T(1,128)S(1)}, f32[16,2048]{1,0:T(8,128)S(1)}) custom-call(f32[2,256,128]{2,1,0:T(8,128)S(1)} %get-tuple-element.31.sums_ref, f32[2,256,128]{2,1,0:T(8,128)S(1)} %collective-permute-done.peer_ref, ...), custom_call_target="tpu_custom_call" | custom-call | flops 16777216 | bytes 9191424 | tf_op jit(solution)/shard_map/pallas_call | solution.py:295
  48.8 1.4 %copy-done.12 = f32[256,2048]{1,0:T(8,128)} copy-done((f32[256,2048]{1,0:T(8,128)}, f32[256,2048]{1,0:T(8,128)S(1)}, u32[]{:S(2)}) %copy-start.12) | copy-done | bytes 2097176
  50.1 0.8 broadcast_in_dim.37
  51.0 6.0 %all-to-all-start.1 = ((bf16[8,16,2048]{2,1,0:T(8,128)(2,1)}), bf16[8,16,2048]{2,1,0:T(8,128)(2,1)S(1)}, u32[]{:S(2)}, u32[]{:S(2)}) async-start(bf16[8,16,2048]{2,1,0:T(8,128)(2,1)} %broadcast_in_dim.37), calls=%async_computation.1 | async-start | bytes 1048576 | tf_op jit(solution)/shard_map/all_to_all | solution.py:310
  57.0 2.2 %copy-done.5 = f32[512,2048]{1,0:T(8,128)S(1)} copy-done((f32[512,2048]{1,0:T(8,128)S(1)}, f32[512,2048]{1,0:T(8,128)}, u32[]{:S(2)}) %copy-start.5) | copy-done | bytes 4194328
  59.2 2.2 %copy-done.7 = f32[512,2048]{1,0:T(8,128)S(1)} copy-done((f32[512,2048]{1,0:T(8,128)S(1)}, f32[512,2048]{1,0:T(8,128)}, u32[]{:S(2)}) %copy-start.7) | copy-done | bytes 4194328
  61.4 1.6 %copy-done.13 = f32[256,2048]{1,0:T(8,128)S(1)} copy-done((f32[256,2048]{1,0:T(8,128)S(1)}, f32[256,2048]{1,0:T(8,128)}, u32[]{:S(2)}) %copy-start.13) | copy-done | bytes 2097176
  63.0 0.9 copy-done.16
  63.9 0.9 copy-done.18
  64.9 0.9 copy-done.20
  65.8 0.9 copy-done.22
  66.8 0.9 copy-done.24
  67.7 0.9 copy-done.26
  68.6 16.8 %shard_map.166 = (f32[256,2048]{1,0:T(8,128)S(1)}, f32[16,48,128]{2,1,0:T(8,128)S(1)}) custom-call(f32[16,2048]{1,0:T(8,128)S(1)} %multiply_bitcast_fusion.lam_ref, f32[16,2048]{1,0:T(8,128)S(1)} %bitcast.29, f32[256,2048]{1,0:T(8,128)S(1)} %copy-done.13, f32[512,2048]{1,0:T(8,128)S(1)} %copy-done.5, f32[512,2048]{1,0:T(8,128)S(1)} %copy-done.7, ...), custom_call_target="tpu_custom_call" | custom-call | flops 2147483648 | bytes 14688256 | tf_op jit(solution)/shard_map/pallas_call | solution.py:295
  85.4 1.4 %copy-done.10 = f32[256,2048]{1,0:T(8,128)} copy-done((f32[256,2048]{1,0:T(8,128)}, f32[256,2048]{1,0:T(8,128)S(1)}, u32[]{:S(2)}) %copy-start.10) | copy-done | bytes 2097176
  86.7 0.0 all-to-all-done.1.pieces_ref
  86.7 0.8 shard_map.167
  87.6 15.3 %all_to_all.20 = bf16[16,48,128]{2,1,0:T(8,128)(2,1)S(1)} all-to-all(bf16[16,48,128]{2,1,0:T(8,128)(2,1)S(1)} %get-tuple-element.48), channel_id=1, replica_groups=mesh['ctx'=8,'chan'=2,'dp'=2] {'ctx','dp'}, dimensions={0} | all-to-all | bytes 393216 | tf_op jit(solution)/shard_map/all_to_all | solution.py:393
  102.9 0.7 broadcast_in_dim.40
  103.6 3.5 %all-to-all-start.3 = ((bf16[16,48,128]{2,1,0:T(8,128)(2,1)}), bf16[16,48,128]{2,1,0:T(8,128)(2,1)S(1)}, u32[]{:S(2)}, u32[]{:S(2)}) async-start(bf16[16,48,128]{2,1,0:T(8,128)(2,1)} %broadcast_in_dim.40), calls=%async_computation.3 | async-start | bytes 393216 | tf_op jit(solution)/shard_map/all_to_all | solution.py:395
  107.2 1.6 %copy-done.11 = f32[256,2048]{1,0:T(8,128)S(1)} copy-done((f32[256,2048]{1,0:T(8,128)S(1)}, f32[256,2048]{1,0:T(8,128)}, u32[]{:S(2)}) %copy-start.11) | copy-done | bytes 2097176
  108.8 4.2 %shard_map.168 = (bf16[256,2048]{1,0:T(8,128)(2,1)}, bf16[256,2048]{1,0:T(8,128)(2,1)}) custom-call(f32[16,2048]{1,0:T(8,128)S(1)} %get-tuple-element.44.adj_ref, f32[16,2048]{1,0:T(8,128)S(1)} %multiply_bitcast_fusion.lam_ref, f32[256,2048]{1,0:T(8,128)S(1)} %copy-done.11, bf16[256,2048]{1,0:T(8,128)(2,1)S(1)} %bitcast.24, bf16[256,2048]{1,0:T(8,128)(2,1)S(1)} %bitcast.26), custom_call_target="tpu_custom_call" | custom-call | flops 16777216 | bytes 6553600 | tf_op jit(solution)/shard_map/pallas_call | solution.py:295
  113.0 2.2 %all-to-all-done.3 = bf16[16,48,128]{2,1,0:T(8,128)(2,1)S(1)} async-done(((bf16[16,48,128]{2,1,0:T(8,128)(2,1)}), bf16[16,48,128]{2,1,0:T(8,128)(2,1)S(1)}, u32[]{:S(2)}, u32[]{:S(2)}) %all-to-all-start.3) | async-done | bytes 196640 | tf_op jit(solution)/shard_map/all_to_all | solution.py:395
  115.2 0.6 slice.14
  115.8 0.7 fusion
  (37 shorter events, 0.1 us)
Async XLA Ops:
  0.6 13.9 %copy-start.15 = (bf16[256,512]{1,0:T(8,128)(2,1)S(1)}, bf16[256,512]{1,0:T(8,128)(2,1)}, u32[]{:S(2)}) copy-start(bf16[256,512]{1,0:T(8,128)(2,1)} %constant.17.clone.tl_ref) | copy-start | bytes 786436
  0.6 13.9 %copy-start.17 = (bf16[256,512]{1,0:T(8,128)(2,1)S(1)}, bf16[256,512]{1,0:T(8,128)(2,1)}, u32[]{:S(2)}) copy-start(bf16[256,512]{1,0:T(8,128)(2,1)} %constant.16.clone.th_ref) | copy-start | bytes 786436
  0.7 13.9 %copy-start.14 = (f32[2048,16]{0,1:T(8,128)S(1)}, f32[2048,16]{0,1:T(8,128)}, u32[]{:S(2)}) copy-start(f32[2048,16]{0,1:T(8,128)} %param.16) | copy-start | bytes 393220
  6.4 8.2 %copy-start.28 = (bf16[256,2048]{1,0:T(8,128)(2,1)}, bf16[256,2048]{1,0:T(8,128)(2,1)S(1)}, u32[]{:S(2)}) copy-start(bf16[256,2048]{1,0:T(8,128)(2,1)S(1)} %get-tuple-element.29.val_ref) | copy-start | bytes 3145732
  7.3 28.0 %all-to-all-start = ((bf16[8,16,2048]{2,1,0:T(8,128)(2,1)}), bf16[8,16,2048]{2,1,0:T(8,128)(2,1)S(1)}, u32[]{:S(2)}, u32[]{:S(2)}) async-start(bf16[8,16,2048]{2,1,0:T(8,128)(2,1)} %broadcast_in_dim.16), calls=%async_computation | async-start | bytes 1048576 | tf_op jit(solution)/shard_map/all_to_all | solution.py:310
  14.6 1.0 copy-start.19
  15.5 0.9 copy-start.21
  16.5 1.2 %copy-start.29 = (bf16[256,2048]{1,0:T(8,128)(2,1)S(1)}, bf16[256,2048]{1,0:T(8,128)(2,1)}, u32[]{:S(2)}) copy-start(bf16[256,2048]{1,0:T(8,128)(2,1)} %copy-done.28) | copy-start | bytes 3145732
  17.7 17.6 %copy-start = (bf16[1,256,2048]{2,1,0:T(8,128)(2,1)S(1)}, bf16[1,256,2048]{2,1,0:T(8,128)(2,1)}, u32[]{:S(2)}) copy-start(bf16[1,256,2048]{2,1,0:T(8,128)(2,1)} %param.11) | copy-start | bytes 3145732
  17.7 17.6 %copy-start.1 = (bf16[1,256,2048]{2,1,0:T(8,128)(2,1)S(1)}, bf16[1,256,2048]{2,1,0:T(8,128)(2,1)}, u32[]{:S(2)}) copy-start(bf16[1,256,2048]{2,1,0:T(8,128)(2,1)} %param.14) | copy-start | bytes 3145732
  17.7 17.6 %copy-start.27 = (f32[2048]{0:T(1024)S(1)}, f32[2048]{0:T(1024)}, u32[]{:S(2)}) copy-start(f32[2048]{0:T(1024)} %param.15) | copy-start | bytes 24580
  29.9 2.0 %copy-start.4 = (f32[512,2048]{1,0:T(8,128)}, f32[512,2048]{1,0:T(8,128)S(1)}, u32[]{:S(2)}) copy-start(f32[512,2048]{1,0:T(8,128)S(1)} %get-tuple-element.38.vs_ref) | copy-start | bytes 12582916
  31.9 2.0 %copy-start.6 = (f32[512,2048]{1,0:T(8,128)}, f32[512,2048]{1,0:T(8,128)S(1)}, u32[]{:S(2)}) copy-start(f32[512,2048]{1,0:T(8,128)S(1)} %get-tuple-element.39.ks_ref) | copy-start | bytes 12582916
  33.9 1.4 %copy-start.8 = (f32[256,2048]{1,0:T(8,128)}, f32[256,2048]{1,0:T(8,128)S(1)}, u32[]{:S(2)}) copy-start(f32[256,2048]{1,0:T(8,128)S(1)} %get-tuple-element.30.conv_in_ref) | copy-start | bytes 6291460
  35.3 1.6 %copy-start.9 = (f32[256,2048]{1,0:T(8,128)S(1)}, f32[256,2048]{1,0:T(8,128)}, u32[]{:S(2)}) copy-start(f32[256,2048]{1,0:T(8,128)} %copy-done.8) | copy-start | bytes 6291460
  41.2 0.7 copy-start.23
  41.8 6.9 %copy-start.25 = (f32[16,2048]{1,0:T(8,128)}, f32[16,2048]{1,0:T(8,128)S(1)}, u32[]{:S(2)}) copy-start(f32[16,2048]{1,0:T(8,128)S(1)} %get-tuple-element.41.moved_ref) | copy-start | bytes 393220
  41.8 1.5 %collective-permute-start = (f32[2,256,128]{2,1,0:T(8,128)S(1)}, f32[2,256,128]{2,1,0:T(8,128)S(1)}, u32[]{:S(2)}, u32[]{:S(2)}) collective-permute-start(f32[2,256,128]{2,1,0:T(8,128)S(1)} %get-tuple-element.31.sums_ref), channel_id=1, source_target_pairs={{0,2},{2,0},{1,3},{3,1},{4,6},{6,4},{5,7},{7,5},{8,10},{10,8},{9,1... | collective-permute-start | bytes 786440 | tf_op jit(solution)/shard_map/ppermute | solution.py:365
  48.8 1.4 %copy-start.12 = (f32[256,2048]{1,0:T(8,128)}, f32[256,2048]{1,0:T(8,128)S(1)}, u32[]{:S(2)}) copy-start(f32[256,2048]{1,0:T(8,128)S(1)} %get-tuple-element.37.gate_ref) | copy-start | bytes 6291460
  51.0 35.7 %all-to-all-start.1 = ((bf16[8,16,2048]{2,1,0:T(8,128)(2,1)}), bf16[8,16,2048]{2,1,0:T(8,128)(2,1)S(1)}, u32[]{:S(2)}, u32[]{:S(2)}) async-start(bf16[8,16,2048]{2,1,0:T(8,128)(2,1)} %broadcast_in_dim.37), calls=%async_computation.1 | async-start | bytes 1048576 | tf_op jit(solution)/shard_map/all_to_all | solution.py:310
  57.0 2.2 %copy-start.5 = (f32[512,2048]{1,0:T(8,128)S(1)}, f32[512,2048]{1,0:T(8,128)}, u32[]{:S(2)}) copy-start(f32[512,2048]{1,0:T(8,128)} %copy-done.4) | copy-start | bytes 12582916
  59.2 2.2 %copy-start.7 = (f32[512,2048]{1,0:T(8,128)S(1)}, f32[512,2048]{1,0:T(8,128)}, u32[]{:S(2)}) copy-start(f32[512,2048]{1,0:T(8,128)} %copy-done.6) | copy-start | bytes 12582916
  61.4 1.6 %copy-start.13 = (f32[256,2048]{1,0:T(8,128)S(1)}, f32[256,2048]{1,0:T(8,128)}, u32[]{:S(2)}) copy-start(f32[256,2048]{1,0:T(8,128)} %copy-done.12) | copy-start | bytes 6291460
  63.0 0.9 copy-start.16
  63.9 0.9 copy-start.18
  64.9 0.9 copy-start.20
  65.8 0.9 copy-start.22
  66.8 0.9 copy-start.24
  67.7 0.9 copy-start.26
  85.4 1.4 %copy-start.10 = (f32[256,2048]{1,0:T(8,128)}, f32[256,2048]{1,0:T(8,128)S(1)}, u32[]{:S(2)}) copy-start(f32[256,2048]{1,0:T(8,128)S(1)} %get-tuple-element.45.vg_ref) | copy-start | bytes 6291460
  86.7 20.4 %copy-start.2 = (bf16[1,256,2048]{2,1,0:T(8,128)(2,1)S(1)}, bf16[1,256,2048]{2,1,0:T(8,128)(2,1)}, u32[]{:S(2)}) copy-start(bf16[1,256,2048]{2,1,0:T(8,128)(2,1)} %param.12) | copy-start | bytes 3145732
  86.7 20.4 %copy-start.3 = (bf16[1,256,2048]{2,1,0:T(8,128)(2,1)S(1)}, bf16[1,256,2048]{2,1,0:T(8,128)(2,1)}, u32[]{:S(2)}) copy-start(bf16[1,256,2048]{2,1,0:T(8,128)(2,1)} %param.13) | copy-start | bytes 3145732
  103.6 11.6 %all-to-all-start.3 = ((bf16[16,48,128]{2,1,0:T(8,128)(2,1)}), bf16[16,48,128]{2,1,0:T(8,128)(2,1)S(1)}, u32[]{:S(2)}, u32[]{:S(2)}) async-start(bf16[16,48,128]{2,1,0:T(8,128)(2,1)} %broadcast_in_dim.40), calls=%async_computation.3 | async-start | bytes 393216 | tf_op jit(solution)/shard_map/all_to_all | solution.py:395
  107.2 1.6 %copy-start.11 = (f32[256,2048]{1,0:T(8,128)S(1)}, f32[256,2048]{1,0:T(8,128)}, u32[]{:S(2)}) copy-start(f32[256,2048]{1,0:T(8,128)} %copy-done.10) | copy-start | bytes 6291460

commit v3 on v2

--- a/solution.py
+++ b/solution.py
@@ -93,7 +93,9 @@
             acc = acc * step + vals[None, :ROWS]
             acc = acc * step + vals[None, ROWS:]
         weight = jnp.exp(-lam * (ROWS - 1 - sublane()))
-        s_ref[:, cols] = jnp.sum(acc * weight, axis=1).astype(s_ref.dtype)
+        state = jnp.sum(acc * weight, axis=1).astype(BF16)
+        for dest in range(s_ref.shape[0]):
+            s_ref[dest, :, cols] = state
         return 0
 
     lax.fori_loop(0, width // LANES, body, 0)
@@ -167,7 +169,7 @@
 
 
 def gate_kernel(model_width, sums_ref, peer_ref, lam_ref, conv_ref, q_ref, og_ref, gain_ref,
-                y_ref, gq_ref, gate_ref, gain_part_ref, gw_ref, inv_ref, coef_ref):
+                y_ref, gq_ref, gate_ref, gain_part_ref, gw_ref, send_ref, inv_ref, coef_ref):
     length, width = q_ref.shape
 
     @pl.when(pl.program_id(0) == 0)
@@ -204,23 +206,24 @@
             acc = acc * step + gate[None, :ROWS]
         gain_part_ref[:, cols] = jnp.sum(gain_acc, axis=0, keepdims=True)
         weight = jnp.exp(-lam * (sublane() + 1.0))
-        gw_ref[:, cols] = jnp.sum(acc * weight, axis=1)
-        return 0
-
-    lax.fori_loop(0, width // LANES, body, 0)
-
-
-def backward_kernel(lam_ref, res_ref, gate_ref, vs_ref, ks_ref, state_ref, moved_ref, gw_ref, gain_part_ref,
-                    fh_ref, fl_ref, th_ref, tl_ref, vg_ref, grads_ref, kg):
+        gw = jnp.sum(acc * weight, axis=1)
+        gw_ref[:, cols] = gw
+        for dest in range(send_ref.shape[0]):
+            send_ref[dest, :, cols] = gw.astype(BF16)
+        return 0
+
+    lax.fori_loop(0, width // LANES, body, 0)
+
+
+def backward_kernel(lam_ref, gate_ref, vs_ref, state_ref, moved_ref, gw_ref, gain_part_ref,
+                    fh_ref, fl_ref, th_ref, tl_ref, gs_ref, grads_ref, kg):
     length, width = gate_ref.shape
     gs = dot3(fh_ref[...], fl_ref[...], gate_ref[...])
+    gs_ref[...] = gs
     gr, gi = gs[:length], gs[length:]
     vr, vi = vs_ref[:length], vs_ref[length:]
     prod = jnp.concatenate([gr * vr + gi * vi, gi * vr - gr * vi], axis=0) * (1.0 / length)
     kg[...] = dot3(th_ref[...], tl_ref[...], prod)
-    kr, ki = ks_ref[:length], ks_ref[length:]
-    prod = jnp.concatenate([gr * kr + gi * ki, gi * kr - gr * ki], axis=0) * (1.0 / length)
-    vg_ref[...] = dot3(th_ref[...], tl_ref[...], prod)
 
     def body(i, _):
         cols = group(i)
@@ -269,8 +272,12 @@
     lax.fori_loop(0, width // LANES, body, 0)
 
 
-def finish_kernel(adj_ref, lam_ref, vg_ref, k_ref, v_ref, gk_ref, gv_ref):
+def finish_kernel(adj_ref, lam_ref, gs_ref, ks_ref, k_ref, v_ref, th_ref, tl_ref, gk_ref, gv_ref, vg_ref):
     length, width = k_ref.shape
+    gr, gi = gs_ref[:length], gs_ref[length:]
+    kr, ki = ks_ref[:length], ks_ref[length:]
+    prod = jnp.concatenate([gr * kr + gi * ki, gi * kr - gr * ki], axis=0) * (1.0 / length)
+    vg_ref[...] = dot3(th_ref[...], tl_ref[...], prod)
 
     def body(i, _):
         cols = group(i)
@@ -290,24 +297,21 @@
 
 
 def call(kernel, grid, ins, outs, scratch, flops):
-    moved = sum(a.size * a.dtype.itemsize for a, _, _ in ins)
+    arrays = [e[0] if e[3:] else pltpu.with_memory_space_constraint(e[0], pltpu.HBM) for e in ins]
+    moved = sum(a.size * a.dtype.itemsize for a in arrays)
     moved += sum(int(np.prod(s)) * jnp.dtype(d).itemsize for s, d, _, _ in outs)
     return pl.pallas_call(
         kernel,
         grid=(grid,),
-        in_specs=[pl.BlockSpec(b, m) for _, b, m in ins],
+        in_specs=[pl.BlockSpec(e[1], e[2]) for e in ins],
         out_specs=[pl.BlockSpec(b, m) for _, _, b, m in outs],
-        out_shape=[jax.ShapeDtypeStruct(s, d) for s, d, _, _ in outs],
+        out_shape=[pltpu.HBM(s, d) for s, d, _, _ in outs],
         scratch_shapes=scratch,
         compiler_params=pltpu.CompilerParams(
             dimension_semantics=("arbitrary",), vmem_limit_bytes=VMEM_LIMIT
         ),
         cost_estimate=pl.CostEstimate(flops=flops, bytes_accessed=moved, transcendentals=0),
-    )(*[a for a, _, _ in ins])
-
-
-def exchange(x, count):
-    return lax.all_to_all(jnp.broadcast_to(x[None], (count,) + x.shape), "ctx", 0, 0)
+    )(*arrays)
 
 
 def shards(q_stream, k_stream, v_stream, out_grad, norm_gain, residue, rate):
@@ -343,13 +347,13 @@
     unit = 2 * length * channels * modes
 
     def stacked(array):
-        return [(array, (array.shape[0], array.shape[1], width), lambda i: (0, 0, i))]
-
-    k_far, v_far = (pltpu.with_memory_space_constraint(x, pltpu.HBM) for x in (k, v))
+        return [(array, (array.shape[0], array.shape[1], width), lambda i: (0, 0, i), True)]
+
+    send_out = ((count, modes, channels), BF16, (count, modes, width), lambda i: (0, 0, i))
     vals, state = call(
-        state_kernel, grid, inputs(k_far, v_far, lam), outputs((length, BF16), (modes, BF16)), [], unit
-    )
-    pieces = exchange(state, count)
+        state_kernel, grid, inputs(k, v, lam), outputs((length, BF16)) + [send_out], [], unit
+    )
+    pieces = lax.all_to_all(state, "ctx", 0, 0)
     conv_local, vs, ks, slope = call(
         local_kernel, grid, inputs(vals, lam, res) + basis,
         outputs((length, F32), (2 * length, F32), (2 * length, F32), (modes, F32)),
@@ -363,20 +367,20 @@
         [pltpu.VMEM((modes, LANES), F32)], unit,
     )
     peers = lax.ppermute(sums, "chan", [(0, 1), (1, 0)])
-    y_out, grad_q, gate, gain_part, gw = call(
+    y_out, grad_q, gate, gain_part, gw, send = call(
         functools.partial(gate_kernel, model_width), grid,
-        [(sums, *fixed(sums_shape)), (peers, *fixed(sums_shape))] + inputs(lam, conv, q, og, gain),
-        outputs((length, BF16), (length, BF16), (length, F32), (1, F32), (modes, F32)),
+        [(sums, *fixed(sums_shape)), (peers, *fixed(sums_shape), True)] + inputs(lam, conv, q, og, gain),
+        outputs((length, BF16), (length, BF16), (length, F32), (1, F32), (modes, F32)) + [send_out],
         [pltpu.VMEM((length, LANES), F32)] * 2, unit,
     )
-    later = exchange(gw.astype(BF16), count)
+    later = lax.all_to_all(send, "ctx", 0, 0)
     rows = 2 * modes + 16
     grads_shape = (groups, rows, LANES)
     grads_spec = ((width // LANES, rows, LANES), lambda i: (i, 0, 0))
-    vg_local, grads = call(
+    gs, grads = call(
         backward_kernel, grid,
-        inputs(lam, res, gate, vs, ks, carried, moved, gw, gain_part) + basis,
-        outputs((length, F32)) + [(grads_shape, F32, *grads_spec)],
+        inputs(lam, gate, vs, carried, moved, gw, gain_part) + basis,
+        outputs((2 * length, F32)) + [(grads_shape, F32, *grads_spec)],
         [pltpu.VMEM((length, width), F32)], 16 * length * length * channels,
     )
     adj, grads = call(
@@ -385,8 +389,8 @@
         outputs((modes, F32)) + [(grads_shape, BF16, *grads_spec)], [], channels * modes * 40,
     )
     grad_k, grad_v = call(
-        finish_kernel, grid, inputs(adj, lam, vg_local, k, v),
-        outputs((length, BF16), (length, BF16)), [], unit,
+        finish_kernel, grid, inputs(adj, lam, gs, ks, k, v) + basis[2:],
+        outputs((length, BF16), (length, BF16)), [pltpu.VMEM((length, width), F32)], unit,
     )
     both = ("ctx", "dp")
     if count * lax.axis_size("dp") == groups:

time: 117 us -> 102 us (0.87)
  local copies, waits for them, and re-layouts: 30.4 us -> 2.03 us
  Pallas kernels: 48.4 us -> 62.6 us
    unnamed x60 -> x0, local copies, waits for them, and re-layouts: 26.6 us -> none
    pallas_call x7, Pallas kernels: 48.4 us -> 62.6 us  [call(): pl.pallas_call(kernel, grid=(grid,), in_specs=[pl.BlockSpec(e[1], e[2]) f...]
    all_to_all x1, waiting for transfers between devices: 2.17 us -> 0.01 us  [shards(): lax.all_to_all(jnp.broadcast_to(mine[None], grads.shape), both, 0, 0)]
    broadcast_in_dim x2 -> x0, local copies, waits for them, and re-layouts: 1.75 us -> none  [exchange(): jnp.broadcast_to(x[None], (count,) + x.shape)]
  transfers between devices with their start and end apart: 4 -> 4, of which waited for: 2 -> 2; matrix products, arithmetic and copies ran while one was open for 0% -> 0% of each run, Pallas kernels for 29% -> 39%
where the time goes in v3:
time: 102 us; the launch traced here: 101 us
  Pallas kernels  62.6 us (61%)
  starting transfers between devices  16 us (16%)
  blocking collectives  15.6 us (15%)
  waiting for transfers between devices  2.65 us (3%)
  local copies, waits for them, and re-layouts  2.03 us (2%)
  other arithmetic  1.65 us (2%)
    pallas_call x7, Pallas kernels, call(): pl.pallas_call(kernel, grid=(grid,), in_specs=[pl.BlockSpec(e[1], e[2]) f...  62.6 us
    all_to_all x1, blocking collectives, shards(): parts = lax.all_to_all(grads, both, 0, 0)  15.6 us
    all_to_all x1, starting transfers between devices, shards(): pieces = lax.all_to_all(state, 'ctx', 0, 0)  7.25 us
    all_to_all x1, starting transfers between devices, shards(): later = lax.all_to_all(send, 'ctx', 0, 0)  5.12 us
    all_to_all x1, starting transfers between devices, shards(): lax.all_to_all(jnp.broadcast_to(mine[None], grads.shape), both, 0, 0)  3.52 us
  transfers between devices with their start and end apart: 4, of which 2 were waited for; matrix products, arithmetic and copies ran while one was open for 0% of the time, Pallas kernels for 39%

profile of v3, /device:TPU:0, one launch (start us, length us, event | category | flops | bytes accessed | tf_op | source)
XLA Modules:
  0.0 101.2 jit_solution(16716744341168553383)
XLA Ops:
  0.6 1.6 %multiply_bitcast_fusion.lam_ref = f32[16,2048]{1,0:T(8,128)} fusion(f32[2048,16]{0,1:T(8,128)} %param.17), kind=kLoop, calls=%fused_computation.2 | loop fusion | flops 32768 | bytes 262144 | tf_op jit(solution)/shard_map/transpose | solution.py:327
  2.2 5.5 %shard_map.162 = (bf16[256,2048]{1,0:T(8,128)(2,1)}, bf16[8,16,2048]{2,1,0:T(8,128)(2,1)}) custom-call(bf16[256,2048]{1,0:T(8,128)(2,1)} %bitcast.23, bf16[256,2048]{1,0:T(8,128)(2,1)} %bitcast.25, f32[16,2048]{1,0:T(8,128)} %multiply_bitcast_fusion.lam_ref), custom_call_target="tpu_custom_call" | custom-call | flops 16777216 | bytes 3801088 | tf_op jit(solution)/shard_map/pallas_call | solution.py:303
  7.7 7.3 %all-to-all-start = ((bf16[8,16,2048]{2,1,0:T(8,128)(2,1)}), bf16[8,16,2048]{2,1,0:T(8,128)(2,1)S(1)}, u32[]{:S(2)}, u32[]{:S(2)}) async-start(bf16[8,16,2048]{2,1,0:T(8,128)(2,1)} %get-tuple-element.29), calls=%async_computation | async-start | bytes 1048576 | tf_op jit(solution)/shard_map/all_to_all | solution.py:356
  15.0 13.6 %shard_map.163 = (f32[256,2048]{1,0:T(8,128)}, f32[512,2048]{1,0:T(8,128)}, f32[512,2048]{1,0:T(8,128)}, f32[16,2048]{1,0:T(8,128)}) custom-call(bf16[256,2048]{1,0:T(8,128)(2,1)} %get-tuple-element.30.val_ref, f32[16,2048]{1,0:T(8,128)} %multiply_bitcast_fusion.lam_ref, f32[16,2048]{1,0:T(8,128)} %bitcast.27, bf16[512,256]{1,0:T(8,128)(2,1)} %constant.14.clone.fh_ref, ...), custom_call_target="tpu_custom_call" | custom-call | flops 2147483648 | bytes 12976128 | tf_op jit(solution)/shard_map/pallas_call | solution.py:303
  28.6 0.9 all-to-all-done.pieces_ref
  29.5 6.4 %shard_map.164 = (f32[256,2048]{1,0:T(8,128)}, f32[2,256,128]{2,1,0:T(8,128)}, f32[16,2048]{1,0:T(8,128)}, f32[16,2048]{1,0:T(8,128)}) custom-call(bf16[8,16,2048]{2,1,0:T(8,128)(2,1)S(1)} %all-to-all-done.pieces_ref, f32[16,2048]{1,0:T(8,128)} %multiply_bitcast_fusion.lam_ref, f32[16,2048]{1,0:T(8,128)} %bitcast.28, ...), custom_call_target="tpu_custom_call" | custom-call | flops 16777216 | bytes 7610368 | tf_op jit(solution)/shard_map/pallas_call | solution.py:303
  35.9 0.1 collective-permute-start
  36.0 1.7 %collective-permute-done.peer_ref = f32[2,256,128]{2,1,0:T(8,128)S(1)} collective-permute-done((f32[2,256,128]{2,1,0:T(8,128)}, f32[2,256,128]{2,1,0:T(8,128)S(1)}, u32[]{:S(2)}, u32[]{:S(2)}) %collective-permute-start) | collective-permute-done | bytes 262176 | tf_op jit(solution)/shard_map/ppermute | solution.py:369
  37.7 7.6 %shard_map.165 = (bf16[256,2048]{1,0:T(8,128)(2,1)}, bf16[256,2048]{1,0:T(8,128)(2,1)}, f32[256,2048]{1,0:T(8,128)}, f32[1,2048]{1,0:T(1,128)}, f32[16,2048]{1,0:T(8,128)}, /*index=5*/bf16[8,16,2048]{2,1,0:T(8,128)(2,1)}) custom-call(f32[2,256,128]{2,1,0:T(8,128)} %get-tuple-element.32.sums_ref, f32[2,256,128]{2,1,0:T(8,128)S(1)} %collective-permute-done.peer_ref, ...), custom_call_target="tpu_custom_call" | custom-call | flops 16777216 | bytes 9715712 | tf_op jit(solution)/shard_map/pallas_call | solution.py:303
  45.3 5.1 %all-to-all-start.1 = ((bf16[8,16,2048]{2,1,0:T(8,128)(2,1)}), bf16[8,16,2048]{2,1,0:T(8,128)(2,1)S(1)}, u32[]{:S(2)}, u32[]{:S(2)}) async-start(bf16[8,16,2048]{2,1,0:T(8,128)(2,1)} %get-tuple-element.36), calls=%async_computation.1 | async-start | bytes 1048576 | tf_op jit(solution)/shard_map/all_to_all | solution.py:376
  50.4 16.4 %shard_map.166 = (f32[512,2048]{1,0:T(8,128)}, f32[16,48,128]{2,1,0:T(8,128)}) custom-call(f32[16,2048]{1,0:T(8,128)} %multiply_bitcast_fusion.lam_ref, f32[256,2048]{1,0:T(8,128)} %get-tuple-element.38.gate_ref, f32[512,2048]{1,0:T(8,128)} %get-tuple-element.39.vs_ref, f32[16,2048]{1,0:T(8,128)} %get-tuple-element.40.state_ref, ...), custom_call_target="tpu_custom_call" | custom-call | flops 2147483648 | bytes 12460032 | tf_op jit(solution)/shard_map/pallas_call | solution.py:303
  66.9 0.0 all-to-all-done.1.pieces_ref
  66.9 3.5 %shard_map.167 = (f32[16,2048]{1,0:T(8,128)}, bf16[16,48,128]{2,1,0:T(8,128)(2,1)}) custom-call(bf16[8,16,2048]{2,1,0:T(8,128)(2,1)S(1)} %all-to-all-done.1.pieces_ref, f32[16,2048]{1,0:T(8,128)} %multiply_bitcast_fusion.lam_ref, f32[16,2048]{1,0:T(8,128)} %bitcast.29, f32[16,2048]{1,0:T(8,128)} %get-tuple-element.37.slope_ref, ...), custom_call_target="tpu_custom_call" | custom-call | flops 1310720 | bytes 1638400 | tf_op jit(solution)/shard_map/pallas_call | solution.py:303
  70.4 15.6 %all_to_all.20 = bf16[16,48,128]{2,1,0:T(8,128)(2,1)S(1)} all-to-all(bf16[16,48,128]{2,1,0:T(8,128)(2,1)} %get-tuple-element.50), channel_id=1, replica_groups=mesh['ctx'=8,'chan'=2,'dp'=2] {'ctx','dp'}, dimensions={0} | all-to-all | bytes 393216 | tf_op jit(solution)/shard_map/all_to_all | solution.py:397
  86.0 0.7 broadcast_in_dim.26
  86.7 3.5 %all-to-all-start.3 = ((bf16[16,48,128]{2,1,0:T(8,128)(2,1)}), bf16[16,48,128]{2,1,0:T(8,128)(2,1)S(1)}, u32[]{:S(2)}, u32[]{:S(2)}) async-start(bf16[16,48,128]{2,1,0:T(8,128)(2,1)} %broadcast_in_dim.26), calls=%async_computation.3 | async-start | bytes 393216 | tf_op jit(solution)/shard_map/all_to_all | solution.py:399
  90.3 9.5 %shard_map.168 = (bf16[256,2048]{1,0:T(8,128)(2,1)}, bf16[256,2048]{1,0:T(8,128)(2,1)}) custom-call(f32[16,2048]{1,0:T(8,128)} %get-tuple-element.45.adj_ref, f32[16,2048]{1,0:T(8,128)} %multiply_bitcast_fusion.lam_ref, f32[512,2048]{1,0:T(8,128)} %get-tuple-element.46.gs_ref, f32[512,2048]{1,0:T(8,128)} %get-tuple-element.47.ks_ref, ...), custom_call_target="tpu_custom_call" | custom-call | flops 16777216 | bytes 13369344 | tf_op jit(solution)/shard_map/pallas_call | solution.py:303
  99.8 0.0 all-to-all-done.3
  99.8 0.6 slice.14
  100.4 0.7 fusion
  (2 shorter events, 0.1 us)
Async XLA Ops:
  7.7 21.7 %all-to-all-start = ((bf16[8,16,2048]{2,1,0:T(8,128)(2,1)}), bf16[8,16,2048]{2,1,0:T(8,128)(2,1)S(1)}, u32[]{:S(2)}, u32[]{:S(2)}) async-start(bf16[8,16,2048]{2,1,0:T(8,128)(2,1)} %get-tuple-element.29), calls=%async_computation | async-start | bytes 1048576 | tf_op jit(solution)/shard_map/all_to_all | solution.py:356
  35.9 1.8 %collective-permute-start = (f32[2,256,128]{2,1,0:T(8,128)}, f32[2,256,128]{2,1,0:T(8,128)S(1)}, u32[]{:S(2)}, u32[]{:S(2)}) collective-permute-start(f32[2,256,128]{2,1,0:T(8,128)} %get-tuple-element.32.sums_ref), channel_id=1, source_target_pairs={{0,2},{2,0},{1,3},{3,1},{4,6},{6,4},{5,7},{7,5},{8,10},{10,8},{9,1... | collective-permute-start | bytes 786440 | tf_op jit(solution)/shard_map/ppermute | solution.py:369
  45.3 21.6 %all-to-all-start.1 = ((bf16[8,16,2048]{2,1,0:T(8,128)(2,1)}), bf16[8,16,2048]{2,1,0:T(8,128)(2,1)S(1)}, u32[]{:S(2)}, u32[]{:S(2)}) async-start(bf16[8,16,2048]{2,1,0:T(8,128)(2,1)} %get-tuple-element.36), calls=%async_computation.1 | async-start | bytes 1048576 | tf_op jit(solution)/shard_map/all_to_all | solution.py:376
  86.7 13.1 %all-to-all-start.3 = ((bf16[16,48,128]{2,1,0:T(8,128)(2,1)}), bf16[16,48,128]{2,1,0:T(8,128)(2,1)S(1)}, u32[]{:S(2)}, u32[]{:S(2)}) async-start(bf16[16,48,128]{2,1,0:T(8,128)(2,1)} %broadcast_in_dim.26), calls=%async_computation.3 | async-start | bytes 393216 | tf_op jit(solution)/shard_map/all_to_all | solution.py:399

commit v4 on v3

v4 whole, which is shorter than its diff:
```python
import functools
import math

import jax
import jax.numpy as jnp
import numpy as np
from jax import lax
from jax.experimental import pallas as pl
from jax.experimental.pallas import tpu as pltpu
from jax.sharding import PartitionSpec as P

EPSILON = 1e-06
LANES = 128
ROWS = 8
F32 = jnp.float32
BF16 = jnp.bfloat16
MIB = 1024 * 1024


def fourier(length):
    freq = 2 * np.arange(length)[:, None] + 1
    phase = (freq * np.arange(length)[None, :]) % (4 * length) * (2.0 * np.pi / (4 * length))
    return np.concatenate([np.cos(phase), -np.sin(phase)], axis=0).astype(np.float32)


def terms(full, order):
    high = full.astype(jnp.bfloat16)
    low = (full - high.astype(np.float32)).astype(jnp.bfloat16)
    return jnp.asarray(np.concatenate([{"h": high, "l": low}[o] for o in order], axis=1))


def triple(x):
    high = x.astype(BF16)
    low = (x - high.astype(F32)).astype(BF16)
    return jnp.concatenate([high, low, high], axis=0)


def dot(a, b):
    return jnp.dot(a, b, preferred_element_type=F32)


def spread(ref, cols, first=0, count=16):
    return jnp.stack(
        [jnp.broadcast_to(ref[m : m + 1, cols], (ROWS, LANES)) for m in range(first, first + count)]
    )


def sublane():
    return lax.broadcasted_iota(jnp.int32, (ROWS, LANES), 0)


def fold(x):
    row = sublane()
    out = []
    for m in range(0, x.shape[0], ROWS):
        regs = [x[m + r] for r in range(ROWS)]
        for half in (4, 2, 1):
            low = (row & half) == 0
            regs = [
                jnp.where(
                    low,
                    regs[r] + pltpu.roll(regs[r], ROWS - half, 0),
                    regs[r + half] + pltpu.roll(regs[r + half], half, 0),
                )
                for r in range(half)
            ]
        out.append(regs[0])
    return jnp.concatenate(out, axis=0)


def groups_of(width, body):
    def step(i, _):
        body(i, pl.ds(pl.multiple_of(i * LANES, LANES), LANES))
        return 0

    lax.fori_loop(0, width // LANES, step, 0, unroll=UNROLL)


UNROLL = True


def evaluate(start, step, tiles):
    term = start
    for i in range(tiles):
        yield jnp.sum(term, axis=0)
        if i + 1 < tiles:
            term = term * step


def gather_states(pieces_ref, cols, decay_block, forward):
    rank = lax.axis_index("ctx")
    count = pieces_ref.shape[0]
    total = jnp.zeros_like(decay_block)
    slope = jnp.zeros_like(decay_block)
    for s in range(count) if forward else range(count - 1, -1, -1):
        inside = (s < rank) if forward else (s > rank)
        piece = pieces_ref[s, :, cols].astype(F32)
        if forward:
            slope = jnp.where(inside, decay_block * (slope + total), slope)
        total = jnp.where(inside, decay_block * total + piece, total)
    return total, slope


def state_kernel(seq_len, chunk, k_ref, v_ref, rate_ref, val_ref, lam_ref, parts_ref, send_ref):
    length, width = k_ref.shape

    def body(i, cols):
        lam_rows = jnp.exp(rate_ref[:, cols]) * (1.0 / seq_len)
        lam_ref[:, cols] = lam_rows
        lam = spread(lam_ref, cols)
        step = jnp.exp(-ROWS * lam)
        weight = jnp.exp(-lam * (ROWS - 1 - sublane()).astype(F32))
        decay_chunk = jnp.exp(-float(chunk) * lam_rows)
        total = None
        for c in range(length // chunk):
            acc = None
            for a in range(c * chunk, (c + 1) * chunk, 16):
                rows = slice(a, a + 16)
                vals = (k_ref[rows, cols].astype(F32) * v_ref[rows, cols].astype(F32)).astype(BF16)
                val_ref[rows, cols] = vals
                vals = vals.astype(F32)
                for tile in (vals[:ROWS], vals[ROWS:]):
                    acc = acc * step + tile[None] if acc is not None else jnp.broadcast_to(tile[None], lam.shape)
            part = fold(acc * weight)
            parts_ref[c, :, cols] = part
            total = part if total is None else total * decay_chunk + part
        for dest in range(send_ref.shape[0]):
            send_ref[dest, :, cols] = total.astype(BF16)

    groups_of(width, body)


def local_kernel(chunk, val_ref, lam_ref, res_ref, parts_ref, fv_ref, fa_ref, ta_ref,
                 conv_ref, ks_ref, slopes_ref, slope_ref, ker):
    length, width = val_ref.shape

    def body(i, cols):
        lam = spread(lam_ref, cols)
        step = jnp.exp(-ROWS * lam)
        row = sublane().astype(F32)
        start = spread(res_ref, cols) * jnp.exp(-lam * row)
        for a, tile in enumerate(evaluate(start, step, chunk // ROWS)):
            ker[a * ROWS : (a + 1) * ROWS, cols] = tile
        weight = jnp.exp(-lam * (ROWS - 1 - row))
        decay_chunk = jnp.exp(-float(chunk) * lam_ref[:, cols])
        total = slope = jnp.zeros_like(decay_chunk)
        for c in range(length // chunk):
            acc = None
            for a in range(0, chunk, 16):
                vals = val_ref[c * chunk + a : c * chunk + a + 16, cols].astype(F32)
                for h in (0, ROWS):
                    tile = (vals[h : h + ROWS] * (float(chunk - 1 - a - h) - row))[None]
                    acc = acc * step + tile if acc is not None else jnp.broadcast_to(tile, lam.shape)
            part = fold(acc * weight)
            slopes_ref[c, :, cols] = part
            slope = decay_chunk * (slope + float(chunk) * total) + part
            total = decay_chunk * total + parts_ref[c, :, cols]
        slope_ref[:, cols] = slope

    groups_of(width, body)
    ks = dot(fa_ref[...], triple(ker[...]))
    ks_ref[...] = ks
    kr, ki = ks[:chunk], ks[chunk:]
    for a in range(0, length, chunk):
        vals = val_ref[a : a + chunk]
        vs = dot(fv_ref[...], jnp.concatenate([vals, vals], axis=0))
        vr, vi = vs[:chunk], vs[chunk:]
        prod = jnp.concatenate([vr * kr - vi * ki, vr * ki + vi * kr], axis=0)
        conv_ref[a : a + chunk] = dot(ta_ref[...], triple(prod))


def forward_kernel(chunk, pieces_ref, lam_ref, res_ref, parts_ref, conv_in_ref, q_ref, og_ref, gain_ref,
                   conv_ref, sums_ref, states_ref, moved_ref, held):
    length, width = q_ref.shape

    @pl.when(pl.program_id(0) == 0)
    def _():
        sums_ref[...] = jnp.zeros_like(sums_ref)

    def body(i, cols):
        lam_rows = lam_ref[:, cols]
        modes = lam_rows.shape[0]
        state, moved = gather_states(pieces_ref, cols, jnp.exp(-float(length) * lam_rows), True)
        moved_ref[:, cols] = moved * float(length)
        decay_chunk = jnp.exp(-float(chunk) * lam_rows)
        res = res_ref[:, cols]
        for c in range(length // chunk):
            states_ref[c, :, cols] = state
            held[i, c * modes : (c + 1) * modes] = state * res
            state = decay_chunk * state + parts_ref[c, :, cols]
        lam = spread(lam_ref, cols)
        step = jnp.exp(-ROWS * lam)
        weight = jnp.exp(-lam * (sublane() + 1).astype(F32))
        gain = gain_ref[:, cols]
        for c in range(length // chunk):
            start = spread(held.at[i], slice(None), c * modes, modes) * weight
            tiles = evaluate(start, step, chunk // ROWS)
            for a in range(c * chunk, (c + 1) * chunk, 16):
                rows = slice(a, a + 16)
                conv = conv_in_ref[rows, cols] + jnp.concatenate([next(tiles), next(tiles)], axis=0)
                conv_ref[rows, cols] = conv
                mixed = q_ref[rows, cols].astype(F32) * conv
                scaled = gain * og_ref[rows, cols].astype(F32)
                sums_ref[0, rows] += mixed * mixed
                sums_ref[1, rows] += scaled * mixed

    groups_of(width, body)


def gate_kernel(model_width, chunk, sums_ref, peer_ref, lam_ref, conv_ref, q_ref, og_ref, gain_ref,
                y_ref, gq_ref, gate_ref, gain_part_ref, gw_ref, send_ref, inv_ref, coef_ref):
    length, width = q_ref.shape

    @pl.when(pl.program_id(0) == 0)
    def _():
        squares = jnp.sum(sums_ref[0] + peer_ref[0], axis=1, keepdims=True)
        inner = jnp.sum(sums_ref[1] + peer_ref[1], axis=1, keepdims=True)
        inv = lax.rsqrt(squares / model_width + EPSILON)
        coef = inv * inv * inv * inner / model_width
        inv_ref[...] = jnp.broadcast_to(inv, inv_ref.shape)
        coef_ref[...] = jnp.broadcast_to(coef, coef_ref.shape)

    def body(i, cols):
        lam = spread(lam_ref, cols)
        step = jnp.exp(-ROWS * lam)
        weight = jnp.exp(-lam * (sublane() + 1).astype(F32))
        decay_chunk = jnp.exp(-float(chunk) * lam_ref[:, cols])
        gain = gain_ref[:, cols]
        gain_acc = jnp.zeros((16, LANES), F32)
        total = None
        for c in range(length // chunk - 1, -1, -1):
            acc = None
            for a in range((c + 1) * chunk - 16, c * chunk - 1, -16):
                rows = slice(a, a + 16)
                inv = inv_ref[rows]
                q = q_ref[rows, cols].astype(F32)
                og = og_ref[rows, cols].astype(F32)
                conv = conv_ref[rows, cols]
                mixed = q * conv
                normed = mixed * inv
                y_ref[rows, cols] = (gain * normed).astype(BF16)
                gain_acc = gain_acc + og * normed
                mixed_grad = inv * (gain * og) - mixed * coef_ref[rows]
                gq_ref[rows, cols] = (mixed_grad * conv).astype(BF16)
                gate = mixed_grad * q
                gate_ref[rows, cols] = gate
                for tile in (gate[ROWS:], gate[:ROWS]):
                    acc = acc * step + tile[None] if acc is not None else jnp.broadcast_to(tile[None], lam.shape)
            part = fold(acc * weight)
            gw_ref[c, :, cols] = part
            total = part if total is None else total * decay_chunk + part
        gain_part_ref[:, cols] = jnp.sum(gain_acc, axis=0, keepdims=True)
        for dest in range(send_ref.shape[0]):
            send_ref[dest, :, cols] = total.astype(BF16)

    groups_of(width, body)


def backward_kernel(chunk, lam_ref, gate_ref, val_ref, ks_ref, states_ref, moved_ref, slopes_ref, gw_ref,
                    gain_part_ref, fv_ref, fa_ref, ta_ref, vg_ref, grads_ref, kg):
    length, width = gate_ref.shape
    kr, ki = ks_ref[:chunk], ks_ref[chunk:]
    cross_r = cross_i = None
    for a in range(0, length, chunk):
        gs = dot(fa_ref[...], triple(gate_ref[a : a + chunk]))
        gr, gi = gs[:chunk], gs[chunk:]
        vals = val_ref[a : a + chunk]
        vs = dot(fv_ref[...], jnp.concatenate([vals, vals], axis=0))
        vr, vi = vs[:chunk], vs[chunk:]
        real, imag = gr * vr + gi * vi, gi * vr - gr * vi
        cross_r = real if cross_r is None else cross_r + real
        cross_i = imag if cross_i is None else cross_i + imag
        prod = jnp.concatenate([gr * kr + gi * ki, gi * kr - gr * ki], axis=0)
        vg_ref[a : a + chunk] = dot(ta_ref[...], triple(prod))
    kg[...] = dot(ta_ref[...], triple(jnp.concatenate([cross_r, cross_i], axis=0)))

    def body(i, cols):
        lam_rows = lam_ref[:, cols]
        modes = lam_rows.shape[0]
        lam = spread(lam_ref, cols)
        row = sublane().astype(F32)
        step = jnp.exp(-ROWS * lam)
        acc_r = acc_s = jnp.zeros_like(lam)
        for a in range(chunk - ROWS, -1, -ROWS):
            tile = kg[a : a + ROWS, cols]
            acc_r = acc_r * step + tile[None]
            acc_s = acc_s * step + (tile * (row + float(a)))[None]
        weight = jnp.exp(-lam * row)
        total_r = fold(acc_r * weight)
        total_s = fold(acc_s * weight)
        weight = jnp.exp(-lam * (row + 1.0))
        decay_chunk = jnp.exp(-float(chunk) * lam_rows)
        slope = moved_ref[:, cols]
        for c in range(length // chunk):
            acc = None
            for a in range(chunk - ROWS, -1, -ROWS):
                tile = gate_ref[c * chunk + a : c * chunk + a + ROWS, cols] * (row + float(a + 1))
                acc = acc * step + tile[None] if acc is not None else jnp.broadcast_to(tile[None], lam.shape)
            g_one = fold(acc * weight)
            state = states_ref[c, :, cols]
            gw = gw_ref[c, :, cols]
            total_r = total_r + gw * state
            total_s = total_s + g_one * state + gw * slope
            slope = decay_chunk * (slope + float(chunk) * state) + slopes_ref[c, :, cols]
        grads_ref[i, :modes] = total_r
        grads_ref[i, modes : 2 * modes] = total_s
        grads_ref[i, 2 * modes :] = jnp.broadcast_to(gain_part_ref[:, cols], (16, LANES))

    groups_of(width, body)


def adjoint_kernel(length, pieces_ref, lam_ref, res_ref, slope_ref, grads_ref, adj_ref, out_ref):
    modes, width = lam_ref.shape

    def body(i, cols):
        lam = lam_ref[:, cols]
        total, _ = gather_states(pieces_ref, cols, jnp.exp(-length * lam), False)
        adj_ref[:, cols] = total
        out_ref[i, :modes] = grads_ref[i, :modes].astype(BF16)
        total_s = grads_ref[i, modes : 2 * modes] + slope_ref[:, cols] * total
        out_ref[i, modes : 2 * modes] = (-lam * res_ref[:, cols] * total_s).astype(BF16)
        out_ref[i, 2 * modes :] = grads_ref[i, 2 * modes :].astype(BF16)

    groups_of(width, body)


def finish_kernel(chunk, adj_ref, lam_ref, res_ref, gw_ref, vg_ref, k_ref, v_ref, gk_ref, gv_ref, held):
    length, width = k_ref.shape

    def body(i, cols):
        lam_rows = lam_ref[:, cols]
        modes = lam_rows.shape[0]
        decay_chunk = jnp.exp(-float(chunk) * lam_rows)
        adj = adj_ref[:, cols]
        res = res_ref[:, cols]
        for c in range(length // chunk - 1, -1, -1):
            held[i, c * modes : (c + 1) * modes] = adj * res
            adj = decay_chunk * adj + gw_ref[c, :, cols]
        lam = spread(lam_ref, cols)
        step = jnp.exp(-ROWS * lam)
        weight = jnp.exp(-lam * (ROWS - 1 - sublane()).astype(F32))
        for c in range(length // chunk - 1, -1, -1):
            start = spread(held.at[i], slice(None), c * modes, modes) * weight
            tiles = evaluate(start, step, chunk // ROWS)
            for a in range((c + 1) * chunk - 16, c * chunk - 1, -16):
                rows = slice(a, a + 16)
                upper = next(tiles)
                grad = vg_ref[rows, cols] + jnp.concatenate([next(tiles), upper], axis=0)
                gk_ref[rows, cols] = (grad * v_ref[rows, cols].astype(F32)).astype(BF16)
                gv_ref[rows, cols] = (grad * k_ref[rows, cols].astype(F32)).astype(BF16)

    groups_of(width, body)


def call(kernel, grid, ins, outs, scratch, flops, limit=16):
    arrays = [e[0] if e[3:] else pltpu.with_memory_space_constraint(e[0], pltpu.HBM) for e in ins]
    moved = sum(a.size * a.dtype.itemsize for a in arrays)
    moved += sum(int(np.prod(s)) * jnp.dtype(d).itemsize for s, d, _, _ in outs)
    return pl.pallas_call(
        kernel,
        grid=(grid,),
        in_specs=[pl.BlockSpec(e[1], e[2]) for e in ins],
        out_specs=[pl.BlockSpec(b, m) for _, _, b, m in outs],
        out_shape=[pltpu.HBM(s, d) for s, d, _, _ in outs],
        scratch_shapes=scratch,
        compiler_params=pltpu.CompilerParams(
            dimension_semantics=("arbitrary",), vmem_limit_bytes=limit * MIB
        ),
        cost_estimate=pl.CostEstimate(flops=flops, bytes_accessed=moved, transcendentals=0),
    )(*arrays)


def shards(q_stream, k_stream, v_stream, out_grad, norm_gain, residue, rate):
    count = lax.axis_size("ctx")
    _, length, channels = q_stream.shape
    seq_len = length * count
    modes = residue.shape[1]
    model_width = float(channels * lax.axis_size("chan"))
    chunk = math.gcd(length, 64)
    chunks = length // chunk
    groups = channels // LANES
    width = min(channels, 512)
    grid = channels // width
    q, k, v, og = (x[0] for x in (q_stream, k_stream, v_stream, out_grad))
    res = residue.T
    gain = norm_gain[None]
    full = fourier(chunk)
    basis = [terms(full, "hl"), terms(full, "hhl"), terms(full.T / np.float32(chunk), "hhl")]

    def block(shape, last=None):
        lead = tuple(shape[:-1])
        return (*lead, last or width), lambda i: (*(0 for _ in lead), i)

    def inputs(*arrays):
        return [(a, *block(a.shape)) for a in arrays]

    def outputs(*shapes_types):
        return [((*s, channels), d, *block((*s, channels))) for s, d in shapes_types]

    def fixed(shape):
        return shape, lambda i: (0,) * len(shape)

    basis = [(x, *fixed(x.shape)) for x in basis]
    unit = 2 * length * channels * modes
    send = ((count, modes), BF16)
    states = ((chunks, modes), F32)
    held = pltpu.VMEM((width // LANES, chunks * modes, LANES), F32)

    vals, lam, parts, state = call(
        functools.partial(state_kernel, float(seq_len), chunk), grid, inputs(k, v, rate.T),
        outputs(((length,), BF16), ((modes,), F32), states, send), [], unit,
    )
    pieces = lax.all_to_all(state, "ctx", 0, 0)
    conv_local, ks, slopes, slope = call(
        functools.partial(local_kernel, chunk), grid, inputs(vals, lam, res, parts) + basis,
        outputs(((length,), F32), ((2 * chunk,), F32), states, ((modes,), F32)),
        [pltpu.VMEM((chunk, width), F32)], 8 * unit,
    )
    sums_shape = (2, length, LANES)
    conv, sums, carried, moved = call(
        functools.partial(forward_kernel, chunk), grid,
        [(pieces, *block(pieces.shape), True)] + inputs(lam, res, parts, conv_local, q, og, gain),
        outputs(((length,), F32)) + [(sums_shape, F32, *fixed(sums_shape))] + outputs(states, ((modes,), F32)),
        [held], unit,
    )
    peers = lax.ppermute(sums, "chan", [(0, 1), (1, 0)])
    y_out, grad_q, gate, gain_part, gw, state = call(
        functools.partial(gate_kernel, model_width, chunk), grid,
        [(sums, *fixed(sums_shape)), (peers, *fixed(sums_shape), True)] + inputs(lam, conv, q, og, gain),
        outputs(((length,), BF16), ((length,), BF16), ((length,), F32), ((1,), F32), states, send),
        [pltpu.VMEM((length, LANES), F32)] * 2, unit,
    )
    later = lax.all_to_all(state, "ctx", 0, 0)
    rows = 2 * modes + 16
    grads_shape = (groups, rows, LANES)
    vg_local, grads = call(
        functools.partial(backward_kernel, chunk), grid,
        inputs(lam, gate, vals, ks, carried, moved, slopes, gw, gain_part) + basis,
        outputs(((length,), F32))
        + [(grads_shape, F32, (width // LANES, rows, LANES), lambda i: (i, 0, 0))],
        [pltpu.VMEM((chunk, width), F32)], 8 * unit,
    )
    adj, grads = call(
        functools.partial(adjoint_kernel, float(length)), 1,
        [(later, *fixed(later.shape), True)] + [(a, *fixed(a.shape)) for a in (lam, res, slope, grads)],
        [(lam.shape, F32, *fixed(lam.shape)), (grads_shape, BF16, *fixed(grads_shape))], [], channels * modes * 40,
    )
    grad_k, grad_v = call(
        functools.partial(finish_kernel, chunk), grid, inputs(adj, lam, res, gw, vg_local, k, v),
        outputs(((length,), BF16), ((length,), BF16)), [held], unit,
    )
    both = ("ctx", "dp")
    if count * lax.axis_size("dp") == groups:
        parts = lax.all_to_all(grads, both, 0, 0)
        mine = jnp.sum(parts.astype(F32), axis=0).astype(BF16)
        total = lax.all_to_all(jnp.broadcast_to(mine[None], grads.shape), both, 0, 0).astype(F32)
    else:
        total = lax.psum(grads.astype(F32), both)
    total = total.transpose(0, 2, 1).reshape(channels, rows)
    return (
        y_out[None],
        grad_q[None],
        grad_k[None],
        grad_v[None],
        total[:, :modes],
        total[:, modes : 2 * modes],
        total[:, 2 * modes],
    )


def solution(mesh):
    streams = P("dp", "ctx", "chan")
    in_specs = (streams,) * 4 + (P("chan"), P("chan", None), P("chan", None))
    out_specs = (streams,) * 4 + (P("chan", None), P("chan", None), P("chan"))
    return jax.shard_map(shards, mesh=mesh, in_specs=in_specs, out_specs=out_specs, check_vma=False)
```

time: 102 us -> 92.2 us (0.904)
  Pallas kernels: 62.6 us -> 50.4 us
  waiting for transfers between devices: 2.65 us -> 10.1 us
  blocking collectives: 15.6 us -> 13.5 us
  other arithmetic: 1.65 us -> 0.06 us
  starting transfers between devices: 16 us -> 14.5 us
    pallas_call x7, Pallas kernels: 62.6 us -> 50.4 us  [call(): pl.pallas_call(kernel, grid=(grid,), in_specs=[pl.BlockSpec(e[1], e[2]) f...]
    all_to_all x1, waiting for transfers between devices: 0.91 us -> 4.12 us  [shards(): pieces = lax.all_to_all(state, 'ctx', 0, 0)]
    all_to_all x1, waiting for transfers between devices: 0.01 us -> 2.24 us  [shards(): later = lax.all_to_all(state, 'ctx', 0, 0)]
    all_to_all x1, blocking collectives: 15.6 us -> 13.5 us  [shards(): parts = lax.all_to_all(grads, both, 0, 0)]
    all_to_all x1, waiting for transfers between devices: 0.01 us -> 2.02 us  [shards(): lax.all_to_all(jnp.broadcast_to(mine[None], grads.shape), both, 0, 0)]
    transpose x1 -> x0, other arithmetic: 1.58 us -> none  [shards(): lam = (jnp.exp(rate) / seq_len).T]
    all_to_all x1, starting transfers between devices: 5.12 us -> 3.64 us  [shards(): later = lax.all_to_all(state, 'ctx', 0, 0)]
  transfers between devices with their start and end apart: 4 -> 4, of which waited for: 2 -> 4; matrix products, arithmetic and copies ran while one was open for 0% -> 0% of each run, Pallas kernels for 39% -> 32%
where the time goes in v4:
time: 92.2 us; the launch traced here: 91.3 us
  Pallas kernels  50.4 us (55%)
  starting transfers between devices  14.5 us (16%)
  blocking collectives  13.5 us (15%)
  waiting for transfers between devices  10.1 us (11%)
  local copies, waits for them, and re-layouts  2.03 us (2%)
    pallas_call x7, Pallas kernels, call(): pl.pallas_call(kernel, grid=(grid,), in_specs=[pl.BlockSpec(e[1], e[2]) f...  50.4 us
    all_to_all x1, blocking collectives, shards(): parts = lax.all_to_all(grads, both, 0, 0)  13.5 us
    all_to_all x1, starting transfers between devices, shards(): pieces = lax.all_to_all(state, 'ctx', 0, 0)  7.25 us
    all_to_all x1, waiting for transfers between devices, shards(): pieces = lax.all_to_all(state, 'ctx', 0, 0)  4.12 us
    all_to_all x1, starting transfers between devices, shards(): later = lax.all_to_all(state, 'ctx', 0, 0)  3.64 us
    all_to_all x1, starting transfers between devices, shards(): lax.all_to_all(jnp.broadcast_to(mine[None], grads.shape), both, 0, 0)  3.52 us
    all_to_all x1, waiting for transfers between devices, shards(): later = lax.all_to_all(state, 'ctx', 0, 0)  2.24 us
    all_to_all x1, waiting for transfers between devices, shards(): lax.all_to_all(jnp.broadcast_to(mine[None], grads.shape), both, 0, 0)  2.02 us
  transfers between devices with their start and end apart: 4, of which 4 were waited for; matrix products, arithmetic and copies ran while one was open for 0% of the time, Pallas kernels for 32%

profile of v4, /device:TPU:0, one launch (start us, length us, event | category | flops | bytes accessed | tf_op | source)
XLA Modules:
  0.0 91.3 jit_solution(5574275444863900860)
XLA Ops:
  0.6 5.7 %shard_map.153 = (bf16[256,2048]{1,0:T(8,128)(2,1)}, f32[16,2048]{1,0:T(8,128)}, f32[4,16,2048]{2,1,0:T(8,128)}, bf16[8,16,2048]{2,1,0:T(8,128)(2,1)}) custom-call(bf16[256,2048]{1,0:T(8,128)(2,1)} %bitcast.18, bf16[256,2048]{1,0:T(8,128)(2,1)} %bitcast.20, f32[16,2048]{1,0:T(8,128)} %bitcast.30), custom_call_target="tpu_custom_call" | custom-call | flops 16777216 | bytes 4456448 | tf_op jit(solution)/shard_map/pallas_call | solution.py:359
  6.3 7.3 %all-to-all-start = ((bf16[8,16,2048]{2,1,0:T(8,128)(2,1)}), bf16[8,16,2048]{2,1,0:T(8,128)(2,1)S(1)}, u32[]{:S(2)}, u32[]{:S(2)}) async-start(bf16[8,16,2048]{2,1,0:T(8,128)(2,1)} %get-tuple-element.31), calls=%async_computation | async-start | bytes 1048576 | tf_op jit(solution)/shard_map/all_to_all | solution.py:413
  13.6 10.4 %shard_map.154 = (f32[256,2048]{1,0:T(8,128)}, f32[128,2048]{1,0:T(8,128)}, f32[4,16,2048]{2,1,0:T(8,128)}, f32[16,2048]{1,0:T(8,128)}) custom-call(bf16[256,2048]{1,0:T(8,128)(2,1)} %get-tuple-element.34.val_ref, f32[16,2048]{1,0:T(8,128)} %get-tuple-element.32.lam_ref, f32[16,2048]{1,0:T(8,128)} %bitcast.26, f32[4,16,2048]{2,1,0:T(8,128)} %get-tuple-element.33.parts_ref, ...), custom_call_target="tpu_custom_call" | custom-call | flops 134217728 | bytes 5767168 | tf_op jit(solution)/shard_map/pallas_call | solution.py:359
  23.9 4.1 %all-to-all-done.pieces_ref = bf16[8,16,2048]{2,1,0:T(8,128)(2,1)S(1)} async-done(((bf16[8,16,2048]{2,1,0:T(8,128)(2,1)}), bf16[8,16,2048]{2,1,0:T(8,128)(2,1)S(1)}, u32[]{:S(2)}, u32[]{:S(2)}) %all-to-all-start) | async-done | bytes 524320 | tf_op jit(solution)/shard_map/all_to_all | solution.py:413
  28.1 6.4 %shard_map.155 = (f32[256,2048]{1,0:T(8,128)}, f32[2,256,128]{2,1,0:T(8,128)}, f32[4,16,2048]{2,1,0:T(8,128)}, f32[16,2048]{1,0:T(8,128)}) custom-call(bf16[8,16,2048]{2,1,0:T(8,128)(2,1)S(1)} %all-to-all-done.pieces_ref, f32[16,2048]{1,0:T(8,128)} %get-tuple-element.32.lam_ref, f32[16,2048]{1,0:T(8,128)} %bitcast.27, ...), custom_call_target="tpu_custom_call" | custom-call | flops 16777216 | bytes 8527872 | tf_op jit(solution)/shard_map/pallas_call | solution.py:359
  34.5 0.1 collective-permute-start
  34.5 1.7 %collective-permute-done.peer_ref = f32[2,256,128]{2,1,0:T(8,128)S(1)} collective-permute-done((f32[2,256,128]{2,1,0:T(8,128)}, f32[2,256,128]{2,1,0:T(8,128)S(1)}, u32[]{:S(2)}, u32[]{:S(2)}) %collective-permute-start) | collective-permute-done | bytes 262176 | tf_op jit(solution)/shard_map/ppermute | solution.py:426
  36.3 7.3 %shard_map.156 = (bf16[256,2048]{1,0:T(8,128)(2,1)}, bf16[256,2048]{1,0:T(8,128)(2,1)}, f32[256,2048]{1,0:T(8,128)}, f32[1,2048]{1,0:T(1,128)}, f32[4,16,2048]{2,1,0:T(8,128)}, /*index=5*/bf16[8,16,2048]{2,1,0:T(8,128)(2,1)}) custom-call(f32[2,256,128]{2,1,0:T(8,128)} %get-tuple-element.36.sums_ref, f32[2,256,128]{2,1,0:T(8,128)S(1)} %collective-permute-done.peer_ref, ...), custom_call_target="tpu_custom_call" | custom-call | flops 16777216 | bytes 10108928 | tf_op jit(solution)/shard_map/pallas_call | solution.py:359
  43.6 3.6 %all-to-all-start.1 = ((bf16[8,16,2048]{2,1,0:T(8,128)(2,1)}), bf16[8,16,2048]{2,1,0:T(8,128)(2,1)S(1)}, u32[]{:S(2)}, u32[]{:S(2)}) async-start(bf16[8,16,2048]{2,1,0:T(8,128)(2,1)} %get-tuple-element.40), calls=%async_computation.1 | async-start | bytes 1048576 | tf_op jit(solution)/shard_map/all_to_all | solution.py:433
  47.2 12.6 %shard_map.157 = (f32[256,2048]{1,0:T(8,128)}, f32[16,48,128]{2,1,0:T(8,128)}) custom-call(f32[16,2048]{1,0:T(8,128)} %get-tuple-element.32.lam_ref, f32[256,2048]{1,0:T(8,128)} %get-tuple-element.42.gate_ref, bf16[256,2048]{1,0:T(8,128)(2,1)} %get-tuple-element.34.val_ref, f32[128,2048]{1,0:T(8,128)} %get-tuple-element.43.ks_ref, ...), custom_call_target="tpu_custom_call" | custom-call | flops 134217728 | bytes 8658944 | tf_op jit(solution)/shard_map/pallas_call | solution.py:359
  59.8 2.2 %all-to-all-done.1.pieces_ref = bf16[8,16,2048]{2,1,0:T(8,128)(2,1)S(1)} async-done(((bf16[8,16,2048]{2,1,0:T(8,128)(2,1)}), bf16[8,16,2048]{2,1,0:T(8,128)(2,1)S(1)}, u32[]{:S(2)}, u32[]{:S(2)}) %all-to-all-start.1) | async-done | bytes 524320 | tf_op jit(solution)/shard_map/all_to_all | solution.py:433
  62.0 2.1 %shard_map.158 = (f32[16,2048]{1,0:T(8,128)}, bf16[16,48,128]{2,1,0:T(8,128)(2,1)}) custom-call(bf16[8,16,2048]{2,1,0:T(8,128)(2,1)S(1)} %all-to-all-done.1.pieces_ref, f32[16,2048]{1,0:T(8,128)} %get-tuple-element.32.lam_ref, f32[16,2048]{1,0:T(8,128)} %bitcast.28, f32[16,2048]{1,0:T(8,128)} %get-tuple-element.41.slope_ref, ...), custom_call_target="tpu_custom_call" | custom-call | flops 1310720 | bytes 1638400 | tf_op jit(solution)/shard_map/pallas_call | solution.py:359
  64.2 13.5 %all_to_all.20 = bf16[16,48,128]{2,1,0:T(8,128)(2,1)S(1)} all-to-all(bf16[16,48,128]{2,1,0:T(8,128)(2,1)} %get-tuple-element.54), channel_id=1, replica_groups=mesh['ctx'=8,'chan'=2,'dp'=2] {'ctx','dp'}, dimensions={0} | all-to-all | bytes 393216 | tf_op jit(solution)/shard_map/all_to_all | solution.py:454
  77.7 0.7 broadcast_in_dim.26
  78.4 3.5 %all-to-all-start.3 = ((bf16[16,48,128]{2,1,0:T(8,128)(2,1)}), bf16[16,48,128]{2,1,0:T(8,128)(2,1)S(1)}, u32[]{:S(2)}, u32[]{:S(2)}) async-start(bf16[16,48,128]{2,1,0:T(8,128)(2,1)} %broadcast_in_dim.26), calls=%async_computation.3 | async-start | bytes 393216 | tf_op jit(solution)/shard_map/all_to_all | solution.py:456
  81.9 6.0 %shard_map.159 = (bf16[256,2048]{1,0:T(8,128)(2,1)}, bf16[256,2048]{1,0:T(8,128)(2,1)}) custom-call(f32[16,2048]{1,0:T(8,128)} %get-tuple-element.50.adj_ref, f32[16,2048]{1,0:T(8,128)} %get-tuple-element.32.lam_ref, f32[16,2048]{1,0:T(8,128)} %bitcast.29, f32[4,16,2048]{2,1,0:T(8,128)} %get-tuple-element.47.gw_ref, f32[256,2048]{1,0:T(8,128)} %get-tuple-element.51.vg_ref, ...), custom_call_target="tpu_custom_call" | custom-call | flops 16777216 | bytes 7208960 | tf_op jit(solution)/shard_map/pallas_call | solution.py:359
  87.9 2.0 %all-to-all-done.3 = bf16[16,48,128]{2,1,0:T(8,128)(2,1)S(1)} async-done(((bf16[16,48,128]{2,1,0:T(8,128)(2,1)}), bf16[16,48,128]{2,1,0:T(8,128)(2,1)S(1)}, u32[]{:S(2)}, u32[]{:S(2)}) %all-to-all-start.3) | async-done | bytes 196640 | tf_op jit(solution)/shard_map/all_to_all | solution.py:456
  90.0 0.6 slice.14
  90.6 0.7 fusion
  (2 shorter events, 0.1 us)
Async XLA Ops:
  6.3 21.7 %all-to-all-start = ((bf16[8,16,2048]{2,1,0:T(8,128)(2,1)}), bf16[8,16,2048]{2,1,0:T(8,128)(2,1)S(1)}, u32[]{:S(2)}, u32[]{:S(2)}) async-start(bf16[8,16,2048]{2,1,0:T(8,128)(2,1)} %get-tuple-element.31), calls=%async_computation | async-start | bytes 1048576 | tf_op jit(solution)/shard_map/all_to_all | solution.py:413
  34.5 1.8 %collective-permute-start = (f32[2,256,128]{2,1,0:T(8,128)}, f32[2,256,128]{2,1,0:T(8,128)S(1)}, u32[]{:S(2)}, u32[]{:S(2)}) collective-permute-start(f32[2,256,128]{2,1,0:T(8,128)} %get-tuple-element.36.sums_ref), channel_id=1, source_target_pairs={{0,2},{2,0},{1,3},{3,1},{4,6},{6,4},{5,7},{7,5},{8,10},{10,8},{9,1... | collective-permute-start | bytes 786440 | tf_op jit(solution)/shard_map/ppermute | solution.py:426
  43.6 18.5 %all-to-all-start.1 = ((bf16[8,16,2048]{2,1,0:T(8,128)(2,1)}), bf16[8,16,2048]{2,1,0:T(8,128)(2,1)S(1)}, u32[]{:S(2)}, u32[]{:S(2)}) async-start(bf16[8,16,2048]{2,1,0:T(8,128)(2,1)} %get-tuple-element.40), calls=%async_computation.1 | async-start | bytes 1048576 | tf_op jit(solution)/shard_map/all_to_all | solution.py:433
  78.4 11.6 %all-to-all-start.3 = ((bf16[16,48,128]{2,1,0:T(8,128)(2,1)}), bf16[16,48,128]{2,1,0:T(8,128)(2,1)S(1)}, u32[]{:S(2)}, u32[]{:S(2)}) async-start(bf16[16,48,128]{2,1,0:T(8,128)(2,1)} %broadcast_in_dim.26), calls=%async_computation.3 | async-start | bytes 393216 | tf_op jit(solution)/shard_map/all_to_all | solution.py:456

commit v5 on v4

--- a/solution.py
+++ b/solution.py
@@ -169,13 +169,14 @@
         conv_ref[a : a + chunk] = dot(ta_ref[...], triple(prod))
 
 
-def forward_kernel(chunk, pieces_ref, lam_ref, res_ref, parts_ref, conv_in_ref, q_ref, og_ref, gain_ref,
+def forward_begin(*refs):
+    sums_ref = refs[9]
+    sums_ref[...] = jnp.zeros_like(sums_ref)
+
+
+def forward_kernel(chunk, lam_ref, res_ref, parts_ref, conv_in_ref, gain_ref, pieces_ref, q_ref, og_ref,
                    conv_ref, sums_ref, states_ref, moved_ref, held):
     length, width = q_ref.shape
-
-    @pl.when(pl.program_id(0) == 0)
-    def _():
-        sums_ref[...] = jnp.zeros_like(sums_ref)
 
     def body(i, cols):
         lam_rows = lam_ref[:, cols]
@@ -207,18 +208,19 @@
     groups_of(width, body)
 
 
-def gate_kernel(model_width, chunk, sums_ref, peer_ref, lam_ref, conv_ref, q_ref, og_ref, gain_ref,
+def gate_begin(model_width, lam_ref, gain_ref, sums_ref, peer_ref, *refs):
+    inv_ref, coef_ref = refs[-2:]
+    squares = jnp.sum(sums_ref[0] + peer_ref[0], axis=1, keepdims=True)
+    inner = jnp.sum(sums_ref[1] + peer_ref[1], axis=1, keepdims=True)
+    inv = lax.rsqrt(squares / model_width + EPSILON)
+    coef = inv * inv * inv * inner / model_width
+    inv_ref[...] = jnp.broadcast_to(inv, inv_ref.shape)
+    coef_ref[...] = jnp.broadcast_to(coef, coef_ref.shape)
+
+
+def gate_kernel(chunk, lam_ref, gain_ref, sums_ref, peer_ref, conv_ref, q_ref, og_ref,
                 y_ref, gq_ref, gate_ref, gain_part_ref, gw_ref, send_ref, inv_ref, coef_ref):
     length, width = q_ref.shape
-
-    @pl.when(pl.program_id(0) == 0)
-    def _():
-        squares = jnp.sum(sums_ref[0] + peer_ref[0], axis=1, keepdims=True)
-        inner = jnp.sum(sums_ref[1] + peer_ref[1], axis=1, keepdims=True)
-        inv = lax.rsqrt(squares / model_width + EPSILON)
-        coef = inv * inv * inv * inner / model_width
-        inv_ref[...] = jnp.broadcast_to(inv, inv_ref.shape)
-        coef_ref[...] = jnp.broadcast_to(coef, coef_ref.shape)
 
     def body(i, cols):
         lam = spread(lam_ref, cols)
@@ -304,12 +306,12 @@
             slope = decay_chunk * (slope + float(chunk) * state) + slopes_ref[c, :, cols]
         grads_ref[i, :modes] = total_r
         grads_ref[i, modes : 2 * modes] = total_s
-        grads_ref[i, 2 * modes :] = jnp.broadcast_to(gain_part_ref[:, cols], (16, LANES))
-
-    groups_of(width, body)
-
-
-def adjoint_kernel(length, pieces_ref, lam_ref, res_ref, slope_ref, grads_ref, adj_ref, out_ref):
+        grads_ref[i, 2 * modes :] = jnp.broadcast_to(gain_part_ref[:, cols], (ROWS, LANES))
+
+    groups_of(width, body)
+
+
+def adjoint_kernel(length, lam_ref, res_ref, slope_ref, grads_ref, pieces_ref, adj_ref, out_ref):
     modes, width = lam_ref.shape
 
     def body(i, cols):
@@ -352,22 +354,85 @@
     groups_of(width, body)
 
 
-def call(kernel, grid, ins, outs, scratch, flops, limit=16):
-    arrays = [e[0] if e[3:] else pltpu.with_memory_space_constraint(e[0], pltpu.HBM) for e in ins]
-    moved = sum(a.size * a.dtype.itemsize for a in arrays)
-    moved += sum(int(np.prod(s)) * jnp.dtype(d).itemsize for s, d, _, _ in outs)
+def streamed(body, begin, steps, kinds_in, kinds_held, kinds_out, *refs):
+    n_in, n_out = len(kinds_in), len(kinds_out)
+    far_in, refs = refs[:n_in], refs[n_in:]
+    here, refs = refs[: len(kinds_held)], refs[len(kinds_held) :]
+    outs, refs = refs[:n_out], refs[n_out:]
+    near_in, refs = refs[:n_in], refs[n_in:]
+    away = [n for n, kind in enumerate(kinds_out) if not kind[2:]]
+    far_out, kinds_far = [outs[n] for n in away], [kinds_out[n][1] for n in away]
+    buffers, refs = refs[: len(away)], refs[len(away) :]
+    near_out = list(outs)
+    for n, buffer in zip(away, buffers):
+        near_out[n] = buffer
+    kinds_out = [kind[1] for kind in kinds_out]
+    scratch, (sem_in, sem_out) = refs[:-2], refs[-2:]
+
+    def view(ref, kind, b):
+        if kind is None:
+            return ref
+        axis, size = kind
+        start = b * size if axis == 0 else pl.multiple_of(b * size, LANES)
+        return ref.at[(slice(None),) * axis + (pl.ds(start, size),)]
+
+    def copies(far, near, kinds, sem, b, whole, outward):
+        for n, kind in enumerate(kinds):
+            if (kind is None) == whole:
+                pair = view(far[n], kind, b), view(near[n], kind, b)
+                source, target = pair[::-1] if outward else pair
+                yield pltpu.make_async_copy(source, target, sem.at[b, n])
+
+    for b in range(steps):
+        for whole in (True, False) if b == 0 else (False,):
+            for copy in copies(far_in, near_in, kinds_in, sem_in, b, whole, False):
+                copy.start()
+    for copy in copies(far_in, near_in, kinds_in, sem_in, 0, True, False):
+        copy.wait()
+    if begin is not None:
+        begin(*near_in, *here, *near_out, *scratch)
+
+    def step(b, _):
+        for copy in copies(far_in, near_in, kinds_in, sem_in, b, False, False):
+            copy.wait()
+        body(
+            *(view(r, k, b) for r, k in zip(near_in, kinds_in)),
+            *(view(r, k, b) for r, k in zip(here, kinds_held)),
+            *(view(r, k, b) for r, k in zip(near_out, kinds_out)),
+            *scratch,
+        )
+        for copy in copies(far_out, buffers, kinds_far, sem_out, b, False, True):
+            copy.start()
+        return 0
+
+    lax.fori_loop(0, steps, step, 0)
+    for copy in copies(far_out, buffers, kinds_far, sem_out, 0, True, True):
+        copy.start()
+    for b in range(steps):
+        for whole in (True, False) if b == 0 else (False,):
+            for copy in copies(far_out, buffers, kinds_far, sem_out, b, whole, True):
+                copy.wait()
+
+
+def call(kernel, steps, ins, outs, scratch, flops, begin=None):
+    here = [e for e in ins if e[2:]]
+    ins = [e for e in ins if not e[2:]]
+    arrays = [pltpu.with_memory_space_constraint(a, pltpu.HBM) for a, _ in ins]
+    buffers = [(a.shape, a.dtype) for a in arrays] + [e[0] for e in outs if not e[2:]]
+    moved = sum(int(np.prod(s)) * jnp.dtype(d).itemsize for s, d in buffers)
+    far = pl.BlockSpec(memory_space=pltpu.HBM)
+    near = pl.BlockSpec(memory_space=pltpu.VMEM)
     return pl.pallas_call(
-        kernel,
-        grid=(grid,),
-        in_specs=[pl.BlockSpec(e[1], e[2]) for e in ins],
-        out_specs=[pl.BlockSpec(b, m) for _, _, b, m in outs],
-        out_shape=[pltpu.HBM(s, d) for s, d, _, _ in outs],
-        scratch_shapes=scratch,
-        compiler_params=pltpu.CompilerParams(
-            dimension_semantics=("arbitrary",), vmem_limit_bytes=limit * MIB
-        ),
+        functools.partial(streamed, kernel, begin, steps, [k for _, k in ins], [e[1] for e in here], outs),
+        in_specs=[far] * len(ins) + [near] * len(here),
+        out_specs=[near if e[2:] else far for e in outs],
+        out_shape=[jax.ShapeDtypeStruct(*e[0]) if e[2:] else pltpu.HBM(*e[0]) for e in outs],
+        scratch_shapes=[pltpu.VMEM(s, d) for s, d in buffers]
+        + scratch
+        + [pltpu.SemaphoreType.DMA((steps, len(ins))), pltpu.SemaphoreType.DMA((steps, len(outs)))],
+        compiler_params=pltpu.CompilerParams(vmem_limit_bytes=24 * MIB),
         cost_estimate=pl.CostEstimate(flops=flops, bytes_accessed=moved, transcendentals=0),
-    )(*arrays)
+    )(*arrays, *(e[0] for e in here))
 
 
 def shards(q_stream, k_stream, v_stream, out_grad, norm_gain, residue, rate):
@@ -386,21 +451,17 @@
     gain = norm_gain[None]
     full = fourier(chunk)
     basis = [terms(full, "hl"), terms(full, "hhl"), terms(full.T / np.float32(chunk), "hhl")]
-
-    def block(shape, last=None):
-        lead = tuple(shape[:-1])
-        return (*lead, last or width), lambda i: (*(0 for _ in lead), i)
+    basis = [(x, None) for x in basis]
 
     def inputs(*arrays):
-        return [(a, *block(a.shape)) for a in arrays]
+        return [(a, (a.ndim - 1, width)) for a in arrays]
 
     def outputs(*shapes_types):
-        return [((*s, channels), d, *block((*s, channels))) for s, d in shapes_types]
-
-    def fixed(shape):
-        return shape, lambda i: (0,) * len(shape)
-
-    basis = [(x, *fixed(x.shape)) for x in basis]
+        return [(((*s, channels), d), (len(s), width)) for s, d in shapes_types]
+
+    def held_inputs(*arrays):
+        return [(a, (a.ndim - 1, width), True) for a in arrays]
+
     unit = 2 * length * channels * modes
     send = ((count, modes), BF16)
     states = ((chunks, modes), F32)
@@ -416,37 +477,36 @@
         outputs(((length,), F32), ((2 * chunk,), F32), states, ((modes,), F32)),
         [pltpu.VMEM((chunk, width), F32)], 8 * unit,
     )
-    sums_shape = (2, length, LANES)
     conv, sums, carried, moved = call(
         functools.partial(forward_kernel, chunk), grid,
-        [(pieces, *block(pieces.shape), True)] + inputs(lam, res, parts, conv_local, q, og, gain),
-        outputs(((length,), F32)) + [(sums_shape, F32, *fixed(sums_shape))] + outputs(states, ((modes,), F32)),
-        [held], unit,
+        inputs(lam, res, parts, conv_local, gain) + held_inputs(pieces, q, og),
+        [(((length, channels), F32), (1, width), True), (((2, length, LANES), F32), None, True)]
+        + outputs(states, ((modes,), F32)),
+        [held], unit, forward_begin,
     )
     peers = lax.ppermute(sums, "chan", [(0, 1), (1, 0)])
     y_out, grad_q, gate, gain_part, gw, state = call(
-        functools.partial(gate_kernel, model_width, chunk), grid,
-        [(sums, *fixed(sums_shape)), (peers, *fixed(sums_shape), True)] + inputs(lam, conv, q, og, gain),
+        functools.partial(gate_kernel, chunk), grid,
+        inputs(lam, gain) + [(sums, None, True), (peers, None, True)] + held_inputs(conv, q, og),
         outputs(((length,), BF16), ((length,), BF16), ((length,), F32), ((1,), F32), states, send),
-        [pltpu.VMEM((length, LANES), F32)] * 2, unit,
+        [pltpu.VMEM((length, LANES), F32)] * 2, unit, functools.partial(gate_begin, model_width),
     )
     later = lax.all_to_all(state, "ctx", 0, 0)
-    rows = 2 * modes + 16
+    rows = 2 * modes + ROWS
     grads_shape = (groups, rows, LANES)
     vg_local, grads = call(
         functools.partial(backward_kernel, chunk), grid,
         inputs(lam, gate, vals, ks, carried, moved, slopes, gw, gain_part) + basis,
-        outputs(((length,), F32))
-        + [(grads_shape, F32, (width // LANES, rows, LANES), lambda i: (i, 0, 0))],
+        outputs(((length,), F32)) + [((grads_shape, F32), (0, width // LANES))],
         [pltpu.VMEM((chunk, width), F32)], 8 * unit,
     )
     adj, grads = call(
-        functools.partial(adjoint_kernel, float(length)), 1,
-        [(later, *fixed(later.shape), True)] + [(a, *fixed(a.shape)) for a in (lam, res, slope, grads)],
-        [(lam.shape, F32, *fixed(lam.shape)), (grads_shape, BF16, *fixed(grads_shape))], [], channels * modes * 40,
+        functools.partial(adjoint_kernel, float(length)), grid,
+        inputs(lam, res, slope) + [(grads, (0, width // LANES)), (later, (2, width), True)],
+        outputs(((modes,), F32)) + [((grads_shape, BF16), (0, width // LANES))], [], channels * modes * 40,
     )
     grad_k, grad_v = call(
-        functools.partial(finish_kernel, chunk), grid, inputs(adj, lam, res, gw, vg_local, k, v),
+        functools.partial(finish_kernel, chunk), grid, inputs(adj, lam, res, gw, vg_local) + held_inputs(k, v),
         outputs(((length,), BF16), ((length,), BF16)), [held], unit,
     )
     both = ("ctx", "dp")

time: 92.2 us -> 89 us (0.965)
  Pallas kernels: 50.4 us -> 48 us
    pallas_call x7, Pallas kernels: 50.4 us -> 48 us  [call(): pl.pallas_call(functools.partial(streamed, kernel, begin, steps, [k for _...]
where the time goes in v5:
time: 89 us; the launch traced here: 88.4 us
  Pallas kernels  48 us (54%)
  starting transfers between devices  14.5 us (16%)
  blocking collectives  13 us (15%)
  waiting for transfers between devices  10.1 us (11%)
  local copies, waits for them, and re-layouts  2.02 us (2%)
    pallas_call x7, Pallas kernels, call(): pl.pallas_call(functools.partial(streamed, kernel, begin, steps, [k for _...  48 us
    all_to_all x1, blocking collectives, shards(): parts = lax.all_to_all(grads, both, 0, 0)  13 us
    all_to_all x1, starting transfers between devices, shards(): pieces = lax.all_to_all(state, 'ctx', 0, 0)  7.26 us
    all_to_all x1, waiting for transfers between devices, shards(): pieces = lax.all_to_all(state, 'ctx', 0, 0)  3.76 us
    all_to_all x1, starting transfers between devices, shards(): later = lax.all_to_all(state, 'ctx', 0, 0)  3.65 us
    all_to_all x1, starting transfers between devices, shards(): lax.all_to_all(jnp.broadcast_to(mine[None], grads.shape), both, 0, 0)  3.52 us
    all_to_all x1, waiting for transfers between devices, shards(): lax.all_to_all(jnp.broadcast_to(mine[None], grads.shape), both, 0, 0)  2.62 us
    all_to_all x1, waiting for transfers between devices, shards(): later = lax.all_to_all(state, 'ctx', 0, 0)  2.17 us
  transfers between devices with their start and end apart: 4, of which 4 were waited for; matrix products, arithmetic and copies ran while one was open for 0% of the time, Pallas kernels for 32%

profile of v5, /device:TPU:0, one launch (start us, length us, event | category | flops | bytes accessed | tf_op | source)
XLA Modules:
  0.0 88.4 jit_solution(9952592794301416685)
XLA Ops:
  0.6 0.0 copy-start.2
  0.6 0.0 copy-start.3
  0.7 5.6 %shard_map.153 = (bf16[256,2048]{1,0:T(8,128)(2,1)}, f32[16,2048]{1,0:T(8,128)}, f32[4,16,2048]{2,1,0:T(8,128)}, bf16[8,16,2048]{2,1,0:T(8,128)(2,1)}) custom-call(bf16[256,2048]{1,0:T(8,128)(2,1)} %bitcast.18, bf16[256,2048]{1,0:T(8,128)(2,1)} %bitcast.20, f32[16,2048]{1,0:T(8,128)} %bitcast.30), custom_call_target="tpu_custom_call" | custom-call | flops 16777216 | bytes 4456448 | tf_op jit(solution)/shard_map/pallas_call | solution.py:425
  6.3 7.3 %all-to-all-start = ((bf16[8,16,2048]{2,1,0:T(8,128)(2,1)}), bf16[8,16,2048]{2,1,0:T(8,128)(2,1)S(1)}, u32[]{:S(2)}, u32[]{:S(2)}) async-start(bf16[8,16,2048]{2,1,0:T(8,128)(2,1)} %get-tuple-element.35), calls=%async_computation | async-start | bytes 1048576 | tf_op jit(solution)/shard_map/all_to_all | solution.py:474
  13.6 10.7 %shard_map.154 = (f32[256,2048]{1,0:T(8,128)}, f32[128,2048]{1,0:T(8,128)}, f32[4,16,2048]{2,1,0:T(8,128)}, f32[16,2048]{1,0:T(8,128)}) custom-call(bf16[256,2048]{1,0:T(8,128)(2,1)} %get-tuple-element.33.refs_0_.refs_2_, f32[16,2048]{1,0:T(8,128)} %get-tuple-element.31.refs_1_.refs_0_, f32[16,2048]{1,0:T(8,128)} %bitcast.26, ...), custom_call_target="tpu_custom_call" | custom-call | flops 134217728 | bytes 5767168 | tf_op jit(solution)/shard_map/pallas_call | solution.py:425
  24.3 3.8 %all-to-all-done.refs_5_ = bf16[8,16,2048]{2,1,0:T(8,128)(2,1)S(1)} async-done(((bf16[8,16,2048]{2,1,0:T(8,128)(2,1)}), bf16[8,16,2048]{2,1,0:T(8,128)(2,1)S(1)}, u32[]{:S(2)}, u32[]{:S(2)}) %all-to-all-start) | async-done | bytes 524320 | tf_op jit(solution)/shard_map/all_to_all | solution.py:474
  28.1 0.0 copy-done.2
  28.1 0.0 copy-done.3
  28.1 5.5 %shard_map.155 = (f32[256,2048]{1,0:T(8,128)S(1)}, f32[2,256,128]{2,1,0:T(8,128)S(1)}, f32[4,16,2048]{2,1,0:T(8,128)}, f32[16,2048]{1,0:T(8,128)}) custom-call(f32[16,2048]{1,0:T(8,128)} %get-tuple-element.31.refs_1_.refs_0_, f32[16,2048]{1,0:T(8,128)} %bitcast.27, f32[4,16,2048]{2,1,0:T(8,128)} %get-tuple-element.32.refs_3_.refs_2_, ...), custom_call_target="tpu_custom_call" | custom-call | flops 16777216 | bytes 3547136 | tf_op jit(solution)/shard_map/pallas_call | solution.py:425
  33.5 0.1 collective-permute-start
  33.6 1.5 %collective-permute-done.refs_3_ = f32[2,256,128]{2,1,0:T(8,128)S(1)} collective-permute-done((f32[2,256,128]{2,1,0:T(8,128)S(1)}, f32[2,256,128]{2,1,0:T(8,128)S(1)}, u32[]{:S(2)}, u32[]{:S(2)}) %collective-permute-start) | collective-permute-done | bytes 262176 | tf_op jit(solution)/shard_map/ppermute | solution.py:487
  35.1 6.2 %shard_map.156 = (bf16[256,2048]{1,0:T(8,128)(2,1)}, bf16[256,2048]{1,0:T(8,128)(2,1)}, f32[256,2048]{1,0:T(8,128)}, f32[1,2048]{1,0:T(1,128)}, f32[4,16,2048]{2,1,0:T(8,128)}, /*index=5*/bf16[8,16,2048]{2,1,0:T(8,128)(2,1)}) custom-call(f32[16,2048]{1,0:T(8,128)} %get-tuple-element.31.refs_1_.refs_0_, f32[1,2048]{1,0:T(1,128)} %bitcast.32, ...), custom_call_target="tpu_custom_call" | custom-call | flops 16777216 | bytes 5390336 | tf_op jit(solution)/shard_map/pallas_call | solution.py:425
  41.4 3.6 %all-to-all-start.1 = ((bf16[8,16,2048]{2,1,0:T(8,128)(2,1)}), bf16[8,16,2048]{2,1,0:T(8,128)(2,1)S(1)}, u32[]{:S(2)}, u32[]{:S(2)}) async-start(bf16[8,16,2048]{2,1,0:T(8,128)(2,1)} %get-tuple-element.49), calls=%async_computation.1 | async-start | bytes 1048576 | tf_op jit(solution)/shard_map/all_to_all | solution.py:494
  45.0 12.6 %shard_map.157 = (f32[256,2048]{1,0:T(8,128)}, f32[16,40,128]{2,1,0:T(8,128)}) custom-call(f32[16,2048]{1,0:T(8,128)} %get-tuple-element.31.refs_1_.refs_0_, f32[256,2048]{1,0:T(8,128)} %get-tuple-element.41.refs_1_, bf16[256,2048]{1,0:T(8,128)(2,1)} %get-tuple-element.33.refs_0_.refs_2_, f32[128,2048]{1,0:T(8,128)} %get-tuple-element.42.refs_3_, ...), custom_call_target="tpu_custom_call" | custom-call | flops 134217728 | bytes 8593408 | tf_op jit(solution)/shard_map/pallas_call | solution.py:425
  57.7 0.0 copy-start
  57.7 0.0 copy-start.1
  57.7 2.2 %all-to-all-done.1.refs_4_ = bf16[8,16,2048]{2,1,0:T(8,128)(2,1)S(1)} async-done(((bf16[8,16,2048]{2,1,0:T(8,128)(2,1)}), bf16[8,16,2048]{2,1,0:T(8,128)(2,1)S(1)}, u32[]{:S(2)}, u32[]{:S(2)}) %all-to-all-start.1) | async-done | bytes 524320 | tf_op jit(solution)/shard_map/all_to_all | solution.py:494
  59.9 2.1 %shard_map.158 = (f32[16,2048]{1,0:T(8,128)}, bf16[16,40,128]{2,1,0:T(8,128)(2,1)}) custom-call(f32[16,2048]{1,0:T(8,128)} %get-tuple-element.31.refs_1_.refs_0_, f32[16,2048]{1,0:T(8,128)} %bitcast.28, f32[16,2048]{1,0:T(8,128)} %get-tuple-element.40.refs_2_, f32[16,40,128]{2,1,0:T(8,128)} %get-tuple-element.48.refs_3_, ...), custom_call_target="tpu_custom_call" | custom-call | flops 1310720 | bytes 1015808 | tf_op jit(solution)/shard_map/pallas_call | solution.py:425
  62.0 13.0 %all_to_all.20 = bf16[16,40,128]{2,1,0:T(8,128)(2,1)S(1)} all-to-all(bf16[16,40,128]{2,1,0:T(8,128)(2,1)} %get-tuple-element.54), channel_id=1, replica_groups=mesh['ctx'=8,'chan'=2,'dp'=2] {'ctx','dp'}, dimensions={0} | all-to-all | bytes 327680 | tf_op jit(solution)/shard_map/all_to_all | solution.py:514
  74.9 0.7 broadcast_in_dim.26
  75.6 3.5 %all-to-all-start.3 = ((bf16[16,40,128]{2,1,0:T(8,128)(2,1)}), bf16[16,40,128]{2,1,0:T(8,128)(2,1)S(1)}, u32[]{:S(2)}, u32[]{:S(2)}) async-start(bf16[16,40,128]{2,1,0:T(8,128)(2,1)} %broadcast_in_dim.26), calls=%async_computation.3 | async-start | bytes 327680 | tf_op jit(solution)/shard_map/all_to_all | solution.py:516
  79.2 0.0 copy-done
  79.2 0.0 copy-done.1
  79.2 5.2 %shard_map.159 = (bf16[256,2048]{1,0:T(8,128)(2,1)}, bf16[256,2048]{1,0:T(8,128)(2,1)}) custom-call(f32[16,2048]{1,0:T(8,128)} %get-tuple-element.50.refs_0_, f32[16,2048]{1,0:T(8,128)} %get-tuple-element.31.refs_1_.refs_0_, f32[16,2048]{1,0:T(8,128)} %bitcast.29, f32[4,16,2048]{2,1,0:T(8,128)} %get-tuple-element.46.refs_7_.refs_3_, ...), custom_call_target="tpu_custom_call" | custom-call | flops 16777216 | bytes 5111808 | tf_op jit(solution)/shard_map/pallas_call | solution.py:425
  84.4 2.6 %all-to-all-done.3 = bf16[16,40,128]{2,1,0:T(8,128)(2,1)S(1)} async-done(((bf16[16,40,128]{2,1,0:T(8,128)(2,1)}), bf16[16,40,128]{2,1,0:T(8,128)(2,1)S(1)}, u32[]{:S(2)}, u32[]{:S(2)}) %all-to-all-start.3) | async-done | bytes 163872 | tf_op jit(solution)/shard_map/all_to_all | solution.py:516
  87.1 0.6 slice.14
  87.7 0.7 fusion
  (2 shorter events, 0.1 us)
Async XLA Ops:
  0.6 27.4 %copy-start.2 = (bf16[1,256,2048]{2,1,0:T(8,128)(2,1)S(1)}, bf16[1,256,2048]{2,1,0:T(8,128)(2,1)}, u32[]{:S(2)}) copy-start(bf16[1,256,2048]{2,1,0:T(8,128)(2,1)} %param.10) | copy-start | bytes 3145732
  0.6 27.4 %copy-start.3 = (bf16[1,256,2048]{2,1,0:T(8,128)(2,1)S(1)}, bf16[1,256,2048]{2,1,0:T(8,128)(2,1)}, u32[]{:S(2)}) copy-start(bf16[1,256,2048]{2,1,0:T(8,128)(2,1)} %param.13) | copy-start | bytes 3145732
  6.3 21.8 %all-to-all-start = ((bf16[8,16,2048]{2,1,0:T(8,128)(2,1)}), bf16[8,16,2048]{2,1,0:T(8,128)(2,1)S(1)}, u32[]{:S(2)}, u32[]{:S(2)}) async-start(bf16[8,16,2048]{2,1,0:T(8,128)(2,1)} %get-tuple-element.35), calls=%async_computation | async-start | bytes 1048576 | tf_op jit(solution)/shard_map/all_to_all | solution.py:474
  33.5 1.6 %collective-permute-start = (f32[2,256,128]{2,1,0:T(8,128)S(1)}, f32[2,256,128]{2,1,0:T(8,128)S(1)}, u32[]{:S(2)}, u32[]{:S(2)}) collective-permute-start(f32[2,256,128]{2,1,0:T(8,128)S(1)} %get-tuple-element.36.refs_2_), channel_id=1, source_target_pairs={{0,2},{2,0},{1,3},{3,1},{4,6},{6,4},{5,7},{7,5},{8,10},{10,8},{9,1... | collective-permute-start | bytes 786440 | tf_op jit(solution)/shard_map/ppermute | solution.py:487
  41.4 18.5 %all-to-all-start.1 = ((bf16[8,16,2048]{2,1,0:T(8,128)(2,1)}), bf16[8,16,2048]{2,1,0:T(8,128)(2,1)S(1)}, u32[]{:S(2)}, u32[]{:S(2)}) async-start(bf16[8,16,2048]{2,1,0:T(8,128)(2,1)} %get-tuple-element.49), calls=%async_computation.1 | async-start | bytes 1048576 | tf_op jit(solution)/shard_map/all_to_all | solution.py:494
  57.7 21.5 %copy-start = (bf16[1,256,2048]{2,1,0:T(8,128)(2,1)S(1)}, bf16[1,256,2048]{2,1,0:T(8,128)(2,1)}, u32[]{:S(2)}) copy-start(bf16[1,256,2048]{2,1,0:T(8,128)(2,1)} %param.11) | copy-start | bytes 3145732
  57.7 21.5 %copy-start.1 = (bf16[1,256,2048]{2,1,0:T(8,128)(2,1)S(1)}, bf16[1,256,2048]{2,1,0:T(8,128)(2,1)}, u32[]{:S(2)}) copy-start(bf16[1,256,2048]{2,1,0:T(8,128)(2,1)} %param.12) | copy-start | bytes 3145732
  75.6 11.4 %all-to-all-start.3 = ((bf16[16,40,128]{2,1,0:T(8,128)(2,1)}), bf16[16,40,128]{2,1,0:T(8,128)(2,1)S(1)}, u32[]{:S(2)}, u32[]{:S(2)}) async-start(bf16[16,40,128]{2,1,0:T(8,128)(2,1)} %broadcast_in_dim.26), calls=%async_computation.3 | async-start | bytes 327680 | tf_op jit(solution)/shard_map/all_to_all | solution.py:516

commit v6 on v5

--- a/solution.py
+++ b/solution.py
@@ -26,13 +26,22 @@
 def terms(full, order):
     high = full.astype(jnp.bfloat16)
     low = (full - high.astype(np.float32)).astype(jnp.bfloat16)
-    return jnp.asarray(np.concatenate([{"h": high, "l": low}[o] for o in order], axis=1))
+    pick = {"h": high, "l": low, "0": np.zeros_like(high)}
+    return jnp.asarray(np.block([[pick[o] for o in row] for row in order]))
 
 
 def triple(x):
     high = x.astype(BF16)
     low = (x - high.astype(F32)).astype(BF16)
     return jnp.concatenate([high, low, high], axis=0)
+
+
+def inverse(t_ref, x):
+    high = x.astype(BF16)
+    low = (x - high.astype(F32)).astype(BF16)
+    both = dot(t_ref[...], jnp.concatenate([high, low], axis=0))
+    half = both.shape[0] // 2
+    return both[:half] + both[half:]
 
 
 def dot(a, b):
@@ -116,7 +125,7 @@
             acc = None
             for a in range(c * chunk, (c + 1) * chunk, 16):
                 rows = slice(a, a + 16)
-                vals = (k_ref[rows, cols].astype(F32) * v_ref[rows, cols].astype(F32)).astype(BF16)
+                vals = k_ref[rows, cols] * v_ref[rows, cols]
                 val_ref[rows, cols] = vals
                 vals = vals.astype(F32)
                 for tile in (vals[:ROWS], vals[ROWS:]):
@@ -166,16 +175,22 @@
         vs = dot(fv_ref[...], jnp.concatenate([vals, vals], axis=0))
         vr, vi = vs[:chunk], vs[chunk:]
         prod = jnp.concatenate([vr * kr - vi * ki, vr * ki + vi * kr], axis=0)
-        conv_ref[a : a + chunk] = dot(ta_ref[...], triple(prod))
+        conv_ref[a : a + chunk] = inverse(ta_ref, prod)
 
 
 def forward_begin(*refs):
-    sums_ref = refs[9]
-    sums_ref[...] = jnp.zeros_like(sums_ref)
+    acc_ref = refs[-1]
+    acc_ref[...] = jnp.zeros_like(acc_ref)
+
+
+def forward_end(*refs):
+    sums_ref, acc_ref = refs[9], refs[-1]
+    for n in range(2):
+        sums_ref[n : n + 1] = jnp.sum(acc_ref[n].T, axis=0, keepdims=True)
 
 
 def forward_kernel(chunk, lam_ref, res_ref, parts_ref, conv_in_ref, gain_ref, pieces_ref, q_ref, og_ref,
-                   conv_ref, sums_ref, states_ref, moved_ref, held):
+                   conv_ref, sums_ref, states_ref, moved_ref, held, acc_ref):
     length, width = q_ref.shape
 
     def body(i, cols):
@@ -202,20 +217,20 @@
                 conv_ref[rows, cols] = conv
                 mixed = q_ref[rows, cols].astype(F32) * conv
                 scaled = gain * og_ref[rows, cols].astype(F32)
-                sums_ref[0, rows] += mixed * mixed
-                sums_ref[1, rows] += scaled * mixed
+                acc_ref[0, rows] += mixed * mixed
+                acc_ref[1, rows] += scaled * mixed
 
     groups_of(width, body)
 
 
 def gate_begin(model_width, lam_ref, gain_ref, sums_ref, peer_ref, *refs):
     inv_ref, coef_ref = refs[-2:]
-    squares = jnp.sum(sums_ref[0] + peer_ref[0], axis=1, keepdims=True)
-    inner = jnp.sum(sums_ref[1] + peer_ref[1], axis=1, keepdims=True)
+    squares = sums_ref[0:1] + peer_ref[0:1]
+    inner = sums_ref[1:2] + peer_ref[1:2]
     inv = lax.rsqrt(squares / model_width + EPSILON)
     coef = inv * inv * inv * inner / model_width
-    inv_ref[...] = jnp.broadcast_to(inv, inv_ref.shape)
-    coef_ref[...] = jnp.broadcast_to(coef, coef_ref.shape)
+    for row, ref in ((inv, inv_ref), (coef, coef_ref)):
+        ref[...] = jnp.broadcast_to(row, (LANES, row.shape[1])).T
 
 
 def gate_kernel(chunk, lam_ref, gain_ref, sums_ref, peer_ref, conv_ref, q_ref, og_ref,
@@ -273,8 +288,8 @@
         cross_r = real if cross_r is None else cross_r + real
         cross_i = imag if cross_i is None else cross_i + imag
         prod = jnp.concatenate([gr * kr + gi * ki, gi * kr - gr * ki], axis=0)
-        vg_ref[a : a + chunk] = dot(ta_ref[...], triple(prod))
-    kg[...] = dot(ta_ref[...], triple(jnp.concatenate([cross_r, cross_i], axis=0)))
+        vg_ref[a : a + chunk] = inverse(ta_ref, prod)
+    kg[...] = inverse(ta_ref, jnp.concatenate([cross_r, cross_i], axis=0))
 
     def body(i, cols):
         lam_rows = lam_ref[:, cols]
@@ -311,7 +326,7 @@
     groups_of(width, body)
 
 
-def adjoint_kernel(length, lam_ref, res_ref, slope_ref, grads_ref, pieces_ref, adj_ref, out_ref):
+def adjoint_kernel(length, grads_ref, lam_ref, res_ref, slope_ref, pieces_ref, adj_ref, out_ref):
     modes, width = lam_ref.shape
 
     def body(i, cols):
@@ -354,19 +369,21 @@
     groups_of(width, body)
 
 
-def streamed(body, begin, steps, kinds_in, kinds_held, kinds_out, *refs):
-    n_in, n_out = len(kinds_in), len(kinds_out)
-    far_in, refs = refs[:n_in], refs[n_in:]
-    here, refs = refs[: len(kinds_held)], refs[len(kinds_held) :]
-    outs, refs = refs[:n_out], refs[n_out:]
-    near_in, refs = refs[:n_in], refs[n_in:]
-    away = [n for n, kind in enumerate(kinds_out) if not kind[2:]]
-    far_out, kinds_far = [outs[n] for n in away], [kinds_out[n][1] for n in away]
-    buffers, refs = refs[: len(away)], refs[len(away) :]
-    near_out = list(outs)
-    for n, buffer in zip(away, buffers):
-        near_out[n] = buffer
-    kinds_out = [kind[1] for kind in kinds_out]
+def streamed(body, begin, end, steps, kinds_in, kinds_out, *refs):
+    ins, refs = refs[: len(kinds_in)], refs[len(kinds_in) :]
+    outs, refs = refs[: len(kinds_out)], refs[len(kinds_out) :]
+
+    def buffered(arrays, kinds, refs):
+        away = [n for n, kind in enumerate(kinds) if not kind[2:]]
+        near = list(arrays)
+        for n, buffer in zip(away, refs):
+            near[n] = buffer
+        far = [arrays[n] for n in away]
+        return near, far, refs[: len(away)], [kinds[n][1] for n in away], refs[len(away) :]
+
+    near_in, far_in, buffers_in, moved_in, refs = buffered(ins, kinds_in, refs)
+    near_out, far_out, buffers_out, moved_out, refs = buffered(outs, kinds_out, refs)
+    kinds_in, kinds_out = [kind[1] for kind in kinds_in], [kind[1] for kind in kinds_out]
     scratch, (sem_in, sem_out) = refs[:-2], refs[-2:]
 
     def view(ref, kind, b):
@@ -385,46 +402,47 @@
 
     for b in range(steps):
         for whole in (True, False) if b == 0 else (False,):
-            for copy in copies(far_in, near_in, kinds_in, sem_in, b, whole, False):
+            for copy in copies(far_in, buffers_in, moved_in, sem_in, b, whole, False):
                 copy.start()
-    for copy in copies(far_in, near_in, kinds_in, sem_in, 0, True, False):
+    for copy in copies(far_in, buffers_in, moved_in, sem_in, 0, True, False):
         copy.wait()
     if begin is not None:
-        begin(*near_in, *here, *near_out, *scratch)
+        begin(*near_in, *near_out, *scratch)
 
     def step(b, _):
-        for copy in copies(far_in, near_in, kinds_in, sem_in, b, False, False):
+        for copy in copies(far_in, buffers_in, moved_in, sem_in, b, False, False):
             copy.wait()
         body(
             *(view(r, k, b) for r, k in zip(near_in, kinds_in)),
-            *(view(r, k, b) for r, k in zip(here, kinds_held)),
             *(view(r, k, b) for r, k in zip(near_out, kinds_out)),
             *scratch,
         )
-        for copy in copies(far_out, buffers, kinds_far, sem_out, b, False, True):
+        for copy in copies(far_out, buffers_out, moved_out, sem_out, b, False, True):
             copy.start()
         return 0
 
     lax.fori_loop(0, steps, step, 0)
-    for copy in copies(far_out, buffers, kinds_far, sem_out, 0, True, True):
+    if end is not None:
+        end(*near_in, *near_out, *scratch)
+    for copy in copies(far_out, buffers_out, moved_out, sem_out, 0, True, True):
         copy.start()
     for b in range(steps):
         for whole in (True, False) if b == 0 else (False,):
-            for copy in copies(far_out, buffers, kinds_far, sem_out, b, whole, True):
+            for copy in copies(far_out, buffers_out, moved_out, sem_out, b, whole, True):
                 copy.wait()
 
 
-def call(kernel, steps, ins, outs, scratch, flops, begin=None):
-    here = [e for e in ins if e[2:]]
-    ins = [e for e in ins if not e[2:]]
-    arrays = [pltpu.with_memory_space_constraint(a, pltpu.HBM) for a, _ in ins]
-    buffers = [(a.shape, a.dtype) for a in arrays] + [e[0] for e in outs if not e[2:]]
-    moved = sum(int(np.prod(s)) * jnp.dtype(d).itemsize for s, d in buffers)
+def call(kernel, steps, ins, outs, scratch, flops, begin=None, end=None):
+    arrays = [e[0] if e[2:] else pltpu.with_memory_space_constraint(e[0], pltpu.HBM) for e in ins]
+    buffers = [(e[0].shape, e[0].dtype) for e in ins if not e[2:]] + [e[0] for e in outs if not e[2:]]
+    moved = sum(a.size * a.dtype.itemsize for a in arrays)
+    moved += sum(int(np.prod(e[0][0])) * jnp.dtype(e[0][1]).itemsize for e in outs)
     far = pl.BlockSpec(memory_space=pltpu.HBM)
     near = pl.BlockSpec(memory_space=pltpu.VMEM)
+    kinds = [(None, *e[1:]) for e in ins]
     return pl.pallas_call(
-        functools.partial(streamed, kernel, begin, steps, [k for _, k in ins], [e[1] for e in here], outs),
-        in_specs=[far] * len(ins) + [near] * len(here),
+        functools.partial(streamed, kernel, begin, end, steps, kinds, outs),
+        in_specs=[near if e[2:] else far for e in ins],
         out_specs=[near if e[2:] else far for e in outs],
         out_shape=[jax.ShapeDtypeStruct(*e[0]) if e[2:] else pltpu.HBM(*e[0]) for e in outs],
         scratch_shapes=[pltpu.VMEM(s, d) for s, d in buffers]
@@ -432,7 +450,7 @@
         + [pltpu.SemaphoreType.DMA((steps, len(ins))), pltpu.SemaphoreType.DMA((steps, len(outs)))],
         compiler_params=pltpu.CompilerParams(vmem_limit_bytes=24 * MIB),
         cost_estimate=pl.CostEstimate(flops=flops, bytes_accessed=moved, transcendentals=0),
-    )(*arrays, *(e[0] for e in here))
+    )(*arrays)
 
 
 def shards(q_stream, k_stream, v_stream, out_grad, norm_gain, residue, rate):
@@ -446,20 +464,21 @@
     groups = channels // LANES
     width = min(channels, 512)
     grid = channels // width
+    broad = min(channels, 1024)
     q, k, v, og = (x[0] for x in (q_stream, k_stream, v_stream, out_grad))
     res = residue.T
     gain = norm_gain[None]
     full = fourier(chunk)
-    basis = [terms(full, "hl"), terms(full, "hhl"), terms(full.T / np.float32(chunk), "hhl")]
+    basis = [terms(full, ["hl"]), terms(full, ["hhl"]), terms(full.T / np.float32(chunk), ["hh", "l0"])]
     basis = [(x, None) for x in basis]
 
-    def inputs(*arrays):
+    def inputs(*arrays, width=width):
         return [(a, (a.ndim - 1, width)) for a in arrays]
 
-    def outputs(*shapes_types):
+    def outputs(*shapes_types, width=width):
         return [(((*s, channels), d), (len(s), width)) for s, d in shapes_types]
 
-    def held_inputs(*arrays):
+    def held_inputs(*arrays, width=width):
         return [(a, (a.ndim - 1, width), True) for a in arrays]
 
     unit = 2 * length * channels * modes
@@ -473,21 +492,21 @@
     )
     pieces = lax.all_to_all(state, "ctx", 0, 0)
     conv_local, ks, slopes, slope = call(
-        functools.partial(local_kernel, chunk), grid, inputs(vals, lam, res, parts) + basis,
-        outputs(((length,), F32), ((2 * chunk,), F32), states, ((modes,), F32)),
-        [pltpu.VMEM((chunk, width), F32)], 8 * unit,
+        functools.partial(local_kernel, chunk), channels // broad, inputs(vals, lam, res, parts, width=broad) + basis,
+        outputs(((length,), F32), ((2 * chunk,), F32), states, ((modes,), F32), width=broad),
+        [pltpu.VMEM((chunk, broad), F32)], 8 * unit,
     )
     conv, sums, carried, moved = call(
         functools.partial(forward_kernel, chunk), grid,
-        inputs(lam, res, parts, conv_local, gain) + held_inputs(pieces, q, og),
-        [(((length, channels), F32), (1, width), True), (((2, length, LANES), F32), None, True)]
+        held_inputs(lam, res, parts) + inputs(conv_local) + held_inputs(gain, pieces, q, og),
+        [(((length, channels), F32), (1, width), True), (((2, length), F32), None, True)]
         + outputs(states, ((modes,), F32)),
-        [held], unit, forward_begin,
+        [held, pltpu.VMEM((2, length, LANES), F32)], unit, forward_begin, forward_end,
     )
     peers = lax.ppermute(sums, "chan", [(0, 1), (1, 0)])
     y_out, grad_q, gate, gain_part, gw, state = call(
         functools.partial(gate_kernel, chunk), grid,
-        inputs(lam, gain) + [(sums, None, True), (peers, None, True)] + held_inputs(conv, q, og),
+        held_inputs(lam, gain) + [(sums, None, True), (peers, None, True)] + held_inputs(conv, q, og),
         outputs(((length,), BF16), ((length,), BF16), ((length,), F32), ((1,), F32), states, send),
         [pltpu.VMEM((length, LANES), F32)] * 2, unit, functools.partial(gate_begin, model_width),
     )
@@ -501,12 +520,12 @@
         [pltpu.VMEM((chunk, width), F32)], 8 * unit,
     )
     adj, grads = call(
-        functools.partial(adjoint_kernel, float(length)), grid,
-        inputs(lam, res, slope) + [(grads, (0, width // LANES)), (later, (2, width), True)],
-        outputs(((modes,), F32)) + [((grads_shape, BF16), (0, width // LANES))], [], channels * modes * 40,
+        functools.partial(adjoint_kernel, float(length)), 1,
+        [(grads, (0, groups))] + [(a, None, True) for a in (lam, res, slope, later)],
+        [((lam.shape, F32), (1, channels)), ((grads_shape, BF16), (0, groups))], [], channels * modes * 40,
     )
     grad_k, grad_v = call(
-        functools.partial(finish_kernel, chunk), grid, inputs(adj, lam, res, gw, vg_local) + held_inputs(k, v),
+        functools.partial(finish_kernel, chunk), grid, inputs(adj) + held_inputs(lam, res) + inputs(gw, vg_local) + held_inputs(k, v),
         outputs(((length,), BF16), ((length,), BF16)), [held], unit,
     )
     both = ("ctx", "dp")
@@ -516,15 +535,15 @@
         total = lax.all_to_all(jnp.broadcast_to(mine[None], grads.shape), both, 0, 0).astype(F32)
     else:
         total = lax.psum(grads.astype(F32), both)
-    total = total.transpose(0, 2, 1).reshape(channels, rows)
+    by_mode = total.transpose(1, 0, 2).reshape(rows, channels)
     return (
         y_out[None],
         grad_q[None],
         grad_k[None],
         grad_v[None],
-        total[:, :modes],
-        total[:, modes : 2 * modes],
-        total[:, 2 * modes],
+        by_mode[:modes].T,
+        by_mode[modes : 2 * modes].T,
+        by_mode[2 * modes],
     )
 
 

time: 89 us -> 88.3 us (level)
  Pallas kernels: 48 us -> 46.3 us
    pallas_call x7, Pallas kernels: 48 us -> 46.3 us  [call(): pl.pallas_call(functools.partial(streamed, kernel, begin, end, steps, kin...]
    all_to_all x1, waiting for transfers between devices: 3.76 us -> 5.04 us  [shards(): pieces = lax.all_to_all(state, 'ctx', 0, 0)]
  transfers between devices with their start and end apart: 4 -> 4, of which waited for: 4 -> 4; matrix products, arithmetic and copies ran while one was open for 0% -> 0% of each run, Pallas kernels for 32% -> 31%
where the time goes in v6:
time: 88.3 us; the launch traced here: 87.7 us
  Pallas kernels  46.3 us (52%)
  starting transfers between devices  14.6 us (17%)
  blocking collectives  13 us (15%)
  waiting for transfers between devices  10.9 us (12%)
  local copies, waits for them, and re-layouts  2.09 us (2%)
    pallas_call x7, Pallas kernels, call(): pl.pallas_call(functools.partial(streamed, kernel, begin, end, steps, kin...  46.3 us
    all_to_all x1, blocking collectives, shards(): parts = lax.all_to_all(grads, both, 0, 0)  13 us
    all_to_all x1, starting transfers between devices, shards(): pieces = lax.all_to_all(state, 'ctx', 0, 0)  7.4 us
    all_to_all x1, waiting for transfers between devices, shards(): pieces = lax.all_to_all(state, 'ctx', 0, 0)  5.04 us
    all_to_all x1, starting transfers between devices, shards(): later = lax.all_to_all(state, 'ctx', 0, 0)  3.65 us
    all_to_all x1, starting transfers between devices, shards(): lax.all_to_all(jnp.broadcast_to(mine[None], grads.shape), both, 0, 0)  3.52 us
    all_to_all x1, waiting for transfers between devices, shards(): lax.all_to_all(jnp.broadcast_to(mine[None], grads.shape), both, 0, 0)  2.58 us
    all_to_all x1, waiting for transfers between devices, shards(): later = lax.all_to_all(state, 'ctx', 0, 0)  2.13 us
  transfers between devices with their start and end apart: 4, of which 4 were waited for; matrix products, arithmetic and copies ran while one was open for 0% of the time, Pallas kernels for 31%

profile of v6, /device:TPU:0, one launch (start us, length us, event | category | flops | bytes accessed | tf_op | source)
XLA Modules:
  0.0 87.7 jit_solution(17653633230326329008)
XLA Ops:
  0.6 0.0 copy-start.4
  0.6 0.0 copy-start.5
  0.7 0.0 copy-start.6
  0.7 0.0 copy-start.9
  0.7 5.5 %shard_map.153 = (bf16[256,2048]{1,0:T(8,128)(2,1)}, f32[16,2048]{1,0:T(8,128)}, f32[4,16,2048]{2,1,0:T(8,128)}, bf16[8,16,2048]{2,1,0:T(8,128)(2,1)}) custom-call(bf16[256,2048]{1,0:T(8,128)(2,1)} %bitcast.26, bf16[256,2048]{1,0:T(8,128)(2,1)} %bitcast.28, f32[16,2048]{1,0:T(8,128)} %bitcast.40), custom_call_target="tpu_custom_call" | custom-call | flops 16777216 | bytes 4456448 | tf_op jit(solution)/shard_map/pallas_call | solution.py:443
  6.2 0.0 copy-start
  6.2 0.0 copy-start.7
  6.2 7.4 %all-to-all-start = ((bf16[8,16,2048]{2,1,0:T(8,128)(2,1)}), bf16[8,16,2048]{2,1,0:T(8,128)(2,1)S(1)}, u32[]{:S(2)}, u32[]{:S(2)}) async-start(bf16[8,16,2048]{2,1,0:T(8,128)(2,1)} %get-tuple-element.35), calls=%async_computation | async-start | bytes 1048576 | tf_op jit(solution)/shard_map/all_to_all | solution.py:493
  13.6 9.4 %shard_map.154 = (f32[256,2048]{1,0:T(8,128)}, f32[128,2048]{1,0:T(8,128)}, f32[4,16,2048]{2,1,0:T(8,128)}, f32[16,2048]{1,0:T(8,128)}) custom-call(bf16[256,2048]{1,0:T(8,128)(2,1)} %get-tuple-element.33.refs_0_.refs_2_, f32[16,2048]{1,0:T(8,128)} %get-tuple-element.31.refs_1_.refs_0_, f32[16,2048]{1,0:T(8,128)} %bitcast.34, ...), custom_call_target="tpu_custom_call" | custom-call | flops 134217728 | bytes 5783552 | tf_op jit(solution)/shard_map/pallas_call | solution.py:443
  23.1 5.0 %all-to-all-done.refs_5_ = bf16[8,16,2048]{2,1,0:T(8,128)(2,1)S(1)} async-done(((bf16[8,16,2048]{2,1,0:T(8,128)(2,1)}), bf16[8,16,2048]{2,1,0:T(8,128)(2,1)S(1)}, u32[]{:S(2)}, u32[]{:S(2)}) %all-to-all-start) | async-done | bytes 524320 | tf_op jit(solution)/shard_map/all_to_all | solution.py:493
  28.1 0.0 copy-done.4
  28.1 0.0 copy-done.5
  28.1 0.0 copy-done.6
  28.1 0.0 copy-done.9
  28.1 0.0 copy-done
  28.1 0.0 copy-done.7
  28.2 5.5 %shard_map.155 = (f32[256,2048]{1,0:T(8,128)S(1)}, f32[2,256]{1,0:T(2,128)S(1)}, f32[4,16,2048]{2,1,0:T(8,128)}, f32[16,2048]{1,0:T(8,128)}) custom-call(f32[16,2048]{1,0:T(8,128)S(1)} %copy-done, f32[16,2048]{1,0:T(8,128)S(1)} %bitcast.35, f32[4,16,2048]{2,1,0:T(8,128)S(1)} %copy-done.7, f32[256,2048]{1,0:T(8,128)} %get-tuple-element.34.refs_3_, ...), custom_call_target="tpu_custom_call" | custom-call | flops 16777216 | bytes 8267776 | tf_op jit(solution)/shard_map/pallas_call | solution.py:443
  33.6 0.1 collective-permute-start
  33.7 1.1 %collective-permute-done.refs_3_ = f32[2,256]{1,0:T(2,128)S(1)} collective-permute-done((f32[2,256]{1,0:T(2,128)S(1)}, f32[2,256]{1,0:T(2,128)S(1)}, u32[]{:S(2)}, u32[]{:S(2)}) %collective-permute-start) | collective-permute-done | bytes 2080 | tf_op jit(solution)/shard_map/ppermute | solution.py:506
  34.9 5.9 %shard_map.156 = (bf16[256,2048]{1,0:T(8,128)(2,1)}, bf16[256,2048]{1,0:T(8,128)(2,1)}, f32[256,2048]{1,0:T(8,128)}, f32[1,2048]{1,0:T(1,128)}, f32[4,16,2048]{2,1,0:T(8,128)}, /*index=5*/bf16[8,16,2048]{2,1,0:T(8,128)(2,1)}) custom-call(f32[16,2048]{1,0:T(8,128)S(1)} %copy-done, f32[1,2048]{1,0:T(1,128)S(1)} %bitcast.39, ...), custom_call_target="tpu_custom_call" | custom-call | flops 16777216 | bytes 9588736 | tf_op jit(solution)/shard_map/pallas_call | solution.py:443
  40.8 3.6 %all-to-all-start.1 = ((bf16[8,16,2048]{2,1,0:T(8,128)(2,1)}), bf16[8,16,2048]{2,1,0:T(8,128)(2,1)S(1)}, u32[]{:S(2)}, u32[]{:S(2)}) async-start(bf16[8,16,2048]{2,1,0:T(8,128)(2,1)} %get-tuple-element.49), calls=%async_computation.1 | async-start | bytes 1048576 | tf_op jit(solution)/shard_map/all_to_all | solution.py:513
  44.4 0.0 copy-start.1
  44.4 0.0 copy-start.8
  44.4 12.7 %shard_map.157 = (f32[256,2048]{1,0:T(8,128)}, f32[16,40,128]{2,1,0:T(8,128)}) custom-call(f32[16,2048]{1,0:T(8,128)} %get-tuple-element.31.refs_1_.refs_0_, f32[256,2048]{1,0:T(8,128)} %get-tuple-element.40.refs_1_, bf16[256,2048]{1,0:T(8,128)(2,1)} %get-tuple-element.33.refs_0_.refs_2_, f32[128,2048]{1,0:T(8,128)} %get-tuple-element.41.refs_3_, ...), custom_call_target="tpu_custom_call" | custom-call | flops 134217728 | bytes 8609792 | tf_op jit(solution)/shard_map/pallas_call | solution.py:443
  57.1 0.0 copy-start.2
  57.1 0.0 copy-start.3
  57.2 2.1 %all-to-all-done.1.refs_4_ = bf16[8,16,2048]{2,1,0:T(8,128)(2,1)S(1)} async-done(((bf16[8,16,2048]{2,1,0:T(8,128)(2,1)}), bf16[8,16,2048]{2,1,0:T(8,128)(2,1)S(1)}, u32[]{:S(2)}, u32[]{:S(2)}) %all-to-all-start.1) | async-done | bytes 524320 | tf_op jit(solution)/shard_map/all_to_all | solution.py:513
  59.3 0.0 copy-done.1
  59.3 0.0 copy-done.8
  59.3 1.9 %shard_map.158 = (f32[16,2048]{1,0:T(8,128)}, bf16[16,40,128]{2,1,0:T(8,128)(2,1)}) custom-call(f32[16,40,128]{2,1,0:T(8,128)} %get-tuple-element.47.refs_0_, f32[16,2048]{1,0:T(8,128)S(1)} %copy-done.1, f32[16,2048]{1,0:T(8,128)S(1)} %bitcast.36, f32[16,2048]{1,0:T(8,128)S(1)} %copy-done.8, bf16[8,16,2048]{2,1,0:T(8,128)(2,1)S(1)} %all-to-all-done.1.refs_4_), custom_call_target="tpu_custom_call" | custom-call | flops 1310720 | bytes 1540096 | tf_op jit(solution)/shard_map/pallas_call | solution.py:443
  61.2 13.0 %all_to_all.20 = bf16[16,40,128]{2,1,0:T(8,128)(2,1)S(1)} all-to-all(bf16[16,40,128]{2,1,0:T(8,128)(2,1)} %get-tuple-element.54), channel_id=1, replica_groups=mesh['ctx'=8,'chan'=2,'dp'=2] {'ctx','dp'}, dimensions={0} | all-to-all | bytes 327680 | tf_op jit(solution)/shard_map/all_to_all | solution.py:533
  74.2 0.7 broadcast_in_dim.26
  74.9 3.5 %all-to-all-start.3 = ((bf16[16,40,128]{2,1,0:T(8,128)(2,1)}), bf16[16,40,128]{2,1,0:T(8,128)(2,1)S(1)}, u32[]{:S(2)}, u32[]{:S(2)}) async-start(bf16[16,40,128]{2,1,0:T(8,128)(2,1)} %broadcast_in_dim.26), calls=%async_computation.3 | async-start | bytes 327680 | tf_op jit(solution)/shard_map/all_to_all | solution.py:535
  78.4 0.0 copy-done.2
  78.5 0.0 copy-done.3
  78.5 5.3 %shard_map.159 = (bf16[256,2048]{1,0:T(8,128)(2,1)}, bf16[256,2048]{1,0:T(8,128)(2,1)}) custom-call(f32[16,2048]{1,0:T(8,128)} %get-tuple-element.50.refs_0_, f32[16,2048]{1,0:T(8,128)S(1)} %copy-done.1, f32[16,2048]{1,0:T(8,128)S(1)} %bitcast.37, f32[4,16,2048]{2,1,0:T(8,128)} %get-tuple-element.45.refs_7_.refs_3_, f32[256,2048]{1,0:T(8,128)} %get-tuple-element.51.refs_4_, ...), custom_call_target="tpu_custom_call" | custom-call | flops 16777216 | bytes 7208960 | tf_op jit(solution)/shard_map/pallas_call | solution.py:443
  83.8 2.6 %all-to-all-done.3 = bf16[16,40,128]{2,1,0:T(8,128)(2,1)S(1)} async-done(((bf16[16,40,128]{2,1,0:T(8,128)(2,1)}), bf16[16,40,128]{2,1,0:T(8,128)(2,1)S(1)}, u32[]{:S(2)}, u32[]{:S(2)}) %all-to-all-start.3) | async-done | bytes 163872 | tf_op jit(solution)/shard_map/all_to_all | solution.py:535
  86.4 0.6 slice.23
  87.0 0.7 bitcast_bitcast_fusion
  (3 shorter events, 0.1 us)
Async XLA Ops:
  0.6 27.5 %copy-start.4 = (bf16[1,256,2048]{2,1,0:T(8,128)(2,1)S(1)}, bf16[1,256,2048]{2,1,0:T(8,128)(2,1)}, u32[]{:S(2)}) copy-start(bf16[1,256,2048]{2,1,0:T(8,128)(2,1)} %param.10) | copy-start | bytes 3145732
  0.6 27.5 %copy-start.5 = (bf16[1,256,2048]{2,1,0:T(8,128)(2,1)S(1)}, bf16[1,256,2048]{2,1,0:T(8,128)(2,1)}, u32[]{:S(2)}) copy-start(bf16[1,256,2048]{2,1,0:T(8,128)(2,1)} %param.13) | copy-start | bytes 3145732
  0.7 27.5 %copy-start.6 = (f32[2048,16]{0,1:T(8,128)S(1)}, f32[2048,16]{0,1:T(8,128)}, u32[]{:S(2)}) copy-start(f32[2048,16]{0,1:T(8,128)} %param.15) | copy-start | bytes 393220
  0.7 27.5 %copy-start.9 = (f32[2048]{0:T(1024)S(1)}, f32[2048]{0:T(1024)}, u32[]{:S(2)}) copy-start(f32[2048]{0:T(1024)} %param.14) | copy-start | bytes 24580
  6.2 21.9 %copy-start = (f32[16,2048]{1,0:T(8,128)S(1)}, f32[16,2048]{1,0:T(8,128)}, u32[]{:S(2)}) copy-start(f32[16,2048]{1,0:T(8,128)} %get-tuple-element.31.refs_1_.refs_0_) | copy-start | bytes 393220
  6.2 21.9 %copy-start.7 = (f32[4,16,2048]{2,1,0:T(8,128)S(1)}, f32[4,16,2048]{2,1,0:T(8,128)}, u32[]{:S(2)}) copy-start(f32[4,16,2048]{2,1,0:T(8,128)} %get-tuple-element.32.refs_3_.refs_2_) | copy-start | bytes 1572868
  6.2 21.9 %all-to-all-start = ((bf16[8,16,2048]{2,1,0:T(8,128)(2,1)}), bf16[8,16,2048]{2,1,0:T(8,128)(2,1)S(1)}, u32[]{:S(2)}, u32[]{:S(2)}) async-start(bf16[8,16,2048]{2,1,0:T(8,128)(2,1)} %get-tuple-element.35), calls=%async_computation | async-start | bytes 1048576 | tf_op jit(solution)/shard_map/all_to_all | solution.py:493
  33.6 1.2 %collective-permute-start = (f32[2,256]{1,0:T(2,128)S(1)}, f32[2,256]{1,0:T(2,128)S(1)}, u32[]{:S(2)}, u32[]{:S(2)}) collective-permute-start(f32[2,256]{1,0:T(2,128)S(1)} %get-tuple-element.36.refs_2_), channel_id=1, source_target_pairs={{0,2},{2,0},{1,3},{3,1},{4,6},{6,4},{5,7},{7,5},{8,10},{10,8},{9,1... | collective-permute-start | bytes 6152 | tf_op jit(solution)/shard_map/ppermute | solution.py:506
  40.8 18.5 %all-to-all-start.1 = ((bf16[8,16,2048]{2,1,0:T(8,128)(2,1)}), bf16[8,16,2048]{2,1,0:T(8,128)(2,1)S(1)}, u32[]{:S(2)}, u32[]{:S(2)}) async-start(bf16[8,16,2048]{2,1,0:T(8,128)(2,1)} %get-tuple-element.49), calls=%async_computation.1 | async-start | bytes 1048576 | tf_op jit(solution)/shard_map/all_to_all | solution.py:513
  44.4 14.9 %copy-start.1 = (f32[16,2048]{1,0:T(8,128)S(1)}, f32[16,2048]{1,0:T(8,128)}, u32[]{:S(2)}) copy-start(f32[16,2048]{1,0:T(8,128)} %get-tuple-element.31.refs_1_.refs_0_) | copy-start | bytes 393220
  44.4 14.9 %copy-start.8 = (f32[16,2048]{1,0:T(8,128)S(1)}, f32[16,2048]{1,0:T(8,128)}, u32[]{:S(2)}) copy-start(f32[16,2048]{1,0:T(8,128)} %get-tuple-element.48.refs_3_) | copy-start | bytes 393220
  57.1 21.3 %copy-start.2 = (bf16[1,256,2048]{2,1,0:T(8,128)(2,1)S(1)}, bf16[1,256,2048]{2,1,0:T(8,128)(2,1)}, u32[]{:S(2)}) copy-start(bf16[1,256,2048]{2,1,0:T(8,128)(2,1)} %param.11) | copy-start | bytes 3145732
  57.1 21.3 %copy-start.3 = (bf16[1,256,2048]{2,1,0:T(8,128)(2,1)S(1)}, bf16[1,256,2048]{2,1,0:T(8,128)(2,1)}, u32[]{:S(2)}) copy-start(bf16[1,256,2048]{2,1,0:T(8,128)(2,1)} %param.12) | copy-start | bytes 3145732
  74.9 11.4 %all-to-all-start.3 = ((bf16[16,40,128]{2,1,0:T(8,128)(2,1)}), bf16[16,40,128]{2,1,0:T(8,128)(2,1)S(1)}, u32[]{:S(2)}, u32[]{:S(2)}) async-start(bf16[16,40,128]{2,1,0:T(8,128)(2,1)} %broadcast_in_dim.26), calls=%async_computation.3 | async-start | bytes 327680 | tf_op jit(solution)/shard_map/all_to_all | solution.py:535

commit v7 on v6

--- a/solution.py
+++ b/solution.py
@@ -77,6 +77,14 @@
     return jnp.concatenate(out, axis=0)
 
 
+def fold_rounded(x):
+    modes = x.shape[0]
+    flat = x.reshape(modes * ROWS, LANES).astype(BF16)
+    own = lax.broadcasted_iota(jnp.int32, (modes, modes * ROWS), 1) // ROWS
+    pick = (own == lax.broadcasted_iota(jnp.int32, own.shape, 0)).astype(F32).astype(BF16)
+    return dot(pick, flat)
+
+
 def groups_of(width, body):
     def step(i, _):
         body(i, pl.ds(pl.multiple_of(i * LANES, LANES), LANES))
@@ -130,7 +138,7 @@
                 vals = vals.astype(F32)
                 for tile in (vals[:ROWS], vals[ROWS:]):
                     acc = acc * step + tile[None] if acc is not None else jnp.broadcast_to(tile[None], lam.shape)
-            part = fold(acc * weight)
+            part = fold_rounded(acc * weight)
             parts_ref[c, :, cols] = part
             total = part if total is None else total * decay_chunk + part
         for dest in range(send_ref.shape[0]):
@@ -263,7 +271,7 @@
                 gate_ref[rows, cols] = gate
                 for tile in (gate[ROWS:], gate[:ROWS]):
                     acc = acc * step + tile[None] if acc is not None else jnp.broadcast_to(tile[None], lam.shape)
-            part = fold(acc * weight)
+            part = fold_rounded(acc * weight)
             gw_ref[c, :, cols] = part
             total = part if total is None else total * decay_chunk + part
         gain_part_ref[:, cols] = jnp.sum(gain_acc, axis=0, keepdims=True)

time: 88.3 us -> 87.7 us (level)
  no operation moved by 1% of the time
where the time goes in v7:
time: 87.7 us; the launch traced here: 87.1 us
  Pallas kernels  45.6 us (52%)
  starting transfers between devices  14.6 us (17%)
  blocking collectives  13 us (15%)
  waiting for transfers between devices  10.9 us (12%)
  local copies, waits for them, and re-layouts  2.09 us (2%)
    pallas_call x7, Pallas kernels, call(): pl.pallas_call(functools.partial(streamed, kernel, begin, end, steps, kin...  45.6 us
    all_to_all x1, blocking collectives, shards(): parts = lax.all_to_all(grads, both, 0, 0)  13 us
    all_to_all x1, starting transfers between devices, shards(): pieces = lax.all_to_all(state, 'ctx', 0, 0)  7.4 us
    all_to_all x1, waiting for transfers between devices, shards(): pieces = lax.all_to_all(state, 'ctx', 0, 0)  5.05 us
    all_to_all x1, starting transfers between devices, shards(): later = lax.all_to_all(state, 'ctx', 0, 0)  3.65 us
    all_to_all x1, starting transfers between devices, shards(): lax.all_to_all(jnp.broadcast_to(mine[None], grads.shape), both, 0, 0)  3.52 us
    all_to_all x1, waiting for transfers between devices, shards(): lax.all_to_all(jnp.broadcast_to(mine[None], grads.shape), both, 0, 0)  2.58 us
    all_to_all x1, waiting for transfers between devices, shards(): later = lax.all_to_all(state, 'ctx', 0, 0)  2.13 us
  transfers between devices with their start and end apart: 4, of which 4 were waited for; matrix products, arithmetic and copies ran while one was open for 0% of the time, Pallas kernels for 31%

profile of v7, /device:TPU:0, one launch (start us, length us, event | category | flops | bytes accessed | tf_op | source)
XLA Modules:
  0.0 87.1 jit_solution(478408955082675707)
XLA Ops:
  0.6 0.0 copy-start.4
  0.6 0.0 copy-start.5
  0.7 0.0 copy-start.6
  0.7 0.0 copy-start.9
  0.7 5.3 %shard_map.153 = (bf16[256,2048]{1,0:T(8,128)(2,1)}, f32[16,2048]{1,0:T(8,128)}, f32[4,16,2048]{2,1,0:T(8,128)}, bf16[8,16,2048]{2,1,0:T(8,128)(2,1)}) custom-call(bf16[256,2048]{1,0:T(8,128)(2,1)} %bitcast.26, bf16[256,2048]{1,0:T(8,128)(2,1)} %bitcast.28, f32[16,2048]{1,0:T(8,128)} %bitcast.40), custom_call_target="tpu_custom_call" | custom-call | flops 16777216 | bytes 4456448 | tf_op jit(solution)/shard_map/pallas_call | solution.py:451
  6.0 0.0 copy-start
  6.0 0.0 copy-start.7
  6.0 7.4 %all-to-all-start = ((bf16[8,16,2048]{2,1,0:T(8,128)(2,1)}), bf16[8,16,2048]{2,1,0:T(8,128)(2,1)S(1)}, u32[]{:S(2)}, u32[]{:S(2)}) async-start(bf16[8,16,2048]{2,1,0:T(8,128)(2,1)} %get-tuple-element.35), calls=%async_computation | async-start | bytes 1048576 | tf_op jit(solution)/shard_map/all_to_all | solution.py:501
  13.4 9.4 %shard_map.154 = (f32[256,2048]{1,0:T(8,128)}, f32[128,2048]{1,0:T(8,128)}, f32[4,16,2048]{2,1,0:T(8,128)}, f32[16,2048]{1,0:T(8,128)}) custom-call(bf16[256,2048]{1,0:T(8,128)(2,1)} %get-tuple-element.33.refs_0_.refs_2_, f32[16,2048]{1,0:T(8,128)} %get-tuple-element.31.refs_1_.refs_0_, f32[16,2048]{1,0:T(8,128)} %bitcast.34, ...), custom_call_target="tpu_custom_call" | custom-call | flops 134217728 | bytes 5783552 | tf_op jit(solution)/shard_map/pallas_call | solution.py:451
  22.8 5.0 %all-to-all-done.refs_5_ = bf16[8,16,2048]{2,1,0:T(8,128)(2,1)S(1)} async-done(((bf16[8,16,2048]{2,1,0:T(8,128)(2,1)}), bf16[8,16,2048]{2,1,0:T(8,128)(2,1)S(1)}, u32[]{:S(2)}, u32[]{:S(2)}) %all-to-all-start) | async-done | bytes 524320 | tf_op jit(solution)/shard_map/all_to_all | solution.py:501
  27.9 0.0 copy-done.4
  27.9 0.0 copy-done.5
  27.9 0.0 copy-done.6
  27.9 0.0 copy-done.9
  27.9 0.0 copy-done
  27.9 0.0 copy-done.7
  27.9 5.5 %shard_map.155 = (f32[256,2048]{1,0:T(8,128)S(1)}, f32[2,256]{1,0:T(2,128)S(1)}, f32[4,16,2048]{2,1,0:T(8,128)}, f32[16,2048]{1,0:T(8,128)}) custom-call(f32[16,2048]{1,0:T(8,128)S(1)} %copy-done, f32[16,2048]{1,0:T(8,128)S(1)} %bitcast.35, f32[4,16,2048]{2,1,0:T(8,128)S(1)} %copy-done.7, f32[256,2048]{1,0:T(8,128)} %get-tuple-element.34.refs_3_, ...), custom_call_target="tpu_custom_call" | custom-call | flops 16777216 | bytes 8267776 | tf_op jit(solution)/shard_map/pallas_call | solution.py:451
  33.4 0.1 collective-permute-start
  33.5 1.1 %collective-permute-done.refs_3_ = f32[2,256]{1,0:T(2,128)S(1)} collective-permute-done((f32[2,256]{1,0:T(2,128)S(1)}, f32[2,256]{1,0:T(2,128)S(1)}, u32[]{:S(2)}, u32[]{:S(2)}) %collective-permute-start) | collective-permute-done | bytes 2080 | tf_op jit(solution)/shard_map/ppermute | solution.py:514
  34.6 5.5 %shard_map.156 = (bf16[256,2048]{1,0:T(8,128)(2,1)}, bf16[256,2048]{1,0:T(8,128)(2,1)}, f32[256,2048]{1,0:T(8,128)}, f32[1,2048]{1,0:T(1,128)}, f32[4,16,2048]{2,1,0:T(8,128)}, /*index=5*/bf16[8,16,2048]{2,1,0:T(8,128)(2,1)}) custom-call(f32[16,2048]{1,0:T(8,128)S(1)} %copy-done, f32[1,2048]{1,0:T(1,128)S(1)} %bitcast.39, ...), custom_call_target="tpu_custom_call" | custom-call | flops 16777216 | bytes 9588736 | tf_op jit(solution)/shard_map/pallas_call | solution.py:451
  40.1 3.6 %all-to-all-start.1 = ((bf16[8,16,2048]{2,1,0:T(8,128)(2,1)}), bf16[8,16,2048]{2,1,0:T(8,128)(2,1)S(1)}, u32[]{:S(2)}, u32[]{:S(2)}) async-start(bf16[8,16,2048]{2,1,0:T(8,128)(2,1)} %get-tuple-element.49), calls=%async_computation.1 | async-start | bytes 1048576 | tf_op jit(solution)/shard_map/all_to_all | solution.py:521
  43.8 0.0 copy-start.1
  43.8 0.0 copy-start.8
  43.8 12.7 %shard_map.157 = (f32[256,2048]{1,0:T(8,128)}, f32[16,40,128]{2,1,0:T(8,128)}) custom-call(f32[16,2048]{1,0:T(8,128)} %get-tuple-element.31.refs_1_.refs_0_, f32[256,2048]{1,0:T(8,128)} %get-tuple-element.40.refs_1_, bf16[256,2048]{1,0:T(8,128)(2,1)} %get-tuple-element.33.refs_0_.refs_2_, f32[128,2048]{1,0:T(8,128)} %get-tuple-element.41.refs_3_, ...), custom_call_target="tpu_custom_call" | custom-call | flops 134217728 | bytes 8609792 | tf_op jit(solution)/shard_map/pallas_call | solution.py:451
  56.5 0.0 copy-start.2
  56.5 0.0 copy-start.3
  56.5 2.1 %all-to-all-done.1.refs_4_ = bf16[8,16,2048]{2,1,0:T(8,128)(2,1)S(1)} async-done(((bf16[8,16,2048]{2,1,0:T(8,128)(2,1)}), bf16[8,16,2048]{2,1,0:T(8,128)(2,1)S(1)}, u32[]{:S(2)}, u32[]{:S(2)}) %all-to-all-start.1) | async-done | bytes 524320 | tf_op jit(solution)/shard_map/all_to_all | solution.py:521
  58.7 0.0 copy-done.1
  58.7 0.0 copy-done.8
  58.7 1.9 %shard_map.158 = (f32[16,2048]{1,0:T(8,128)}, bf16[16,40,128]{2,1,0:T(8,128)(2,1)}) custom-call(f32[16,40,128]{2,1,0:T(8,128)} %get-tuple-element.47.refs_0_, f32[16,2048]{1,0:T(8,128)S(1)} %copy-done.1, f32[16,2048]{1,0:T(8,128)S(1)} %bitcast.36, f32[16,2048]{1,0:T(8,128)S(1)} %copy-done.8, bf16[8,16,2048]{2,1,0:T(8,128)(2,1)S(1)} %all-to-all-done.1.refs_4_), custom_call_target="tpu_custom_call" | custom-call | flops 1310720 | bytes 1540096 | tf_op jit(solution)/shard_map/pallas_call | solution.py:451
  60.6 13.0 %all_to_all.20 = bf16[16,40,128]{2,1,0:T(8,128)(2,1)S(1)} all-to-all(bf16[16,40,128]{2,1,0:T(8,128)(2,1)} %get-tuple-element.54), channel_id=1, replica_groups=mesh['ctx'=8,'chan'=2,'dp'=2] {'ctx','dp'}, dimensions={0} | all-to-all | bytes 327680 | tf_op jit(solution)/shard_map/all_to_all | solution.py:541
  73.6 0.7 broadcast_in_dim.26
  74.3 3.5 %all-to-all-start.3 = ((bf16[16,40,128]{2,1,0:T(8,128)(2,1)}), bf16[16,40,128]{2,1,0:T(8,128)(2,1)S(1)}, u32[]{:S(2)}, u32[]{:S(2)}) async-start(bf16[16,40,128]{2,1,0:T(8,128)(2,1)} %broadcast_in_dim.26), calls=%async_computation.3 | async-start | bytes 327680 | tf_op jit(solution)/shard_map/all_to_all | solution.py:543
  77.8 0.0 copy-done.2
  77.8 0.0 copy-done.3
  77.9 5.3 %shard_map.159 = (bf16[256,2048]{1,0:T(8,128)(2,1)}, bf16[256,2048]{1,0:T(8,128)(2,1)}) custom-call(f32[16,2048]{1,0:T(8,128)} %get-tuple-element.50.refs_0_, f32[16,2048]{1,0:T(8,128)S(1)} %copy-done.1, f32[16,2048]{1,0:T(8,128)S(1)} %bitcast.37, f32[4,16,2048]{2,1,0:T(8,128)} %get-tuple-element.45.refs_7_.refs_3_, f32[256,2048]{1,0:T(8,128)} %get-tuple-element.51.refs_4_, ...), custom_call_target="tpu_custom_call" | custom-call | flops 16777216 | bytes 7208960 | tf_op jit(solution)/shard_map/pallas_call | solution.py:451
  83.2 2.6 %all-to-all-done.3 = bf16[16,40,128]{2,1,0:T(8,128)(2,1)S(1)} async-done(((bf16[16,40,128]{2,1,0:T(8,128)(2,1)}), bf16[16,40,128]{2,1,0:T(8,128)(2,1)S(1)}, u32[]{:S(2)}, u32[]{:S(2)}) %all-to-all-start.3) | async-done | bytes 163872 | tf_op jit(solution)/shard_map/all_to_all | solution.py:543
  85.8 0.6 slice.23
  86.4 0.7 bitcast_bitcast_fusion
  (3 shorter events, 0.1 us)
Async XLA Ops:
  0.6 27.3 %copy-start.4 = (bf16[1,256,2048]{2,1,0:T(8,128)(2,1)S(1)}, bf16[1,256,2048]{2,1,0:T(8,128)(2,1)}, u32[]{:S(2)}) copy-start(bf16[1,256,2048]{2,1,0:T(8,128)(2,1)} %param.10) | copy-start | bytes 3145732
  0.6 27.3 %copy-start.5 = (bf16[1,256,2048]{2,1,0:T(8,128)(2,1)S(1)}, bf16[1,256,2048]{2,1,0:T(8,128)(2,1)}, u32[]{:S(2)}) copy-start(bf16[1,256,2048]{2,1,0:T(8,128)(2,1)} %param.13) | copy-start | bytes 3145732
  0.7 27.2 %copy-start.6 = (f32[2048,16]{0,1:T(8,128)S(1)}, f32[2048,16]{0,1:T(8,128)}, u32[]{:S(2)}) copy-start(f32[2048,16]{0,1:T(8,128)} %param.15) | copy-start | bytes 393220
  0.7 27.2 %copy-start.9 = (f32[2048]{0:T(1024)S(1)}, f32[2048]{0:T(1024)}, u32[]{:S(2)}) copy-start(f32[2048]{0:T(1024)} %param.14) | copy-start | bytes 24580
  6.0 21.9 %copy-start = (f32[16,2048]{1,0:T(8,128)S(1)}, f32[16,2048]{1,0:T(8,128)}, u32[]{:S(2)}) copy-start(f32[16,2048]{1,0:T(8,128)} %get-tuple-element.31.refs_1_.refs_0_) | copy-start | bytes 393220
  6.0 21.9 %copy-start.7 = (f32[4,16,2048]{2,1,0:T(8,128)S(1)}, f32[4,16,2048]{2,1,0:T(8,128)}, u32[]{:S(2)}) copy-start(f32[4,16,2048]{2,1,0:T(8,128)} %get-tuple-element.32.refs_3_.refs_2_) | copy-start | bytes 1572868
  6.0 21.9 %all-to-all-start = ((bf16[8,16,2048]{2,1,0:T(8,128)(2,1)}), bf16[8,16,2048]{2,1,0:T(8,128)(2,1)S(1)}, u32[]{:S(2)}, u32[]{:S(2)}) async-start(bf16[8,16,2048]{2,1,0:T(8,128)(2,1)} %get-tuple-element.35), calls=%async_computation | async-start | bytes 1048576 | tf_op jit(solution)/shard_map/all_to_all | solution.py:501
  33.4 1.2 %collective-permute-start = (f32[2,256]{1,0:T(2,128)S(1)}, f32[2,256]{1,0:T(2,128)S(1)}, u32[]{:S(2)}, u32[]{:S(2)}) collective-permute-start(f32[2,256]{1,0:T(2,128)S(1)} %get-tuple-element.36.refs_2_), channel_id=1, source_target_pairs={{0,2},{2,0},{1,3},{3,1},{4,6},{6,4},{5,7},{7,5},{8,10},{10,8},{9,1... | collective-permute-start | bytes 6152 | tf_op jit(solution)/shard_map/ppermute | solution.py:514
  40.1 18.5 %all-to-all-start.1 = ((bf16[8,16,2048]{2,1,0:T(8,128)(2,1)}), bf16[8,16,2048]{2,1,0:T(8,128)(2,1)S(1)}, u32[]{:S(2)}, u32[]{:S(2)}) async-start(bf16[8,16,2048]{2,1,0:T(8,128)(2,1)} %get-tuple-element.49), calls=%async_computation.1 | async-start | bytes 1048576 | tf_op jit(solution)/shard_map/all_to_all | solution.py:521
  43.8 14.9 %copy-start.1 = (f32[16,2048]{1,0:T(8,128)S(1)}, f32[16,2048]{1,0:T(8,128)}, u32[]{:S(2)}) copy-start(f32[16,2048]{1,0:T(8,128)} %get-tuple-element.31.refs_1_.refs_0_) | copy-start | bytes 393220
  43.8 14.9 %copy-start.8 = (f32[16,2048]{1,0:T(8,128)S(1)}, f32[16,2048]{1,0:T(8,128)}, u32[]{:S(2)}) copy-start(f32[16,2048]{1,0:T(8,128)} %get-tuple-element.48.refs_3_) | copy-start | bytes 393220
  56.5 21.3 %copy-start.2 = (bf16[1,256,2048]{2,1,0:T(8,128)(2,1)S(1)}, bf16[1,256,2048]{2,1,0:T(8,128)(2,1)}, u32[]{:S(2)}) copy-start(bf16[1,256,2048]{2,1,0:T(8,128)(2,1)} %param.11) | copy-start | bytes 3145732
  56.5 21.3 %copy-start.3 = (bf16[1,256,2048]{2,1,0:T(8,128)(2,1)S(1)}, bf16[1,256,2048]{2,1,0:T(8,128)(2,1)}, u32[]{:S(2)}) copy-start(bf16[1,256,2048]{2,1,0:T(8,128)(2,1)} %param.12) | copy-start | bytes 3145732
  74.3 11.4 %all-to-all-start.3 = ((bf16[16,40,128]{2,1,0:T(8,128)(2,1)}), bf16[16,40,128]{2,1,0:T(8,128)(2,1)S(1)}, u32[]{:S(2)}, u32[]{:S(2)}) async-start(bf16[16,40,128]{2,1,0:T(8,128)(2,1)} %broadcast_in_dim.26), calls=%async_computation.3 | async-start | bytes 327680 | tf_op jit(solution)/shard_map/all_to_all | solution.py:543

commit v8 on v7

--- a/solution.py
+++ b/solution.py
@@ -198,7 +198,7 @@
 
 
 def forward_kernel(chunk, lam_ref, res_ref, parts_ref, conv_in_ref, gain_ref, pieces_ref, q_ref, og_ref,
-                   conv_ref, sums_ref, states_ref, moved_ref, held, acc_ref):
+                   conv_ref, sums_ref, states_ref, moved_ref, held, steps_ref, acc_ref):
     length, width = q_ref.shape
 
     def body(i, cols):
@@ -213,7 +213,8 @@
             held[i, c * modes : (c + 1) * modes] = state * res
             state = decay_chunk * state + parts_ref[c, :, cols]
         lam = spread(lam_ref, cols)
-        step = jnp.exp(-ROWS * lam)
+        steps_ref[i] = jnp.exp(-float(ROWS) * lam_ref[:, cols])
+        step = spread(steps_ref.at[i], slice(None))
         weight = jnp.exp(-lam * (sublane() + 1).astype(F32))
         gain = gain_ref[:, cols]
         for c in range(length // chunk):
@@ -247,8 +248,8 @@
 
     def body(i, cols):
         lam = spread(lam_ref, cols)
-        step = jnp.exp(-ROWS * lam)
         weight = jnp.exp(-lam * (sublane() + 1).astype(F32))
+        step = jnp.broadcast_to(weight[:, ROWS - 1 :], weight.shape)
         decay_chunk = jnp.exp(-float(chunk) * lam_ref[:, cols])
         gain = gain_ref[:, cols]
         gain_acc = jnp.zeros((16, LANES), F32)
@@ -492,6 +493,7 @@
     unit = 2 * length * channels * modes
     send = ((count, modes), BF16)
     states = ((chunks, modes), F32)
+    steps = pltpu.VMEM((width // LANES, modes, LANES), F32)
     held = pltpu.VMEM((width // LANES, chunks * modes, LANES), F32)
 
     vals, lam, parts, state = call(
@@ -509,7 +511,7 @@
         held_inputs(lam, res, parts) + inputs(conv_local) + held_inputs(gain, pieces, q, og),
         [(((length, channels), F32), (1, width), True), (((2, length), F32), None, True)]
         + outputs(states, ((modes,), F32)),
-        [held, pltpu.VMEM((2, length, LANES), F32)], unit, forward_begin, forward_end,
+        [held, steps, pltpu.VMEM((2, length, LANES), F32)], unit, forward_begin, forward_end,
     )
     peers = lax.ppermute(sums, "chan", [(0, 1), (1, 0)])
     y_out, grad_q, gate, gain_part, gw, state = call(

time: 87.7 us -> 87.4 us (level)
  transfers between devices with their start and end apart: 4 -> 4, of which waited for: 4 -> 4; matrix products, arithmetic and copies ran while one was open for 0% -> 0% of each run, Pallas kernels for 31% -> 32%
where the time goes in v8:
time: 87.4 us; the launch traced here: 86.9 us
  Pallas kernels  45.4 us (52%)
  starting transfers between devices  14.6 us (17%)
  blocking collectives  13 us (15%)
  waiting for transfers between devices  10.9 us (12%)
  local copies, waits for them, and re-layouts  2.09 us (2%)
    pallas_call x7, Pallas kernels, call(): pl.pallas_call(functools.partial(streamed, kernel, begin, end, steps, kin...  45.4 us
    all_to_all x1, blocking collectives, shards(): parts = lax.all_to_all(grads, both, 0, 0)  13 us
    all_to_all x1, starting transfers between devices, shards(): pieces = lax.all_to_all(state, 'ctx', 0, 0)  7.4 us
    all_to_all x1, waiting for transfers between devices, shards(): pieces = lax.all_to_all(state, 'ctx', 0, 0)  5.05 us
    all_to_all x1, starting transfers between devices, shards(): later = lax.all_to_all(state, 'ctx', 0, 0)  3.65 us
    all_to_all x1, starting transfers between devices, shards(): lax.all_to_all(jnp.broadcast_to(mine[None], grads.shape), both, 0, 0)  3.52 us
    all_to_all x1, waiting for transfers between devices, shards(): lax.all_to_all(jnp.broadcast_to(mine[None], grads.shape), both, 0, 0)  2.58 us
    all_to_all x1, waiting for transfers between devices, shards(): later = lax.all_to_all(state, 'ctx', 0, 0)  2.12 us
  transfers between devices with their start and end apart: 4, of which 4 were waited for; matrix products, arithmetic and copies ran while one was open for 0% of the time, Pallas kernels for 32%

profile of v8, /device:TPU:0, one launch (start us, length us, event | category | flops | bytes accessed | tf_op | source)
XLA Modules:
  0.0 86.9 jit_solution(18099870862806985057)
XLA Ops:
  0.6 0.0 copy-start.4
  0.6 0.0 copy-start.5
  0.7 0.0 copy-start.6
  0.7 0.0 copy-start.9
  0.7 5.3 %shard_map.153 = (bf16[256,2048]{1,0:T(8,128)(2,1)}, f32[16,2048]{1,0:T(8,128)}, f32[4,16,2048]{2,1,0:T(8,128)}, bf16[8,16,2048]{2,1,0:T(8,128)(2,1)}) custom-call(bf16[256,2048]{1,0:T(8,128)(2,1)} %bitcast.26, bf16[256,2048]{1,0:T(8,128)(2,1)} %bitcast.28, f32[16,2048]{1,0:T(8,128)} %bitcast.40), custom_call_target="tpu_custom_call" | custom-call | flops 16777216 | bytes 4456448 | tf_op jit(solution)/shard_map/pallas_call | solution.py:452
  6.0 0.0 copy-start
  6.0 0.0 copy-start.7
  6.0 7.4 %all-to-all-start = ((bf16[8,16,2048]{2,1,0:T(8,128)(2,1)}), bf16[8,16,2048]{2,1,0:T(8,128)(2,1)S(1)}, u32[]{:S(2)}, u32[]{:S(2)}) async-start(bf16[8,16,2048]{2,1,0:T(8,128)(2,1)} %get-tuple-element.35), calls=%async_computation | async-start | bytes 1048576 | tf_op jit(solution)/shard_map/all_to_all | solution.py:503
  13.4 9.4 %shard_map.154 = (f32[256,2048]{1,0:T(8,128)}, f32[128,2048]{1,0:T(8,128)}, f32[4,16,2048]{2,1,0:T(8,128)}, f32[16,2048]{1,0:T(8,128)}) custom-call(bf16[256,2048]{1,0:T(8,128)(2,1)} %get-tuple-element.33.refs_0_.refs_2_, f32[16,2048]{1,0:T(8,128)} %get-tuple-element.31.refs_1_.refs_0_, f32[16,2048]{1,0:T(8,128)} %bitcast.34, ...), custom_call_target="tpu_custom_call" | custom-call | flops 134217728 | bytes 5783552 | tf_op jit(solution)/shard_map/pallas_call | solution.py:452
  22.8 5.0 %all-to-all-done.refs_5_ = bf16[8,16,2048]{2,1,0:T(8,128)(2,1)S(1)} async-done(((bf16[8,16,2048]{2,1,0:T(8,128)(2,1)}), bf16[8,16,2048]{2,1,0:T(8,128)(2,1)S(1)}, u32[]{:S(2)}, u32[]{:S(2)}) %all-to-all-start) | async-done | bytes 524320 | tf_op jit(solution)/shard_map/all_to_all | solution.py:503
  27.9 0.0 copy-done.4
  27.9 0.0 copy-done.5
  27.9 0.0 copy-done.6
  27.9 0.0 copy-done.9
  27.9 0.0 copy-done
  27.9 0.0 copy-done.7
  27.9 5.3 %shard_map.155 = (f32[256,2048]{1,0:T(8,128)S(1)}, f32[2,256]{1,0:T(2,128)S(1)}, f32[4,16,2048]{2,1,0:T(8,128)}, f32[16,2048]{1,0:T(8,128)}) custom-call(f32[16,2048]{1,0:T(8,128)S(1)} %copy-done, f32[16,2048]{1,0:T(8,128)S(1)} %bitcast.35, f32[4,16,2048]{2,1,0:T(8,128)S(1)} %copy-done.7, f32[256,2048]{1,0:T(8,128)} %get-tuple-element.34.refs_3_, ...), custom_call_target="tpu_custom_call" | custom-call | flops 16777216 | bytes 8267776 | tf_op jit(solution)/shard_map/pallas_call | solution.py:452
  33.3 0.1 collective-permute-start
  33.4 1.1 %collective-permute-done.refs_3_ = f32[2,256]{1,0:T(2,128)S(1)} collective-permute-done((f32[2,256]{1,0:T(2,128)S(1)}, f32[2,256]{1,0:T(2,128)S(1)}, u32[]{:S(2)}, u32[]{:S(2)}) %collective-permute-start) | collective-permute-done | bytes 2080 | tf_op jit(solution)/shard_map/ppermute | solution.py:516
  34.5 5.4 %shard_map.156 = (bf16[256,2048]{1,0:T(8,128)(2,1)}, bf16[256,2048]{1,0:T(8,128)(2,1)}, f32[256,2048]{1,0:T(8,128)}, f32[1,2048]{1,0:T(1,128)}, f32[4,16,2048]{2,1,0:T(8,128)}, /*index=5*/bf16[8,16,2048]{2,1,0:T(8,128)(2,1)}) custom-call(f32[16,2048]{1,0:T(8,128)S(1)} %copy-done, f32[1,2048]{1,0:T(1,128)S(1)} %bitcast.39, ...), custom_call_target="tpu_custom_call" | custom-call | flops 16777216 | bytes 9588736 | tf_op jit(solution)/shard_map/pallas_call | solution.py:452
  39.9 3.6 %all-to-all-start.1 = ((bf16[8,16,2048]{2,1,0:T(8,128)(2,1)}), bf16[8,16,2048]{2,1,0:T(8,128)(2,1)S(1)}, u32[]{:S(2)}, u32[]{:S(2)}) async-start(bf16[8,16,2048]{2,1,0:T(8,128)(2,1)} %get-tuple-element.49), calls=%async_computation.1 | async-start | bytes 1048576 | tf_op jit(solution)/shard_map/all_to_all | solution.py:523
  43.6 0.0 copy-start.1
  43.6 0.0 copy-start.8
  43.6 12.7 %shard_map.157 = (f32[256,2048]{1,0:T(8,128)}, f32[16,40,128]{2,1,0:T(8,128)}) custom-call(f32[16,2048]{1,0:T(8,128)} %get-tuple-element.31.refs_1_.refs_0_, f32[256,2048]{1,0:T(8,128)} %get-tuple-element.40.refs_1_, bf16[256,2048]{1,0:T(8,128)(2,1)} %get-tuple-element.33.refs_0_.refs_2_, f32[128,2048]{1,0:T(8,128)} %get-tuple-element.41.refs_3_, ...), custom_call_target="tpu_custom_call" | custom-call | flops 134217728 | bytes 8609792 | tf_op jit(solution)/shard_map/pallas_call | solution.py:452
  56.3 0.0 copy-start.2
  56.3 0.0 copy-start.3
  56.3 2.1 %all-to-all-done.1.refs_4_ = bf16[8,16,2048]{2,1,0:T(8,128)(2,1)S(1)} async-done(((bf16[8,16,2048]{2,1,0:T(8,128)(2,1)}), bf16[8,16,2048]{2,1,0:T(8,128)(2,1)S(1)}, u32[]{:S(2)}, u32[]{:S(2)}) %all-to-all-start.1) | async-done | bytes 524320 | tf_op jit(solution)/shard_map/all_to_all | solution.py:523
  58.4 0.0 copy-done.1
  58.4 0.0 copy-done.8
  58.5 1.9 %shard_map.158 = (f32[16,2048]{1,0:T(8,128)}, bf16[16,40,128]{2,1,0:T(8,128)(2,1)}) custom-call(f32[16,40,128]{2,1,0:T(8,128)} %get-tuple-element.47.refs_0_, f32[16,2048]{1,0:T(8,128)S(1)} %copy-done.1, f32[16,2048]{1,0:T(8,128)S(1)} %bitcast.36, f32[16,2048]{1,0:T(8,128)S(1)} %copy-done.8, bf16[8,16,2048]{2,1,0:T(8,128)(2,1)S(1)} %all-to-all-done.1.refs_4_), custom_call_target="tpu_custom_call" | custom-call | flops 1310720 | bytes 1540096 | tf_op jit(solution)/shard_map/pallas_call | solution.py:452
  60.4 13.0 %all_to_all.20 = bf16[16,40,128]{2,1,0:T(8,128)(2,1)S(1)} all-to-all(bf16[16,40,128]{2,1,0:T(8,128)(2,1)} %get-tuple-element.54), channel_id=1, replica_groups=mesh['ctx'=8,'chan'=2,'dp'=2] {'ctx','dp'}, dimensions={0} | all-to-all | bytes 327680 | tf_op jit(solution)/shard_map/all_to_all | solution.py:543
  73.4 0.7 broadcast_in_dim.26
  74.1 3.5 %all-to-all-start.3 = ((bf16[16,40,128]{2,1,0:T(8,128)(2,1)}), bf16[16,40,128]{2,1,0:T(8,128)(2,1)S(1)}, u32[]{:S(2)}, u32[]{:S(2)}) async-start(bf16[16,40,128]{2,1,0:T(8,128)(2,1)} %broadcast_in_dim.26), calls=%async_computation.3 | async-start | bytes 327680 | tf_op jit(solution)/shard_map/all_to_all | solution.py:545
  77.6 0.0 copy-done.2
  77.6 0.0 copy-done.3
  77.6 5.3 %shard_map.159 = (bf16[256,2048]{1,0:T(8,128)(2,1)}, bf16[256,2048]{1,0:T(8,128)(2,1)}) custom-call(f32[16,2048]{1,0:T(8,128)} %get-tuple-element.50.refs_0_, f32[16,2048]{1,0:T(8,128)S(1)} %copy-done.1, f32[16,2048]{1,0:T(8,128)S(1)} %bitcast.37, f32[4,16,2048]{2,1,0:T(8,128)} %get-tuple-element.45.refs_7_.refs_3_, f32[256,2048]{1,0:T(8,128)} %get-tuple-element.51.refs_4_, ...), custom_call_target="tpu_custom_call" | custom-call | flops 16777216 | bytes 7208960 | tf_op jit(solution)/shard_map/pallas_call | solution.py:452
  82.9 2.6 %all-to-all-done.3 = bf16[16,40,128]{2,1,0:T(8,128)(2,1)S(1)} async-done(((bf16[16,40,128]{2,1,0:T(8,128)(2,1)}), bf16[16,40,128]{2,1,0:T(8,128)(2,1)S(1)}, u32[]{:S(2)}, u32[]{:S(2)}) %all-to-all-start.3) | async-done | bytes 163872 | tf_op jit(solution)/shard_map/all_to_all | solution.py:545
  85.5 0.6 slice.23
  86.2 0.7 bitcast_bitcast_fusion
  (3 shorter events, 0.1 us)
Async XLA Ops:
  0.6 27.3 %copy-start.4 = (bf16[1,256,2048]{2,1,0:T(8,128)(2,1)S(1)}, bf16[1,256,2048]{2,1,0:T(8,128)(2,1)}, u32[]{:S(2)}) copy-start(bf16[1,256,2048]{2,1,0:T(8,128)(2,1)} %param.10) | copy-start | bytes 3145732
  0.6 27.3 %copy-start.5 = (bf16[1,256,2048]{2,1,0:T(8,128)(2,1)S(1)}, bf16[1,256,2048]{2,1,0:T(8,128)(2,1)}, u32[]{:S(2)}) copy-start(bf16[1,256,2048]{2,1,0:T(8,128)(2,1)} %param.13) | copy-start | bytes 3145732
  0.7 27.2 %copy-start.6 = (f32[2048,16]{0,1:T(8,128)S(1)}, f32[2048,16]{0,1:T(8,128)}, u32[]{:S(2)}) copy-start(f32[2048,16]{0,1:T(8,128)} %param.15) | copy-start | bytes 393220
  0.7 27.2 %copy-start.9 = (f32[2048]{0:T(1024)S(1)}, f32[2048]{0:T(1024)}, u32[]{:S(2)}) copy-start(f32[2048]{0:T(1024)} %param.14) | copy-start | bytes 24580
  6.0 21.9 %copy-start = (f32[16,2048]{1,0:T(8,128)S(1)}, f32[16,2048]{1,0:T(8,128)}, u32[]{:S(2)}) copy-start(f32[16,2048]{1,0:T(8,128)} %get-tuple-element.31.refs_1_.refs_0_) | copy-start | bytes 393220
  6.0 21.9 %copy-start.7 = (f32[4,16,2048]{2,1,0:T(8,128)S(1)}, f32[4,16,2048]{2,1,0:T(8,128)}, u32[]{:S(2)}) copy-start(f32[4,16,2048]{2,1,0:T(8,128)} %get-tuple-element.32.refs_3_.refs_2_) | copy-start | bytes 1572868
  6.0 21.9 %all-to-all-start = ((bf16[8,16,2048]{2,1,0:T(8,128)(2,1)}), bf16[8,16,2048]{2,1,0:T(8,128)(2,1)S(1)}, u32[]{:S(2)}, u32[]{:S(2)}) async-start(bf16[8,16,2048]{2,1,0:T(8,128)(2,1)} %get-tuple-element.35), calls=%async_computation | async-start | bytes 1048576 | tf_op jit(solution)/shard_map/all_to_all | solution.py:503
  33.3 1.2 %collective-permute-start = (f32[2,256]{1,0:T(2,128)S(1)}, f32[2,256]{1,0:T(2,128)S(1)}, u32[]{:S(2)}, u32[]{:S(2)}) collective-permute-start(f32[2,256]{1,0:T(2,128)S(1)} %get-tuple-element.36.refs_2_), channel_id=1, source_target_pairs={{0,2},{2,0},{1,3},{3,1},{4,6},{6,4},{5,7},{7,5},{8,10},{10,8},{9,1... | collective-permute-start | bytes 6152 | tf_op jit(solution)/shard_map/ppermute | solution.py:516
  39.9 18.5 %all-to-all-start.1 = ((bf16[8,16,2048]{2,1,0:T(8,128)(2,1)}), bf16[8,16,2048]{2,1,0:T(8,128)(2,1)S(1)}, u32[]{:S(2)}, u32[]{:S(2)}) async-start(bf16[8,16,2048]{2,1,0:T(8,128)(2,1)} %get-tuple-element.49), calls=%async_computation.1 | async-start | bytes 1048576 | tf_op jit(solution)/shard_map/all_to_all | solution.py:523
  43.6 14.9 %copy-start.1 = (f32[16,2048]{1,0:T(8,128)S(1)}, f32[16,2048]{1,0:T(8,128)}, u32[]{:S(2)}) copy-start(f32[16,2048]{1,0:T(8,128)} %get-tuple-element.31.refs_1_.refs_0_) | copy-start | bytes 393220
  43.6 14.9 %copy-start.8 = (f32[16,2048]{1,0:T(8,128)S(1)}, f32[16,2048]{1,0:T(8,128)}, u32[]{:S(2)}) copy-start(f32[16,2048]{1,0:T(8,128)} %get-tuple-element.48.refs_3_) | copy-start | bytes 393220
  56.3 21.3 %copy-start.2 = (bf16[1,256,2048]{2,1,0:T(8,128)(2,1)S(1)}, bf16[1,256,2048]{2,1,0:T(8,128)(2,1)}, u32[]{:S(2)}) copy-start(bf16[1,256,2048]{2,1,0:T(8,128)(2,1)} %param.11) | copy-start | bytes 3145732
  56.3 21.3 %copy-start.3 = (bf16[1,256,2048]{2,1,0:T(8,128)(2,1)S(1)}, bf16[1,256,2048]{2,1,0:T(8,128)(2,1)}, u32[]{:S(2)}) copy-start(bf16[1,256,2048]{2,1,0:T(8,128)(2,1)} %param.12) | copy-start | bytes 3145732
  74.1 11.4 %all-to-all-start.3 = ((bf16[16,40,128]{2,1,0:T(8,128)(2,1)}), bf16[16,40,128]{2,1,0:T(8,128)(2,1)S(1)}, u32[]{:S(2)}, u32[]{:S(2)}) async-start(bf16[16,40,128]{2,1,0:T(8,128)(2,1)} %broadcast_in_dim.26), calls=%async_computation.3 | async-start | bytes 327680 | tf_op jit(solution)/shard_map/all_to_all | solution.py:545
